TPU v7x, 32 devices: a whole 2x2x4 slice. The times are simulated.
32 devices in a mesh: rows: 16 (over z, y, x), cols: 2 (over core).
Axes of the slice: x: 2, y: 2, z: 4, core: 2. Of those that a mesh axis runs over, the one named last changes fastest.
Arguments:
- tokens: bfloat16 [128, 32, 384], P('rows', 'cols'), may hold values from -6 to 6
- teacher: bfloat16 [128, 32, 384], P('rows', 'cols'), may hold values from -6 to 6
- tissue: int32 [16, 4], P('rows', 'cols'), may hold values 0 or 1
- weights: bfloat16 [589824], P(('rows', 'cols')), may hold values from -0.3125 to 0.3125
Outputs:
- token_grads: bfloat16 [128, 32, 384], P('rows', 'cols')
- weight_grads: float32 [589824], P(('rows', 'cols'))
All inputs are finite; a program needn't handle non-finite values. No bound on the sum of `tissue` on one device may be relied on, other than what follows from the above.
Results may differ from a plain program's by a relative error of at most 0.0075.
Values may be sent and summed in bfloat16 or wider, within the bound.
No kernel may reach another device: no remote copies, remote signals or barrier semaphores. Data moves between devices by JAX's collectives and lax.ppermute only.
A program may use at most 64 MiB of HBM per device.

v0:
```python
import functools
import math

import jax
import jax.numpy as jnp
from jax import lax
from jax.experimental import pallas as pl
from jax.experimental.pallas import tpu as pltpu
from jax.sharding import PartitionSpec as P


HEADS = 6
TILE = 8
PER = TILE * TILE
BLK = PER + 16
AXES = ("rows", "cols")

norm_epsilon = 1e-05
head_epsilon = 1e-06

F32 = jnp.float32
BF16 = jnp.bfloat16


def dot(a, b):
    return jnp.dot(a, b, preferred_element_type=F32)


def dot_nt(a, b):
    return lax.dot_general(a, b, (((1,), (1,)), ((), ())), preferred_element_type=F32)


def dot_tn(a, b):
    return lax.dot_general(a, b, (((0,), (0,)), ((), ())), preferred_element_type=F32)


def tiles_of(block):
    parts = [
        block[:, t * TILE : (t + 1) * TILE, :].reshape(PER, block.shape[2])
        for t in range(block.shape[1] // TILE)
    ]
    return jnp.concatenate(parts, axis=0)


def normalise(flat):
    mean = jnp.mean(flat, axis=-1, keepdims=True)
    centred = flat - mean
    inv_std = lax.rsqrt(jnp.mean(centred * centred, axis=-1, keepdims=True) + norm_epsilon)
    return centred * inv_std, inv_std


def pair_ones(width):
    row = lax.broadcasted_iota(jnp.int32, (2 * width, 2 * width), 0) // width
    col = lax.broadcasted_iota(jnp.int32, (2 * width, 2 * width), 1) // width
    return (row == col).astype(F32).astype(BF16)


def head_sums(x, ones):
    step = ones.shape[0]
    high = x.astype(BF16)
    low = (x - high.astype(F32)).astype(BF16)
    parts = [
        dot(high[:, p : p + step], ones) + dot(low[:, p : p + step], ones)
        for p in range(0, x.shape[1], step)
    ]
    return jnp.concatenate(parts, axis=1)


def head_normalise(raw, ones, width):
    factor = lax.rsqrt(head_sums(raw * raw, ones) * (1.0 / width) + head_epsilon)
    return raw * factor, factor


def head_back(normal, factor, upstream, ones, width):
    inner = head_sums(upstream * normal, ones) * (1.0 / width)
    return factor * (upstream - normal * inner)


def split_heads(pair, width):
    lane = lax.broadcasted_iota(jnp.int32, (1, 2 * width), 1)
    first = (lane < width).astype(F32).astype(BF16)
    second = (lane >= width).astype(F32).astype(BF16)
    return jnp.concatenate([pair * first, pair * second], axis=0)


def join_heads(stacked, width):
    half = stacked.shape[0] // 2
    lane = lax.broadcasted_iota(jnp.int32, (1, 2 * width), 1)
    return jnp.where(lane < width, stacked[:half], stacked[half:])


def strip_tiles(groups, refs):
    tiles = []
    for s in range(3):
        own, *sides = refs[s * (groups - 1) : (s + 1) * (groups - 1)]
        tiles += [own.at[0], own.at[1]] + list(sides)
    return tiles


def near_rows(groups, odd, n_tiles):
    lanes = n_tiles * PER
    group = (lax.broadcasted_iota(jnp.int32, (1, lanes), 1) // PER) % groups
    oddf = odd.astype(F32)
    left = jnp.where(group == 2, oddf, jnp.where(group == 3, 1.0 - oddf, 1.0))
    right = jnp.where(group == 2, 1.0 - oddf, jnp.where(group == 3, oddf, 1.0))
    return left, right


def prep_kernel(scalars, tissue, tokens, low_out, send_a_out, send_b_out):
    odd = scalars[0]
    normed, _ = normalise(tiles_of(tokens[...].astype(F32)))
    low = normed.astype(BF16)
    width = low.shape[1]
    for t in range(2):
        low_out[t, 0:PER, :] = low[t * PER : (t + 1) * PER]
        low_out[t, PER:BLK, :] = jnp.full((BLK - PER, width), tissue[0, t].astype(F32)).astype(BF16)
    send_a_out[...] = low_out[1 - odd]
    if send_b_out is not None:
        send_b_out[...] = low_out[odd]


def forward_kernel(groups, place, *refs):
    scalars, wblk, tokens, teacher = refs[:4]
    n_sides = 3 * (groups - 1)
    tiles = strip_tiles(groups, refs[4 : 4 + n_sides])
    (
        wq_out,
        wk_out,
        wv_out,
        x_out,
        k_out,
        v_out,
        kn_out,
        kf_out,
        mixed_out,
        gout_out,
        near_out,
        stats_out,
        pack_out,
        *sends_out,
        wo_scr,
    ) = refs[4 + n_sides :]
    odd, base = scalars[0], scalars[1]
    n_blocks, per_block, model = wblk.shape
    width = model // HEADS
    own = 2 * PER
    per_matrix = n_blocks // 4
    for d in range(n_blocks):
        whole = (wq_out, wk_out, wv_out, wo_scr)[d // per_matrix]
        at = d % per_matrix * per_block
        whole[at : at + per_block, :] = wblk[jnp.bitwise_xor(base, place[d])]
    n_tiles = 3 * groups
    flag_rows = []
    for n, tile in enumerate(tiles):
        x_out[n * PER : (n + 1) * PER, :] = tile[0:PER, :]
        flag_rows.append(tile[PER:BLK, :].astype(F32)[0:1, 0:PER])
    ones = pair_ones(width)
    x = x_out[...]
    k_raw = dot(x, wk_out[...])
    k_normal, k_factor = head_normalise(k_raw, ones, width)
    kn_out[...] = k_normal[0:own]
    kf_out[...] = k_factor[0:own]
    keys = k_normal.astype(BF16)
    k_out[...] = keys
    values = dot(x, wv_out[...]).astype(BF16)
    v_out[...] = values
    q_normal, _ = head_normalise(dot(x[0:own], wq_out[...]), ones, width)
    queries = q_normal.astype(BF16)

    flags = jnp.concatenate(flag_rows, axis=1)
    left, right = near_rows(groups, odd, n_tiles)
    near_out[...] = jnp.concatenate([flags * left, flags * right], axis=0)
    near = jnp.stack([flags * left, flags * right] * 2)
    own_mask = [flag_rows[t][0:1, 0:1] for t in range(2)]
    query_mask = jnp.concatenate(
        [jnp.broadcast_to(own_mask[t], (PER, 1)) for t in range(2)], axis=0
    )
    rest = 1.0 - jnp.concatenate([query_mask, query_mask], axis=0).reshape(4, PER, 1)
    scale = 1.0 / math.sqrt(width)
    mixed_parts, inverses = [], []
    for p in range(HEADS // 2):
        lanes = slice(2 * width * p, 2 * width * (p + 1))
        scores = dot_nt(split_heads(queries[:, lanes], width), keys[:, lanes]) * scale
        raised = jnp.exp(scores).reshape(4, PER, n_tiles * PER) * near
        total = jnp.sum(raised, axis=-1, keepdims=True) + rest
        inverse = (1.0 / total).astype(BF16).astype(F32)
        low = (raised * inverse).reshape(4 * PER, n_tiles * PER).astype(BF16)
        mixed_parts.append(join_heads(dot(low, values[:, lanes]), width))
        inverse = inverse.reshape(4 * PER, 1)
        inverses += [inverse[0:own], inverse[own:]]
    mixed = (jnp.concatenate(mixed_parts, axis=1) * query_mask).astype(BF16)
    mixed_out[...] = mixed
    w_o = wo_scr[...]
    residual = tiles_of(tokens[...].astype(F32)) + dot(mixed, w_o)
    grad_out = query_mask * (residual - tiles_of(teacher[...].astype(F32)))
    gout_out[...] = grad_out
    grad_mixed = dot_nt(grad_out.astype(BF16), w_o).astype(BF16)
    delta = head_sums(grad_mixed.astype(F32) * mixed.astype(F32), ones)
    lane = lax.broadcasted_iota(jnp.int32, (1, own), 1)
    table = jnp.zeros((own, own), F32)
    for h in range(HEADS):
        table = jnp.where(lane == h, inverses[h], table)
        table = jnp.where(lane == HEADS + h, delta[:, h * width : h * width + 1], table)
    stats_out[...] = table
    stats = table.T[0:16, :]
    for t in range(2):
        here = slice(t * PER, (t + 1) * PER)
        pack_out[t, 0:PER, :] = grad_mixed[here]
        padded = jnp.concatenate([stats[:, here], jnp.zeros((16, model - PER), F32)], axis=1)
        pack_out[t, PER:BLK, :] = padded.astype(BF16)
    sends_out[0][...] = pack_out[1 - odd]
    if len(sends_out) > 1:
        sends_out[1][...] = pack_out[odd]


def store_terms(fast, odd, grads, outs):
    if not fast:
        for m, grad in enumerate(grads):
            outs[0][m] = grad
        return
    keep, send = outs
    rows = keep.shape[2]
    for m, grad in enumerate(grads):
        for b in range(keep.shape[1]):
            even_part = grad[2 * b * rows : (2 * b + 1) * rows]
            odd_part = grad[(2 * b + 1) * rows : (2 * b + 2) * rows]
            is_odd = odd == 1
            keep[m, b] = jnp.where(is_odd, odd_part, even_part)
            send[m, b] = jnp.where(is_odd, even_part, odd_part).astype(BF16)


def query_kernel(fast, scalars, wq, x, k, v, mixed, gout, near_in, stats_in, pack, q_out, gl_out, *outs):
    core = scalars[2]
    model = wq.shape[0]
    width = model // HEADS
    own = 2 * PER
    n_tiles = near_in.shape[1] // PER
    ones = pair_ones(width)
    q_normal, q_factor = head_normalise(dot(x[...], wq[...]), ones, width)
    q_all = q_normal.astype(BF16)
    q_out[...] = q_all
    q_normal, q_factor, queries = q_normal[0:own], q_factor[0:own], q_all[0:own]
    near = jnp.stack([near_in[0:1], near_in[1:2]] * 2)
    stats = stats_in[...].astype(BF16).astype(F32)
    grad_mixed = jnp.concatenate([pack[t, 0:PER, :] for t in range(2)], axis=0)
    scale = 1.0 / math.sqrt(width)
    parts = []
    for p in range(HEADS // 2):
        lanes = slice(2 * width * p, 2 * width * (p + 1))
        keys, values = k[:, lanes], v[:, lanes]
        scores = dot_nt(split_heads(queries[:, lanes], width), keys) * scale
        inverse = jnp.concatenate([stats[:, 2 * p : 2 * p + 1], stats[:, 2 * p + 1 : 2 * p + 2]], axis=0)
        at = HEADS + 2 * p
        delta = jnp.concatenate([stats[:, at : at + 1], stats[:, at + 1 : at + 2]], axis=0)
        full = jnp.exp(scores).reshape(4, PER, n_tiles * PER) * near
        full = full.reshape(4 * PER, n_tiles * PER) * inverse
        grad_attn = dot_nt(split_heads(grad_mixed[:, lanes], width), values)
        grad_scores = (full * (grad_attn - delta) * scale).astype(BF16)
        parts.append(join_heads(dot(grad_scores, keys), width))
    grad_qn = jnp.concatenate(parts, axis=1)
    grad_query = head_back(q_normal, q_factor, grad_qn, ones, width).astype(BF16)
    gl_out[...] = dot_nt(grad_query, wq[...])
    grad_wq = dot_tn(x[0:own, :], grad_query)
    grad_wo = dot_tn(mixed[...], gout[...].astype(BF16))
    store_terms(fast, core, [grad_wq, grad_wo], outs)


def key_kernel(groups, fast, scalars, x, k, v, q, kn, kf, near_in, *refs):
    n_sides = 3 * (groups - 1)
    tiles = strip_tiles(groups, refs[:n_sides])
    gk_out, gv_out, *outs, g_scr = refs[n_sides:]
    odd, core = scalars[0], scalars[2]
    model = q.shape[1]
    width = model // HEADS
    own = 2 * PER
    n_tiles = 3 * groups
    ones = pair_ones(width)
    stat_parts = []
    for n, tile in enumerate(tiles):
        g_scr[n * PER : (n + 1) * PER, :] = tile[0:PER, :]
        stat_parts.append(tile[PER:BLK, :].astype(F32)[:, 0:PER])
    stats = jnp.concatenate(stat_parts, axis=1)
    left, right = near_rows(groups, odd, n_tiles)
    near = [left * near_in[0:1, 0:1], right * near_in[0:1, PER : PER + 1]]
    scale = 1.0 / math.sqrt(width)
    key_parts, value_parts = [], []
    for p in range(HEADS // 2):
        lanes = slice(2 * width * p, 2 * width * (p + 1))
        queries, grads = q[:, lanes], g_scr[:, lanes]
        scores = dot_nt(split_heads(k[0:own, lanes], width), queries) * scale
        inv = [stats[2 * p + j : 2 * p + j + 1] for j in range(2)]
        rows = jnp.stack([inv[j] * near[t] for j in range(2) for t in range(2)])
        at = HEADS + 2 * p
        delta = jnp.stack([stats[at + j : at + j + 1] for j in range(2) for _ in range(2)])
        full = jnp.exp(scores).reshape(4, PER, n_tiles * PER) * rows
        grad_attn = dot_nt(split_heads(v[0:own, lanes], width), grads)
        grad_attn = grad_attn.reshape(4, PER, n_tiles * PER) - delta
        grad_scores = (full * grad_attn * scale).reshape(4 * PER, n_tiles * PER).astype(BF16)
        low = full.reshape(4 * PER, n_tiles * PER).astype(BF16)
        key_parts.append(join_heads(dot(grad_scores, queries), width))
        value_parts.append(join_heads(dot(low, grads), width))
    grad_kn = jnp.concatenate(key_parts, axis=1)
    grad_key = head_back(kn[...], kf[...], grad_kn, ones, width).astype(BF16)
    grad_value = jnp.concatenate(value_parts, axis=1).astype(BF16)
    gk_out[...] = grad_key
    gv_out[...] = grad_value
    x_own = x[0:own, :]
    store_terms(fast, core, [dot_tn(x_own, grad_key), dot_tn(x_own, grad_value)], outs)


def final_kernel(tokens, wk, wv, gk, gv, gl, gout, out):
    model = gk.shape[1]
    grad_lowered = gl[...] + dot_nt(gk[...], wk[...]) + dot_nt(gv[...], wv[...])
    normed, inv_std = normalise(tiles_of(tokens[...].astype(F32)))
    grads = gout[...] + inv_std * (
        grad_lowered
        - jnp.mean(grad_lowered, axis=-1, keepdims=True)
        - normed * jnp.mean(grad_lowered * normed, axis=-1, keepdims=True)
    )
    pieces = [grads[t * PER : (t + 1) * PER].reshape(TILE, TILE, model) for t in range(2)]
    out[...] = jnp.concatenate(pieces, axis=1).astype(BF16)


SMEM = pl.BlockSpec(memory_space=pltpu.SMEM)
VMEM = pl.BlockSpec(memory_space=pltpu.VMEM)


def call(kernel, in_specs, shapes, args, scratch=()):
    return pl.pallas_call(
        kernel,
        out_shape=[jax.ShapeDtypeStruct(s, t) for s, t in shapes],
        in_specs=in_specs,
        out_specs=[VMEM] * len(shapes),
        scratch_shapes=list(scratch),
    )(*args)


def swap(value, count, mask):
    return lax.ppermute(value, AXES, [(i, i ^ mask) for i in range(count)])


def side_pairs(length, side):
    if side is None:
        return [(i, i) for i in range(length)]
    pairs = []
    for i in range(side, length - 1, 2):
        pairs += [(i, i + 1), (i + 1, i)]
    return pairs


def around(own, sides):
    rows, cols = lax.axis_size("rows"), lax.axis_size("cols")
    parts = []
    for strip in (None, 0, 1):
        for side, value in [(None, own)] + list(enumerate(sides)):
            if strip is None and side is None:
                parts.append(value)
                continue
            pairs = [
                (r * cols + c, to_r * cols + to_c)
                for r, to_r in side_pairs(rows, strip)
                for c, to_c in side_pairs(cols, side)
            ]
            parts.append(lax.ppermute(value, AXES, pairs))
    return parts


def layer(tokens, teacher, tissue, weights):
    model = tokens.shape[2]
    rows, cols = lax.axis_size("rows"), lax.axis_size("cols")
    count = rows * cols
    groups = 3 if cols == 2 else 4
    n_sides = 3 * (groups - 1)
    per_block = 4 * model // count
    fast = count & (count - 1) == 0 and count >= 16 and per_block % 16 == 0
    per_matrix = count // 4
    spots = per_matrix // 2
    index = lax.axis_index("rows") * cols + lax.axis_index("cols")
    odd = lax.axis_index("cols") % 2
    own = 2 * PER
    n_keys = 3 * groups * PER

    def spot(d):
        return (d % 2) * (count // 2) + (d // 2 % spots) * 4 + d // per_matrix

    if fast:
        place, base = [spot(d) for d in range(count)], spot(index)
    else:
        place, base = list(range(4)), jnp.int32(0)
    scalars = jnp.stack([odd, base, index % 2, index]).astype(jnp.int32)

    tile_shape = ((BLK, model), BF16)
    sends_shape = [tile_shape] * (groups - 2)
    prep = prep_kernel if groups == 4 else lambda *refs: prep_kernel(*refs, None)
    low, *sends = call(
        prep, [SMEM, SMEM, VMEM], [((2, BLK, model), BF16)] + sends_shape, (scalars, tissue, tokens)
    )
    if fast:
        wblk = weights.reshape(1, per_block, model)
        parts = [swap(wblk, count, per_matrix * step) for step in range(1, 4)]
        wblk = jnp.concatenate([wblk] + parts, axis=0)
        wblk, low, sends = lax.optimization_barrier((wblk, low, sends))
        parts = [swap(wblk, count, 2 * step) for step in range(1, spots)]
        sides = around(low, sends)
        wblk = jnp.concatenate([wblk] + parts, axis=0)
        wblk, sides = lax.optimization_barrier((wblk, sides))
        wblk = jnp.concatenate([wblk, swap(wblk, count, 1)], axis=0)
    else:
        sides = around(low, sends)
        wblk = lax.all_gather(weights, AXES, axis=0, tiled=True).reshape(4, model, model)

    wq, wk, wv, x, k, v, kn, kf, mixed, gout, near, stats, pack, *sends = call(
        functools.partial(forward_kernel, groups, place),
        [SMEM] + [VMEM] * (3 + n_sides),
        [((model, model), BF16)] * 3
        + [((n_keys, model), BF16)] * 3
        + [
            ((own, model), F32),
            ((own, model), F32),
            ((own, model), BF16),
            ((own, model), F32),
            ((2, n_keys), F32),
            ((own, own), F32),
            ((2, BLK, model), BF16),
        ]
        + sends_shape,
        (scalars, wblk, tokens, teacher, *sides),
        scratch=[pltpu.VMEM((model, model), BF16)],
    )
    packs = around(pack, sends)

    if fast:
        term_shapes = [
            ((2, spots, per_block, model), F32),
            ((2, spots, per_block, model), BF16),
        ]
    else:
        term_shapes = [((2, model, model), F32)]
    q, gl, *terms_qo = call(
        functools.partial(query_kernel, fast),
        [SMEM] + [VMEM] * 9,
        [((n_keys, model), BF16), ((own, model), F32)] + term_shapes,
        (scalars, wq, x, k, v, mixed, gout, near, stats, pack),
    )
    gk, gv, *terms_kv = call(
        functools.partial(key_kernel, groups, fast),
        [SMEM] + [VMEM] * (7 + n_sides),
        [((own, model), BF16), ((own, model), BF16)] + term_shapes,
        (scalars, x, k, v, q, kn, kf, near, *packs),
        scratch=[pltpu.VMEM((n_keys, model), BF16)],
    )
    (grads,) = call(
        final_kernel, [VMEM] * 7, [(tokens.shape, BF16)], (tokens, wk, wv, gk, gv, gl, gout)
    )

    n_tokens = tokens.shape[0] * rows * tokens.shape[1] * cols
    norm = math.sqrt(n_tokens)
    if not fast:
        whole = jnp.stack([terms_qo[0][0], terms_kv[0][0], terms_kv[0][1], terms_qo[0][1]])
        sums = lax.psum_scatter(whole.reshape(-1), AXES, scatter_dimension=0, tiled=True)
        return grads, sums / norm

    here, mine = index // 2 % spots, index // per_matrix

    def pick(values, at, axis):
        return lax.dynamic_index_in_dim(values, at, axis, keepdims=False)

    def with_core(keep, send):
        return keep + swap(send, count, 1).astype(F32)

    sums_qo = with_core(*terms_qo)
    sums_kv = with_core(*terms_kv)

    def all_four(at):
        qo, kv = pick(sums_qo, at, 1), pick(sums_kv, at, 1)
        return jnp.concatenate([qo[0:1], kv, qo[1:2]], axis=0)

    arrived = [
        swap(all_four(here ^ step).astype(BF16), count, 2 * step) for step in range(1, spots)
    ]
    pieces = all_four(here)
    for part in arrived:
        pieces = pieces + part.astype(F32)
    arrived = [
        swap(pick(pieces, mine ^ step, 0).astype(BF16), count, per_matrix * step)
        for step in range(1, 4)
    ]
    result = pick(pieces, mine, 0)
    for part in arrived:
        result = result + part.astype(F32)
    return grads, (result / norm).reshape(-1)


def solution(mesh):
    return jax.shard_map(
        layer,
        mesh=mesh,
        in_specs=(
            P("rows", "cols", None),
            P("rows", "cols", None),
            P("rows", "cols"),
            P(("rows", "cols")),
        ),
        out_specs=(P("rows", "cols", None), P(("rows", "cols"))),
        check_vma=False,
    )
```

profile of v0, /device:TPU:0, one launch (start us, length us, event | category | flops | bytes accessed | tf_op | source)
XLA Modules:
  0.0 83.5 jit_solution(5006730973228192598)
XLA Ops:
  0.6 0.8 reshape.27
  1.4 5.1 %collective-permute-start.2 = (bf16[1,48,384]{2,1,0:T(8,128)(2,1)S(1)}, bf16[1,48,384]{2,1,0:T(8,128)(2,1)S(1)}, u32[]{:S(2)}, u32[]{:S(2)}) collective-permute-start(bf16[1,48,384]{2,1,0:T(8,128)(2,1)S(1)} %reshape.27), channel_id=1, source_target_pairs={{0,24},{1,25},{2,26},{3,27},{4,28},{5,29},{6,30},{7,31},{8,16},{9,... | collective-permute-start | bytes 110600 | tf_op jit(solution)/shard_map/ppermute | solution.py:339
  6.6 0.0 collective-permute-start.1
  6.6 0.6 collective-permute-start
  7.2 0.6 pad_add_fusion.refs_0_.scalars
  7.9 1.8 %shard_map.59 = (bf16[2,80,384]{2,1,0:T(8,128)(2,1)}, bf16[80,384]{1,0:T(8,128)(2,1)}) custom-call(s32[4]{0:T(128)} %pad_add_fusion.refs_0_.scalars, s32[1,2]{1,0:T(1,128)} %refs_1_.1, bf16[8,16,384]{2,1,0:T(8,128)(2,1)} %tokens.1), custom_call_target="tpu_custom_call" | custom-call | tf_op jit(solution)/shard_map/pallas_call | solution.py:329
  9.6 0.0 collective-permute-done.2
  9.6 1.8 %collective-permute-done.1 = bf16[1,48,384]{2,1,0:T(8,128)(2,1)S(1)} collective-permute-done((bf16[1,48,384]{2,1,0:T(8,128)(2,1)S(1)}, bf16[1,48,384]{2,1,0:T(8,128)(2,1)S(1)}, u32[]{:S(2)}, u32[]{:S(2)}) %collective-permute-start.1) | collective-permute-done | bytes 36896 | tf_op jit(solution)/shard_map/ppermute | solution.py:339
  11.4 0.0 collective-permute-done
  11.5 2.5 %collective-permute-start.5 = (bf16[4,48,384]{2,1,0:T(8,128)(2,1)S(1)}, bf16[4,48,384]{2,1,0:T(8,128)(2,1)S(1)}, u32[]{:S(2)}, u32[]{:S(2)}) collective-permute-start(bf16[4,48,384]{2,1,0:T(8,128)(2,1)S(1)} %pad_maximum_fusion.2), channel_id=1, source_target_pairs={{0,6},{1,7},{2,4},{3,5},{4,2},{5,3},{6,0},{7,1},{8,14},{9,15},{10,... | collective-permute-start | bytes 442376 | tf_op jit(solution)/shard_map/ppermute | solution.py:339
  14.0 0.5 collective-permute-start.4
  14.5 0.5 collective-permute-start.3
  15.0 0.0 collective-permute-start.6
  15.0 1.6 %collective-permute-start.8 = (bf16[80,384]{1,0:T(8,128)(2,1)}, bf16[80,384]{1,0:T(8,128)(2,1)S(1)}, u32[]{:S(2)}, u32[]{:S(2)}) collective-permute-start(bf16[80,384]{1,0:T(8,128)(2,1)} %get-tuple-element.40), channel_id=1, source_target_pairs={{0,3},{1,2},{2,1},{3,0},{4,7},{5,6},{6,5},{7,4},{8,11},{9,10},{10,... | collective-permute-start | bytes 184328 | tf_op jit(solution)/shard_map/ppermute | solution.py:364
  16.6 2.5 %collective-permute-done.5 = bf16[4,48,384]{2,1,0:T(8,128)(2,1)S(1)} collective-permute-done((bf16[4,48,384]{2,1,0:T(8,128)(2,1)S(1)}, bf16[4,48,384]{2,1,0:T(8,128)(2,1)S(1)}, u32[]{:S(2)}, u32[]{:S(2)}) %collective-permute-start.5) | collective-permute-done | bytes 147488 | tf_op jit(solution)/shard_map/ppermute | solution.py:339
  19.1 0.6 collective-permute-start.7
  19.8 0.2 collective-permute-done.4
  19.9 0.7 collective-permute-start.9
  20.6 0.9 %collective-permute-done.3 = bf16[4,48,384]{2,1,0:T(8,128)(2,1)S(1)} collective-permute-done((bf16[4,48,384]{2,1,0:T(8,128)(2,1)S(1)}, bf16[4,48,384]{2,1,0:T(8,128)(2,1)S(1)}, u32[]{:S(2)}, u32[]{:S(2)}) %collective-permute-start.3) | collective-permute-done | bytes 147488 | tf_op jit(solution)/shard_map/ppermute | solution.py:339
  21.4 0.7 collective-permute-start.10
  22.1 0.1 pad_maximum_fusion.1
  22.2 0.0 collective-permute-done.6.refs_5_
  22.2 0.0 collective-permute-done.8.refs_7_
  22.2 0.0 collective-permute-done.10.refs_9_
  22.3 2.0 %collective-permute-done.7.refs_6_ = bf16[2,80,384]{2,1,0:T(8,128)(2,1)S(1)} collective-permute-done((bf16[2,80,384]{2,1,0:T(8,128)(2,1)}, bf16[2,80,384]{2,1,0:T(8,128)(2,1)S(1)}, u32[]{:S(2)}, u32[]{:S(2)}) %collective-permute-start.7) | collective-permute-done | bytes 122912 | tf_op jit(solution)/shard_map/ppermute | solution.py:364
  24.3 0.1 collective-permute-start.11
  24.3 2.0 %collective-permute-done.11 = bf16[16,48,384]{2,1,0:T(8,128)(2,1)S(1)} collective-permute-done((bf16[16,48,384]{2,1,0:T(8,128)(2,1)S(1)}, bf16[16,48,384]{2,1,0:T(8,128)(2,1)S(1)}, u32[]{:S(2)}, u32[]{:S(2)}) %collective-permute-start.11) | collective-permute-done | bytes 589856 | tf_op jit(solution)/shard_map/ppermute | solution.py:339
  26.3 1.2 %pad_maximum_fusion.refs_1_ = bf16[32,48,384]{2,1,0:T(8,128)(2,1)} fusion(bf16[16,48,384]{2,1,0:T(8,128)(2,1)S(1)} %collective-permute-done.11, bf16[16,48,384]{2,1,0:T(8,128)(2,1)S(1)} %pad_maximum_fusion.1), kind=kLoop, calls=%fused_computation | loop fusion | flops 589824 | bytes 2359296 | tf_op jit(solution)/shard_map/concatenate | solution.py:407
  27.5 6.1 %shard_map.60 = (bf16[384,384]{1,0:T(8,128)(2,1)}, bf16[384,384]{1,0:T(8,128)(2,1)}, bf16[384,384]{1,0:T(8,128)(2,1)}, bf16[576,384]{1,0:T(8,128)(2,1)}, bf16[57...) custom-call(s32[4]{0:T(128)} %pad_add_fusion.refs_0_.scalars, ...), custom_call_target="tpu_custom_call" | custom-call | tf_op jit(solution)/shard_map/pallas_call | solution.py:329
  33.6 4.7 %shard_map.61 = (bf16[576,384]{1,0:T(8,128)(2,1)}, f32[128,384]{1,0:T(8,128)}, f32[2,4,48,384]{3,2,1,0:T(8,128)}, bf16[2,4,48,384]{3,2,1,0:T(8,128)(2,1)}) custom-call(s32[4]{0:T(128)} %pad_add_fusion.refs_0_.scalars, bf16[384,384]{1,0:T(8,128)(2,1)} %get-tuple-element.53.wq, bf16[576,384]{1,0:T(8,128)(2,1)} %get-tuple-element.50.x, ...), custom_call_target="tpu_custom_call" | custom-call | tf_op jit(solution)/shard_map/pallas_call | solution.py:329
  38.3 0.1 collective-permute-start.17
  38.5 0.4 collective-permute-start.12
  38.8 7.1 %collective-permute-start.13 = (bf16[2,80,384]{2,1,0:T(8,128)(2,1)S(1)}, bf16[2,80,384]{2,1,0:T(8,128)(2,1)S(1)}, u32[]{:S(2)}, u32[]{:S(2)}) collective-permute-start(bf16[2,80,384]{2,1,0:T(8,128)(2,1)S(1)} %copy-done.2), channel_id=1, source_target_pairs={{0,2},{1,3},{2,0},{3,1},{4,6},{5,7},{6,4},{7,5},{8,10},{9,11},{10,... | collective-permute-start | bytes 368648 | tf_op jit(solution)/shard_map/ppermute | solution.py:364
  46.0 0.7 collective-permute-start.15
  46.6 3.4 %collective-permute-start.14 = (bf16[80,384]{1,0:T(8,128)(2,1)S(1)}, bf16[80,384]{1,0:T(8,128)(2,1)S(1)}, u32[]{:S(2)}, u32[]{:S(2)}) collective-permute-start(bf16[80,384]{1,0:T(8,128)(2,1)S(1)} %copy-done.13), channel_id=1, source_target_pairs={{0,3},{1,2},{2,1},{3,0},{4,7},{5,6},{6,5},{7,4},{8,11},{9,10},{10,... | collective-permute-start | bytes 184328 | tf_op jit(solution)/shard_map/ppermute | solution.py:364
  50.0 0.0 collective-permute-done.12.refs_1_
  50.0 0.7 collective-permute-start.16
  50.7 3.3 %collective-permute-done.14.refs_3_ = bf16[80,384]{1,0:T(8,128)(2,1)S(1)} collective-permute-done((bf16[80,384]{1,0:T(8,128)(2,1)S(1)}, bf16[80,384]{1,0:T(8,128)(2,1)S(1)}, u32[]{:S(2)}, u32[]{:S(2)}) %collective-permute-start.14) | collective-permute-done | bytes 61472 | tf_op jit(solution)/shard_map/ppermute | solution.py:364
  54.0 0.0 collective-permute-done.16.refs_5_
  54.0 0.0 collective-permute-done.13.refs_2_
  54.0 0.0 collective-permute-done.15.refs_4_
  54.1 0.6 copy-done.8
  54.6 0.0 copy-done.9
  54.7 0.1 copy-done.3
  54.7 0.0 copy-done.4
  54.8 4.4 %shard_map.62 = (bf16[128,384]{1,0:T(8,128)(2,1)}, bf16[128,384]{1,0:T(8,128)(2,1)}, f32[2,4,48,384]{3,2,1,0:T(8,128)}, bf16[2,4,48,384]{3,2,1,0:T(8,128)(2,1)}) custom-call(s32[4]{0:T(128)} %pad_add_fusion.refs_0_.scalars, bf16[576,384]{1,0:T(8,128)(2,1)} %get-tuple-element.50.x, bf16[576,384]{1,0:T(8,128)(2,1)} %get-tuple-element.51.k, ...), custom_call_target="tpu_custom_call" | custom-call | tf_op jit(solution)/shard_map/pallas_call | solution.py:329
  59.1 0.9 %collective-permute-start.18 = (bf16[2,4,48,384]{3,2,1,0:T(8,128)(2,1)}, bf16[2,4,48,384]{3,2,1,0:T(8,128)(2,1)S(1)}, u32[]{:S(2)}, u32[]{:S(2)}) collective-permute-start(bf16[2,4,48,384]{3,2,1,0:T(8,128)(2,1)} %get-tuple-element.69), channel_id=1, source_target_pairs={{0,1},{1,0},{2,3},{3,2},{4,5},{5,4},{6,7},{7,6},{8,9},{9,8},{10,11... | collective-permute-start | bytes 884744 | tf_op jit(solution)/shard_map/ppermute | solution.py:339
  60.0 0.0 collective-permute-done.17
  60.0 0.1 convert_add_fusion.1
  60.2 1.3 %collective-permute-done.18 = bf16[2,4,48,384]{3,2,1,0:T(8,128)(2,1)S(1)} collective-permute-done((bf16[2,4,48,384]{3,2,1,0:T(8,128)(2,1)}, bf16[2,4,48,384]{3,2,1,0:T(8,128)(2,1)S(1)}, u32[]{:S(2)}, u32[]{:S(2)}) %collective-permute-start.18) | collective-permute-done | bytes 294944 | tf_op jit(solution)/shard_map/ppermute | solution.py:339
  61.5 0.1 convert_add_fusion
  61.6 5.0 %collective-permute-start.21 = (bf16[4,48,384]{2,1,0:T(8,128)(2,1)S(1)}, bf16[4,48,384]{2,1,0:T(8,128)(2,1)S(1)}, u32[]{:S(2)}, u32[]{:S(2)}) collective-permute-start(bf16[4,48,384]{2,1,0:T(8,128)(2,1)S(1)} %pad_maximum_fusion.5), channel_id=1, source_target_pairs={{0,6},{1,7},{2,4},{3,5},{4,2},{5,3},{6,0},{7,1},{8,14},{9,15},{10,... | collective-permute-start | bytes 442376 | tf_op jit(solution)/shard_map/ppermute | solution.py:339
  66.6 0.1 collective-permute-start.20
  66.7 0.6 collective-permute-start.19
  67.4 3.7 %collective-permute-done.21 = bf16[4,48,384]{2,1,0:T(8,128)(2,1)S(1)} collective-permute-done((bf16[4,48,384]{2,1,0:T(8,128)(2,1)S(1)}, bf16[4,48,384]{2,1,0:T(8,128)(2,1)S(1)}, u32[]{:S(2)}, u32[]{:S(2)}) %collective-permute-start.21) | collective-permute-done | bytes 147488 | tf_op jit(solution)/shard_map/ppermute | solution.py:339
  71.0 2.8 %collective-permute-done.20 = bf16[4,48,384]{2,1,0:T(8,128)(2,1)S(1)} collective-permute-done((bf16[4,48,384]{2,1,0:T(8,128)(2,1)S(1)}, bf16[4,48,384]{2,1,0:T(8,128)(2,1)S(1)}, u32[]{:S(2)}, u32[]{:S(2)}) %collective-permute-start.20) | collective-permute-done | bytes 147488 | tf_op jit(solution)/shard_map/ppermute | solution.py:339
  73.9 0.1 collective-permute-done.19
  74.0 0.1 fusion.1
  74.1 2.6 %collective-permute-start.24 = (bf16[48,384]{1,0:T(8,128)(2,1)S(1)}, bf16[48,384]{1,0:T(8,128)(2,1)S(1)}, u32[]{:S(2)}, u32[]{:S(2)}) collective-permute-start(bf16[48,384]{1,0:T(8,128)(2,1)S(1)} %get-tuple-element.79), channel_id=1, source_target_pairs={{0,24},{1,25},{2,26},{3,27},{4,28},{5,29},{6,30},{7,31},{8,16},{9,... | collective-permute-start | bytes 110600 | tf_op jit(solution)/shard_map/ppermute | solution.py:339
  76.7 2.2 %collective-permute-start.23 = (bf16[48,384]{1,0:T(8,128)(2,1)S(1)}, bf16[48,384]{1,0:T(8,128)(2,1)S(1)}, u32[]{:S(2)}, u32[]{:S(2)}) collective-permute-start(bf16[48,384]{1,0:T(8,128)(2,1)S(1)} %get-tuple-element.80), channel_id=1, source_target_pairs={{0,16},{1,17},{2,18},{3,19},{4,20},{5,21},{6,22},{7,23},{8,24},{9,... | collective-permute-start | bytes 110600 | tf_op jit(solution)/shard_map/ppermute | solution.py:339
  78.9 2.4 %shard_map.63 = bf16[8,16,384]{2,1,0:T(8,128)(2,1)} custom-call(bf16[8,16,384]{2,1,0:T(8,128)(2,1)} %tokens.1, bf16[384,384]{1,0:T(8,128)(2,1)} %get-tuple-element.48.wk, bf16[384,384]{1,0:T(8,128)(2,1)} %get-tuple-element.49.wv, bf16[128,384]{1,0:T(8,128)(2,1)} %get-tuple-element.63.gk, bf16[128,384]{1,0:T(8,128)(2,1)} %get-tuple-element.64.gv, ...), custom_call_target="tpu_custom_call" | custom-call | tf_op jit(solution)/shard_map/pallas_call | solution.py:329
  81.3 0.5 collective-permute-done.23
  81.7 1.1 %collective-permute-done.22 = bf16[48,384]{1,0:T(8,128)(2,1)S(1)} collective-permute-done((bf16[48,384]{1,0:T(8,128)(2,1)S(1)}, bf16[48,384]{1,0:T(8,128)(2,1)S(1)}, u32[]{:S(2)}, u32[]{:S(2)}) %collective-permute-start.22) | collective-permute-done | bytes 36896 | tf_op jit(solution)/shard_map/ppermute | solution.py:339
  82.9 0.6 reshape.28
  (39 shorter events, 0.3 us)
Async XLA Ops:
  1.4 8.2 %collective-permute-start.2 = (bf16[1,48,384]{2,1,0:T(8,128)(2,1)S(1)}, bf16[1,48,384]{2,1,0:T(8,128)(2,1)S(1)}, u32[]{:S(2)}, u32[]{:S(2)}) collective-permute-start(bf16[1,48,384]{2,1,0:T(8,128)(2,1)S(1)} %reshape.27), channel_id=1, source_target_pairs={{0,24},{1,25},{2,26},{3,27},{4,28},{5,29},{6,30},{7,31},{8,16},{9,... | collective-permute-start | bytes 110600 | tf_op jit(solution)/shard_map/ppermute | solution.py:339
  6.6 4.9 %collective-permute-start.1 = (bf16[1,48,384]{2,1,0:T(8,128)(2,1)S(1)}, bf16[1,48,384]{2,1,0:T(8,128)(2,1)S(1)}, u32[]{:S(2)}, u32[]{:S(2)}) collective-permute-start(bf16[1,48,384]{2,1,0:T(8,128)(2,1)S(1)} %reshape.27), channel_id=1, source_target_pairs={{0,16},{1,17},{2,18},{3,19},{4,20},{5,21},{6,22},{7,23},{8,24},{9,... | collective-permute-start | bytes 110600 | tf_op jit(solution)/shard_map/ppermute | solution.py:339
  6.6 4.9 %collective-permute-start = (bf16[1,48,384]{2,1,0:T(8,128)(2,1)S(1)}, bf16[1,48,384]{2,1,0:T(8,128)(2,1)S(1)}, u32[]{:S(2)}, u32[]{:S(2)}) collective-permute-start(bf16[1,48,384]{2,1,0:T(8,128)(2,1)S(1)} %reshape.27), channel_id=1, source_target_pairs={{0,8},{1,9},{2,10},{3,11},{4,12},{5,13},{6,14},{7,15},{8,0},{9,1},... | collective-permute-start | bytes 110600 | tf_op jit(solution)/shard_map/ppermute | solution.py:339
  11.5 7.7 %collective-permute-start.5 = (bf16[4,48,384]{2,1,0:T(8,128)(2,1)S(1)}, bf16[4,48,384]{2,1,0:T(8,128)(2,1)S(1)}, u32[]{:S(2)}, u32[]{:S(2)}) collective-permute-start(bf16[4,48,384]{2,1,0:T(8,128)(2,1)S(1)} %pad_maximum_fusion.2), channel_id=1, source_target_pairs={{0,6},{1,7},{2,4},{3,5},{4,2},{5,3},{6,0},{7,1},{8,14},{9,15},{10,... | collective-permute-start | bytes 442376 | tf_op jit(solution)/shard_map/ppermute | solution.py:339
  14.0 6.0 %collective-permute-start.4 = (bf16[4,48,384]{2,1,0:T(8,128)(2,1)S(1)}, bf16[4,48,384]{2,1,0:T(8,128)(2,1)S(1)}, u32[]{:S(2)}, u32[]{:S(2)}) collective-permute-start(bf16[4,48,384]{2,1,0:T(8,128)(2,1)S(1)} %pad_maximum_fusion.2), channel_id=1, source_target_pairs={{0,4},{1,5},{2,6},{3,7},{4,0},{5,1},{6,2},{7,3},{8,12},{9,13},{10,... | collective-permute-start | bytes 442376 | tf_op jit(solution)/shard_map/ppermute | solution.py:339
  14.5 7.0 %collective-permute-start.3 = (bf16[4,48,384]{2,1,0:T(8,128)(2,1)S(1)}, bf16[4,48,384]{2,1,0:T(8,128)(2,1)S(1)}, u32[]{:S(2)}, u32[]{:S(2)}) collective-permute-start(bf16[4,48,384]{2,1,0:T(8,128)(2,1)S(1)} %pad_maximum_fusion.2), channel_id=1, source_target_pairs={{0,2},{1,3},{2,0},{3,1},{4,6},{5,7},{6,4},{7,5},{8,10},{9,11},{10,... | collective-permute-start | bytes 442376 | tf_op jit(solution)/shard_map/ppermute | solution.py:339
  15.0 7.2 %collective-permute-start.6 = (bf16[80,384]{1,0:T(8,128)(2,1)}, bf16[80,384]{1,0:T(8,128)(2,1)S(1)}, u32[]{:S(2)}, u32[]{:S(2)}) collective-permute-start(bf16[80,384]{1,0:T(8,128)(2,1)} %get-tuple-element.40), channel_id=1, source_target_pairs={{0,1},{1,0},{2,3},{3,2},{4,5},{5,4},{6,7},{7,6},{8,9},{9,8},{10,11... | collective-permute-start | bytes 184328 | tf_op jit(solution)/shard_map/ppermute | solution.py:364
  15.0 7.2 %collective-permute-start.8 = (bf16[80,384]{1,0:T(8,128)(2,1)}, bf16[80,384]{1,0:T(8,128)(2,1)S(1)}, u32[]{:S(2)}, u32[]{:S(2)}) collective-permute-start(bf16[80,384]{1,0:T(8,128)(2,1)} %get-tuple-element.40), channel_id=1, source_target_pairs={{0,3},{1,2},{2,1},{3,0},{4,7},{5,6},{6,5},{7,4},{8,11},{9,10},{10,... | collective-permute-start | bytes 184328 | tf_op jit(solution)/shard_map/ppermute | solution.py:364
  19.1 5.1 %collective-permute-start.7 = (bf16[2,80,384]{2,1,0:T(8,128)(2,1)}, bf16[2,80,384]{2,1,0:T(8,128)(2,1)S(1)}, u32[]{:S(2)}, u32[]{:S(2)}) collective-permute-start(bf16[2,80,384]{2,1,0:T(8,128)(2,1)} %get-tuple-element.42.refs_4_), channel_id=1, source_target_pairs={{0,2},{1,3},{2,0},{3,1},{4,6},{5,7},{6,4},{7,5},{8,10},{9,11},{10,... | collective-permute-start | bytes 368648 | tf_op jit(solution)/shard_map/ppermute | solution.py:364
  19.9 4.3 %collective-permute-start.9 = (bf16[2,80,384]{2,1,0:T(8,128)(2,1)}, bf16[2,80,384]{2,1,0:T(8,128)(2,1)S(1)}, u32[]{:S(2)}, u32[]{:S(2)}) collective-permute-start(bf16[2,80,384]{2,1,0:T(8,128)(2,1)} %get-tuple-element.42.refs_4_), channel_id=1, source_target_pairs={{2,4},{3,5},{4,2},{5,3},{6,8},{7,9},{8,6},{9,7},{10,12},{11,13},{1... | collective-permute-start | bytes 368648 | tf_op jit(solution)/shard_map/ppermute | solution.py:364
  21.4 0.8 collective-permute-start.10
  22.2 5.3 %copy-start.10 = (bf16[80,384]{1,0:T(8,128)(2,1)}, bf16[80,384]{1,0:T(8,128)(2,1)S(1)}, u32[]{:S(2)}) copy-start(bf16[80,384]{1,0:T(8,128)(2,1)S(1)} %collective-permute-done.6.refs_5_) | copy-start | bytes 184324
  22.2 5.3 %copy-start.11 = (bf16[80,384]{1,0:T(8,128)(2,1)}, bf16[80,384]{1,0:T(8,128)(2,1)S(1)}, u32[]{:S(2)}) copy-start(bf16[80,384]{1,0:T(8,128)(2,1)S(1)} %collective-permute-done.8.refs_7_) | copy-start | bytes 184324
  22.3 5.2 %copy-start.12 = (bf16[80,384]{1,0:T(8,128)(2,1)}, bf16[80,384]{1,0:T(8,128)(2,1)S(1)}, u32[]{:S(2)}) copy-start(bf16[80,384]{1,0:T(8,128)(2,1)S(1)} %collective-permute-done.10.refs_9_) | copy-start | bytes 184324
  24.3 3.2 %copy-start.5 = (bf16[2,80,384]{2,1,0:T(8,128)(2,1)}, bf16[2,80,384]{2,1,0:T(8,128)(2,1)S(1)}, u32[]{:S(2)}) copy-start(bf16[2,80,384]{2,1,0:T(8,128)(2,1)S(1)} %collective-permute-done.7.refs_6_) | copy-start | bytes 368644
  24.3 3.2 %copy-start.6 = (bf16[2,80,384]{2,1,0:T(8,128)(2,1)}, bf16[2,80,384]{2,1,0:T(8,128)(2,1)S(1)}, u32[]{:S(2)}) copy-start(bf16[2,80,384]{2,1,0:T(8,128)(2,1)S(1)} %collective-permute-done.9.refs_8_) | copy-start | bytes 368644
  24.3 2.0 %collective-permute-start.11 = (bf16[16,48,384]{2,1,0:T(8,128)(2,1)S(1)}, bf16[16,48,384]{2,1,0:T(8,128)(2,1)S(1)}, u32[]{:S(2)}, u32[]{:S(2)}) collective-permute-start(bf16[16,48,384]{2,1,0:T(8,128)(2,1)S(1)} %pad_maximum_fusion.1), channel_id=1, source_target_pairs={{0,1},{1,0},{2,3},{3,2},{4,5},{5,4},{6,7},{7,6},{8,9},{9,8},{10,11... | collective-permute-start | bytes 1769480 | tf_op jit(solution)/shard_map/ppermute | solution.py:339
  33.6 4.9 %copy-start.13 = (bf16[80,384]{1,0:T(8,128)(2,1)S(1)}, bf16[80,384]{1,0:T(8,128)(2,1)}, u32[]{:S(2)}) copy-start(bf16[80,384]{1,0:T(8,128)(2,1)} %get-tuple-element.62) | copy-start | bytes 184324
  33.6 5.2 %copy-start.2 = (bf16[2,80,384]{2,1,0:T(8,128)(2,1)S(1)}, bf16[2,80,384]{2,1,0:T(8,128)(2,1)}, u32[]{:S(2)}) copy-start(bf16[2,80,384]{2,1,0:T(8,128)(2,1)} %get-tuple-element.58.pack.refs_0_) | copy-start | bytes 368644
  38.3 21.7 %collective-permute-start.17 = (bf16[2,4,48,384]{3,2,1,0:T(8,128)(2,1)}, bf16[2,4,48,384]{3,2,1,0:T(8,128)(2,1)S(1)}, u32[]{:S(2)}, u32[]{:S(2)}) collective-permute-start(bf16[2,4,48,384]{3,2,1,0:T(8,128)(2,1)} %get-tuple-element.67), channel_id=1, source_target_pairs={{0,1},{1,0},{2,3},{3,2},{4,5},{5,4},{6,7},{7,6},{8,9},{9,8},{10,11... | collective-permute-start | bytes 884744 | tf_op jit(solution)/shard_map/ppermute | solution.py:339
  38.5 11.5 %collective-permute-start.12 = (bf16[80,384]{1,0:T(8,128)(2,1)S(1)}, bf16[80,384]{1,0:T(8,128)(2,1)S(1)}, u32[]{:S(2)}, u32[]{:S(2)}) collective-permute-start(bf16[80,384]{1,0:T(8,128)(2,1)S(1)} %copy-done.13), channel_id=1, source_target_pairs={{0,1},{1,0},{2,3},{3,2},{4,5},{5,4},{6,7},{7,6},{8,9},{9,8},{10,11... | collective-permute-start | bytes 184328 | tf_op jit(solution)/shard_map/ppermute | solution.py:364
  38.8 15.2 %collective-permute-start.13 = (bf16[2,80,384]{2,1,0:T(8,128)(2,1)S(1)}, bf16[2,80,384]{2,1,0:T(8,128)(2,1)S(1)}, u32[]{:S(2)}, u32[]{:S(2)}) collective-permute-start(bf16[2,80,384]{2,1,0:T(8,128)(2,1)S(1)} %copy-done.2), channel_id=1, source_target_pairs={{0,2},{1,3},{2,0},{3,1},{4,6},{5,7},{6,4},{7,5},{8,10},{9,11},{10,... | collective-permute-start | bytes 368648 | tf_op jit(solution)/shard_map/ppermute | solution.py:364
  46.0 8.1 %collective-permute-start.15 = (bf16[2,80,384]{2,1,0:T(8,128)(2,1)S(1)}, bf16[2,80,384]{2,1,0:T(8,128)(2,1)S(1)}, u32[]{:S(2)}, u32[]{:S(2)}) collective-permute-start(bf16[2,80,384]{2,1,0:T(8,128)(2,1)S(1)} %copy-done.2), channel_id=1, source_target_pairs={{2,4},{3,5},{4,2},{5,3},{6,8},{7,9},{8,6},{9,7},{10,12},{11,13},{1... | collective-permute-start | bytes 368648 | tf_op jit(solution)/shard_map/ppermute | solution.py:364
  46.6 7.4 %collective-permute-start.14 = (bf16[80,384]{1,0:T(8,128)(2,1)S(1)}, bf16[80,384]{1,0:T(8,128)(2,1)S(1)}, u32[]{:S(2)}, u32[]{:S(2)}) collective-permute-start(bf16[80,384]{1,0:T(8,128)(2,1)S(1)} %copy-done.13), channel_id=1, source_target_pairs={{0,3},{1,2},{2,1},{3,0},{4,7},{5,6},{6,5},{7,4},{8,11},{9,10},{10,... | collective-permute-start | bytes 184328 | tf_op jit(solution)/shard_map/ppermute | solution.py:364
  50.0 4.1 %copy-start.7 = (bf16[80,384]{1,0:T(8,128)(2,1)}, bf16[80,384]{1,0:T(8,128)(2,1)S(1)}, u32[]{:S(2)}) copy-start(bf16[80,384]{1,0:T(8,128)(2,1)S(1)} %collective-permute-done.12.refs_1_) | copy-start | bytes 184324
  50.0 4.0 %collective-permute-start.16 = (bf16[80,384]{1,0:T(8,128)(2,1)S(1)}, bf16[80,384]{1,0:T(8,128)(2,1)S(1)}, u32[]{:S(2)}, u32[]{:S(2)}) collective-permute-start(bf16[80,384]{1,0:T(8,128)(2,1)S(1)} %copy-done.13), channel_id=1, source_target_pairs={{2,5},{3,4},{4,3},{5,2},{6,9},{7,8},{8,7},{9,6},{10,13},{11,12},{1... | collective-permute-start | bytes 184328 | tf_op jit(solution)/shard_map/ppermute | solution.py:364
  54.0 0.6 copy-start.8
  54.0 0.6 copy-start.9
  54.0 0.7 copy-start.3
  54.1 0.7 copy-start.4
  54.8 5.3 %copy-start = (f32[2,4,48,384]{3,2,1,0:T(8,128)S(1)}, f32[2,4,48,384]{3,2,1,0:T(8,128)}, u32[]{:S(2)}) copy-start(f32[2,4,48,384]{3,2,1,0:T(8,128)} %get-tuple-element.66) | copy-start | bytes 1769476
  59.1 2.3 %collective-permute-start.18 = (bf16[2,4,48,384]{3,2,1,0:T(8,128)(2,1)}, bf16[2,4,48,384]{3,2,1,0:T(8,128)(2,1)S(1)}, u32[]{:S(2)}, u32[]{:S(2)}) collective-permute-start(bf16[2,4,48,384]{3,2,1,0:T(8,128)(2,1)} %get-tuple-element.69), channel_id=1, source_target_pairs={{0,1},{1,0},{2,3},{3,2},{4,5},{5,4},{6,7},{7,6},{8,9},{9,8},{10,11... | collective-permute-start | bytes 884744 | tf_op jit(solution)/shard_map/ppermute | solution.py:339
  60.0 1.4 %copy-start.1 = (f32[2,4,48,384]{3,2,1,0:T(8,128)S(1)}, f32[2,4,48,384]{3,2,1,0:T(8,128)}, u32[]{:S(2)}) copy-start(f32[2,4,48,384]{3,2,1,0:T(8,128)} %get-tuple-element.68) | copy-start | bytes 1769476
  61.6 9.4 %collective-permute-start.21 = (bf16[4,48,384]{2,1,0:T(8,128)(2,1)S(1)}, bf16[4,48,384]{2,1,0:T(8,128)(2,1)S(1)}, u32[]{:S(2)}, u32[]{:S(2)}) collective-permute-start(bf16[4,48,384]{2,1,0:T(8,128)(2,1)S(1)} %pad_maximum_fusion.5), channel_id=1, source_target_pairs={{0,6},{1,7},{2,4},{3,5},{4,2},{5,3},{6,0},{7,1},{8,14},{9,15},{10,... | collective-permute-start | bytes 442376 | tf_op jit(solution)/shard_map/ppermute | solution.py:339
  66.6 7.3 %collective-permute-start.20 = (bf16[4,48,384]{2,1,0:T(8,128)(2,1)S(1)}, bf16[4,48,384]{2,1,0:T(8,128)(2,1)S(1)}, u32[]{:S(2)}, u32[]{:S(2)}) collective-permute-start(bf16[4,48,384]{2,1,0:T(8,128)(2,1)S(1)} %pad_maximum_fusion.4), channel_id=1, source_target_pairs={{0,4},{1,5},{2,6},{3,7},{4,0},{5,1},{6,2},{7,3},{8,12},{9,13},{10,... | collective-permute-start | bytes 442376 | tf_op jit(solution)/shard_map/ppermute | solution.py:339
  66.7 7.3 %collective-permute-start.19 = (bf16[4,48,384]{2,1,0:T(8,128)(2,1)S(1)}, bf16[4,48,384]{2,1,0:T(8,128)(2,1)S(1)}, u32[]{:S(2)}, u32[]{:S(2)}) collective-permute-start(bf16[4,48,384]{2,1,0:T(8,128)(2,1)S(1)} %pad_maximum_fusion.3), channel_id=1, source_target_pairs={{0,2},{1,3},{2,0},{3,1},{4,6},{5,7},{6,4},{7,5},{8,10},{9,11},{10,... | collective-permute-start | bytes 442376 | tf_op jit(solution)/shard_map/ppermute | solution.py:339
  74.1 7.2 %collective-permute-start.24 = (bf16[48,384]{1,0:T(8,128)(2,1)S(1)}, bf16[48,384]{1,0:T(8,128)(2,1)S(1)}, u32[]{:S(2)}, u32[]{:S(2)}) collective-permute-start(bf16[48,384]{1,0:T(8,128)(2,1)S(1)} %get-tuple-element.79), channel_id=1, source_target_pairs={{0,24},{1,25},{2,26},{3,27},{4,28},{5,29},{6,30},{7,31},{8,16},{9,... | collective-permute-start | bytes 110600 | tf_op jit(solution)/shard_map/ppermute | solution.py:339
  76.7 5.1 %collective-permute-start.23 = (bf16[48,384]{1,0:T(8,128)(2,1)S(1)}, bf16[48,384]{1,0:T(8,128)(2,1)S(1)}, u32[]{:S(2)}, u32[]{:S(2)}) collective-permute-start(bf16[48,384]{1,0:T(8,128)(2,1)S(1)} %get-tuple-element.80), channel_id=1, source_target_pairs={{0,16},{1,17},{2,18},{3,19},{4,20},{5,21},{6,22},{7,23},{8,24},{9,... | collective-permute-start | bytes 110600 | tf_op jit(solution)/shard_map/ppermute | solution.py:339
  78.9 4.0 %collective-permute-start.22 = (bf16[48,384]{1,0:T(8,128)(2,1)S(1)}, bf16[48,384]{1,0:T(8,128)(2,1)S(1)}, u32[]{:S(2)}, u32[]{:S(2)}) collective-permute-start(bf16[48,384]{1,0:T(8,128)(2,1)S(1)} %get-tuple-element.78), channel_id=1, source_target_pairs={{0,8},{1,9},{2,10},{3,11},{4,12},{5,13},{6,14},{7,15},{8,0},{9,1},... | collective-permute-start | bytes 110600 | tf_op jit(solution)/shard_map/ppermute | solution.py:339
where the time goes:
time: 83.9 us; the launch traced here: 83.5 us
  starting transfers between devices  36.6 us (44%)
  waiting for transfers between devices  22.1 us (26%)
  Pallas kernels  19.3 us (23%)
  local copies, waits for them, and re-layouts  2.32 us (3%)
  other arithmetic  2.24 us (3%)
  between operations  0.94 us (1%)
    ppermute x15, starting transfers between devices, swap(): return lax.ppermute(value, AXES, [(i, i ^ mask) for i in range(count)])  20.9 us
    pallas_call x5, Pallas kernels, call(): pl.pallas_call(kernel, out_shape=[jax.ShapeDtypeStruct(s, t) for s, t in...  19.3 us
    ppermute x15, waiting for transfers between devices, swap(): return lax.ppermute(value, AXES, [(i, i ^ mask) for i in range(count)])  16.8 us
    ppermute x10, starting transfers between devices, around(): parts.append(lax.ppermute(value, AXES, pairs))  15.7 us
    ppermute x10, waiting for transfers between devices, around(): parts.append(lax.ppermute(value, AXES, pairs))  5.33 us
  transfers between devices with their start and end apart: 25, of which 13 were waited for; matrix products, arithmetic and copies ran while one was open for 1% of the time, Pallas kernels for 10%

commit v1 on v0

--- a/solution.py
+++ b/solution.py
@@ -20,6 +20,7 @@
 
 F32 = jnp.float32
 BF16 = jnp.bfloat16
+VMEM_LIMIT = 12 << 20
 
 
 def dot(a, b):
@@ -89,12 +90,8 @@
     return jnp.where(lane < width, stacked[:half], stacked[half:])
 
 
-def strip_tiles(groups, refs):
-    tiles = []
-    for s in range(3):
-        own, *sides = refs[s * (groups - 1) : (s + 1) * (groups - 1)]
-        tiles += [own.at[0], own.at[1]] + list(sides)
-    return tiles
+def strip_tiles(strips):
+    return [strip.at[g] for strip in strips for g in range(strip.shape[0])]
 
 
 def near_rows(groups, odd, n_tiles):
@@ -121,8 +118,7 @@
 
 def forward_kernel(groups, place, *refs):
     scalars, wblk, tokens, teacher = refs[:4]
-    n_sides = 3 * (groups - 1)
-    tiles = strip_tiles(groups, refs[4 : 4 + n_sides])
+    tiles = strip_tiles(refs[4:7])
     (
         wq_out,
         wk_out,
@@ -130,8 +126,6 @@
         x_out,
         k_out,
         v_out,
-        kn_out,
-        kf_out,
         mixed_out,
         gout_out,
         near_out,
@@ -139,7 +133,7 @@
         pack_out,
         *sends_out,
         wo_scr,
-    ) = refs[4 + n_sides :]
+    ) = refs[7:]
     odd, base = scalars[0], scalars[1]
     n_blocks, per_block, model = wblk.shape
     width = model // HEADS
@@ -156,10 +150,7 @@
         flag_rows.append(tile[PER:BLK, :].astype(F32)[0:1, 0:PER])
     ones = pair_ones(width)
     x = x_out[...]
-    k_raw = dot(x, wk_out[...])
-    k_normal, k_factor = head_normalise(k_raw, ones, width)
-    kn_out[...] = k_normal[0:own]
-    kf_out[...] = k_factor[0:own]
+    k_normal, _ = head_normalise(dot(x, wk_out[...]), ones, width)
     keys = k_normal.astype(BF16)
     k_out[...] = keys
     values = dot(x, wv_out[...]).astype(BF16)
@@ -201,6 +192,7 @@
     for h in range(HEADS):
         table = jnp.where(lane == h, inverses[h], table)
         table = jnp.where(lane == HEADS + h, delta[:, h * width : h * width + 1], table)
+    table = jnp.where(lane == 2 * HEADS, query_mask, table)
     stats_out[...] = table
     stats = table.T[0:16, :]
     for t in range(2):
@@ -265,10 +257,10 @@
     store_terms(fast, core, [grad_wq, grad_wo], outs)
 
 
-def key_kernel(groups, fast, scalars, x, k, v, q, kn, kf, near_in, *refs):
-    n_sides = 3 * (groups - 1)
-    tiles = strip_tiles(groups, refs[:n_sides])
-    gk_out, gv_out, *outs, g_scr = refs[n_sides:]
+def key_kernel(groups, fast, scalars, x, k, v, q, wk, gl, mid, near, far, gk_out, gv_out, gl_out, *rest):
+    *outs, g_scr = rest
+    tiles = strip_tiles((mid, near, far))
+    gl_out[...] = gl[...]
     odd, core = scalars[0], scalars[2]
     model = q.shape[1]
     width = model // HEADS
@@ -281,7 +273,8 @@
         stat_parts.append(tile[PER:BLK, :].astype(F32)[:, 0:PER])
     stats = jnp.concatenate(stat_parts, axis=1)
     left, right = near_rows(groups, odd, n_tiles)
-    near = [left * near_in[0:1, 0:1], right * near_in[0:1, PER : PER + 1]]
+    flag = stats[2 * HEADS : 2 * HEADS + 1]
+    near = [left * flag[:, 0:1], right * flag[:, PER : PER + 1]]
     scale = 1.0 / math.sqrt(width)
     key_parts, value_parts = [], []
     for p in range(HEADS // 2):
@@ -300,11 +293,12 @@
         key_parts.append(join_heads(dot(grad_scores, queries), width))
         value_parts.append(join_heads(dot(low, grads), width))
     grad_kn = jnp.concatenate(key_parts, axis=1)
-    grad_key = head_back(kn[...], kf[...], grad_kn, ones, width).astype(BF16)
+    x_own = x[0:own, :]
+    k_normal, k_factor = head_normalise(dot(x_own, wk[...]), ones, width)
+    grad_key = head_back(k_normal, k_factor, grad_kn, ones, width).astype(BF16)
     grad_value = jnp.concatenate(value_parts, axis=1).astype(BF16)
     gk_out[...] = grad_key
     gv_out[...] = grad_value
-    x_own = x[0:own, :]
     store_terms(fast, core, [dot_tn(x_own, grad_key), dot_tn(x_own, grad_value)], outs)
 
 
@@ -325,13 +319,21 @@
 VMEM = pl.BlockSpec(memory_space=pltpu.VMEM)
 
 
-def call(kernel, in_specs, shapes, args, scratch=()):
+def call(kernel, in_specs, shapes, args, scratch=(), kept=0, held=()):
+    args = [
+        pltpu.with_memory_space_constraint(a, pltpu.VMEM) if n in held else a
+        for n, a in enumerate(args)
+    ]
     return pl.pallas_call(
         kernel,
-        out_shape=[jax.ShapeDtypeStruct(s, t) for s, t in shapes],
+        out_shape=[
+            pltpu.VMEM(s, t) if n < kept else jax.ShapeDtypeStruct(s, t)
+            for n, (s, t) in enumerate(shapes)
+        ],
         in_specs=in_specs,
         out_specs=[VMEM] * len(shapes),
         scratch_shapes=list(scratch),
+        compiler_params=pltpu.CompilerParams(vmem_limit_bytes=VMEM_LIMIT),
     )(*args)
 
 
@@ -340,29 +342,21 @@
 
 
 def side_pairs(length, side):
-    if side is None:
-        return [(i, i) for i in range(length)]
     pairs = []
     for i in range(side, length - 1, 2):
         pairs += [(i, i + 1), (i + 1, i)]
     return pairs
 
 
-def around(own, sides):
-    rows, cols = lax.axis_size("rows"), lax.axis_size("cols")
-    parts = []
-    for strip in (None, 0, 1):
-        for side, value in [(None, own)] + list(enumerate(sides)):
-            if strip is None and side is None:
-                parts.append(value)
-                continue
-            pairs = [
-                (r * cols + c, to_r * cols + to_c)
-                for r, to_r in side_pairs(rows, strip)
-                for c, to_c in side_pairs(cols, side)
-            ]
-            parts.append(lax.ppermute(value, AXES, pairs))
-    return parts
+def across(own, sides):
+    cols = lax.axis_size("cols")
+    parts = [lax.ppermute(v, "cols", side_pairs(cols, n))[None] for n, v in enumerate(sides)]
+    return jnp.concatenate([own] + parts, axis=0)
+
+
+def beside(strip):
+    rows = lax.axis_size("rows")
+    return [lax.ppermute(strip, "rows", side_pairs(rows, n)) for n in range(2)]
 
 
 def layer(tokens, teacher, tissue, weights):
@@ -370,7 +364,6 @@
     rows, cols = lax.axis_size("rows"), lax.axis_size("cols")
     count = rows * cols
     groups = 3 if cols == 2 else 4
-    n_sides = 3 * (groups - 1)
     per_block = 4 * model // count
     fast = count & (count - 1) == 0 and count >= 16 and per_block % 16 == 0
     per_matrix = count // 4
@@ -399,24 +392,24 @@
         wblk = weights.reshape(1, per_block, model)
         parts = [swap(wblk, count, per_matrix * step) for step in range(1, 4)]
         wblk = jnp.concatenate([wblk] + parts, axis=0)
-        wblk, low, sends = lax.optimization_barrier((wblk, low, sends))
+        mid = across(low, sends)
+        wblk, mid = lax.optimization_barrier((wblk, mid))
         parts = [swap(wblk, count, 2 * step) for step in range(1, spots)]
-        sides = around(low, sends)
+        sides = beside(mid)
         wblk = jnp.concatenate([wblk] + parts, axis=0)
         wblk, sides = lax.optimization_barrier((wblk, sides))
         wblk = jnp.concatenate([wblk, swap(wblk, count, 1)], axis=0)
     else:
-        sides = around(low, sends)
+        mid = across(low, sends)
+        sides = beside(mid)
         wblk = lax.all_gather(weights, AXES, axis=0, tiled=True).reshape(4, model, model)
 
-    wq, wk, wv, x, k, v, kn, kf, mixed, gout, near, stats, pack, *sends = call(
+    wq, wk, wv, x, k, v, mixed, gout, near, stats, pack, *sends = call(
         functools.partial(forward_kernel, groups, place),
-        [SMEM] + [VMEM] * (3 + n_sides),
+        [SMEM] + [VMEM] * 6,
         [((model, model), BF16)] * 3
         + [((n_keys, model), BF16)] * 3
         + [
-            ((own, model), F32),
-            ((own, model), F32),
             ((own, model), BF16),
             ((own, model), F32),
             ((2, n_keys), F32),
@@ -424,10 +417,12 @@
             ((2, BLK, model), BF16),
         ]
         + sends_shape,
-        (scalars, wblk, tokens, teacher, *sides),
+        (scalars, wblk, tokens, teacher, mid, *sides),
         scratch=[pltpu.VMEM((model, model), BF16)],
-    )
-    packs = around(pack, sends)
+        kept=10,
+    )
+    packs = across(pack, sends)
+    packs = [packs] + beside(packs)
 
     if fast:
         term_shapes = [
@@ -441,16 +436,24 @@
         [SMEM] + [VMEM] * 9,
         [((n_keys, model), BF16), ((own, model), F32)] + term_shapes,
         (scalars, wq, x, k, v, mixed, gout, near, stats, pack),
-    )
-    gk, gv, *terms_kv = call(
+        kept=4 if fast else 2,
+        held=range(1, 9),
+    )
+    gk, gv, gl, *terms_kv = call(
         functools.partial(key_kernel, groups, fast),
-        [SMEM] + [VMEM] * (7 + n_sides),
-        [((own, model), BF16), ((own, model), BF16)] + term_shapes,
-        (scalars, x, k, v, q, kn, kf, near, *packs),
+        [SMEM] + [VMEM] * 9,
+        [((own, model), BF16), ((own, model), BF16), ((own, model), F32)] + term_shapes,
+        (scalars, x, k, v, q, wk, gl, *packs),
         scratch=[pltpu.VMEM((n_keys, model), BF16)],
+        kept=5 if fast else 3,
+        held=range(1, 7),
     )
     (grads,) = call(
-        final_kernel, [VMEM] * 7, [(tokens.shape, BF16)], (tokens, wk, wv, gk, gv, gl, gout)
+        final_kernel,
+        [VMEM] * 7,
+        [(tokens.shape, BF16)],
+        (tokens, wk, wv, gk, gv, gl, gout),
+        held=range(1, 7),
     )
 
     n_tokens = tokens.shape[0] * rows * tokens.shape[1] * cols

time: 83.9 us -> 76.5 us (0.912)
  starting transfers between devices: 36.6 us -> 27.8 us
  waiting for transfers between devices: 22.1 us -> 28.9 us
  Pallas kernels: 19.3 us -> 12.7 us
  local copies, waits for them, and re-layouts: 2.32 us -> 4.38 us
    ppermute x10 -> x6, starting transfers between devices: 15.7 us -> 6.25 us  [the longest x4 5.98 us: beside(): return [lax.ppermute(strip, 'rows', side_pairs(rows, n)) for n in range(2)]]
    pallas_call x5, Pallas kernels: 19.3 us -> 12.7 us  [call(): pl.pallas_call(kernel, out_shape=[pltpu.VMEM(s, t) if n < kept else jax.S...]
    ppermute x15, waiting for transfers between devices: 16.8 us -> 22 us  [swap(): return lax.ppermute(value, AXES, [(i, i ^ mask) for i in range(count)])]
    unnamed x28 -> x20, local copies, waits for them, and re-layouts: 0.72 us -> 2.78 us
    ppermute x10 -> x6, waiting for transfers between devices: 5.33 us -> 6.88 us  [the longest x4 6.87 us: beside(): return [lax.ppermute(strip, 'rows', side_pairs(rows, n)) for n in range(2)]]
    concatenate x1, other arithmetic: 1.18 us -> 0.13 us  [layer(): wblk = jnp.concatenate([wblk, swap(wblk, count, 1)], axis=0)]
    add x2, other arithmetic: 0.12 us -> 1.08 us  [with_core(): return keep + swap(send, count, 1).astype(F32)]
  transfers between devices with their start and end apart: 25 -> 21, of which waited for: 13 -> 12; matrix products, arithmetic and copies ran while one was open for 1% -> 2% of each run, Pallas kernels for 10% -> 11%
where the time goes in v1:
time: 76.5 us; the launch traced here: 76.2 us
  waiting for transfers between devices  28.9 us (38%)
  starting transfers between devices  27.8 us (36%)
  Pallas kernels  12.7 us (17%)
  local copies, waits for them, and re-layouts  4.38 us (6%)
  other arithmetic  1.64 us (2%)
  between operations  0.88 us (1%)
    ppermute x15, waiting for transfers between devices, swap(): return lax.ppermute(value, AXES, [(i, i ^ mask) for i in range(count)])  22 us
    ppermute x15, starting transfers between devices, swap(): return lax.ppermute(value, AXES, [(i, i ^ mask) for i in range(count)])  21.5 us
    pallas_call x5, Pallas kernels, call(): pl.pallas_call(kernel, out_shape=[pltpu.VMEM(s, t) if n < kept else jax.S...  12.7 us
    ppermute x4, waiting for transfers between devices, beside(): return [lax.ppermute(strip, 'rows', side_pairs(rows, n)) for n in range(2)]  6.87 us
    ppermute x4, starting transfers between devices, beside(): return [lax.ppermute(strip, 'rows', side_pairs(rows, n)) for n in range(2)]  5.98 us
    unnamed x20, local copies, waits for them, and re-layouts  2.78 us
  transfers between devices with their start and end apart: 21, of which 12 were waited for; matrix products, arithmetic and copies ran while one was open for 2% of the time, Pallas kernels for 11%

profile of v1, /device:TPU:0, one launch (start us, length us, event | category | flops | bytes accessed | tf_op | source)
XLA Modules:
  0.0 76.2 jit_solution(16823989139890310270)
XLA Ops:
  0.6 0.8 %reshape.27 = bf16[1,48,384]{2,1,0:T(8,128)(2,1)S(1)} reshape(bf16[18432]{0:T(1024)(128)(2,1)} %param.7) | data formatting | bytes 73728 | tf_op jit(solution)/shard_map/reshape | solution.py:392
  1.4 5.1 %collective-permute-start.2 = (bf16[1,48,384]{2,1,0:T(8,128)(2,1)S(1)}, bf16[1,48,384]{2,1,0:T(8,128)(2,1)S(1)}, u32[]{:S(2)}, u32[]{:S(2)}) collective-permute-start(bf16[1,48,384]{2,1,0:T(8,128)(2,1)S(1)} %reshape.27), channel_id=1, source_target_pairs={{0,24},{1,25},{2,26},{3,27},{4,28},{5,29},{6,30},{7,31},{8,16},{9,... | collective-permute-start | bytes 110600 | tf_op jit(solution)/shard_map/ppermute | solution.py:341
  6.6 0.0 collective-permute-start.1
  6.6 0.6 collective-permute-start
  7.2 0.1 pad_add_fusion.refs_0_.scalars
  7.3 0.9 %copy-done = bf16[8,16,384]{2,1,0:T(8,128)(2,1)S(1)} copy-done((bf16[8,16,384]{2,1,0:T(8,128)(2,1)S(1)}, bf16[8,16,384]{2,1,0:T(8,128)(2,1)}, u32[]{:S(2)}) %copy-start) | copy-done | bytes 98328
  8.2 0.7 copy-done.9
  8.8 0.7 shard_map.59
  9.6 0.1 collective-permute-start.3
  9.7 0.0 collective-permute-done.2
  9.7 1.8 %collective-permute-done.1 = bf16[1,48,384]{2,1,0:T(8,128)(2,1)S(1)} collective-permute-done((bf16[1,48,384]{2,1,0:T(8,128)(2,1)S(1)}, bf16[1,48,384]{2,1,0:T(8,128)(2,1)S(1)}, u32[]{:S(2)}, u32[]{:S(2)}) %collective-permute-start.1) | collective-permute-done | bytes 36896 | tf_op jit(solution)/shard_map/ppermute | solution.py:341
  11.4 0.0 collective-permute-done
  11.5 0.0 collective-permute-done.3
  11.5 2.5 %collective-permute-start.6 = (bf16[4,48,384]{2,1,0:T(8,128)(2,1)S(1)}, bf16[4,48,384]{2,1,0:T(8,128)(2,1)S(1)}, u32[]{:S(2)}, u32[]{:S(2)}) collective-permute-start(bf16[4,48,384]{2,1,0:T(8,128)(2,1)S(1)} %pad_maximum_fusion.4), channel_id=1, source_target_pairs={{0,6},{1,7},{2,4},{3,5},{4,2},{5,3},{6,0},{7,1},{8,14},{9,15},{10,... | collective-permute-start | bytes 442376 | tf_op jit(solution)/shard_map/ppermute | solution.py:341
  14.0 0.5 collective-permute-start.5
  14.5 0.5 collective-permute-start.4
  15.1 1.5 %collective-permute-start.7 = (bf16[3,80,384]{2,1,0:T(8,128)(2,1)S(1)}, bf16[3,80,384]{2,1,0:T(8,128)(2,1)S(1)}, u32[]{:S(2)}, u32[]{:S(2)}) collective-permute-start(bf16[3,80,384]{2,1,0:T(8,128)(2,1)S(1)} %pad_maximum_fusion.2.refs_4_), channel_id=1, source_target_pairs={{0,2},{2,0},{4,6},{6,4},{8,10},{10,8},{12,14},{14,12},{16,18},{18,... | collective-permute-start | bytes 552968 | tf_op jit(solution)/shard_map/ppermute | solution.py:359
  16.6 0.7 collective-permute-start.8
  17.2 1.1 %collective-permute-done.6 = bf16[4,48,384]{2,1,0:T(8,128)(2,1)S(1)} collective-permute-done((bf16[4,48,384]{2,1,0:T(8,128)(2,1)S(1)}, bf16[4,48,384]{2,1,0:T(8,128)(2,1)S(1)}, u32[]{:S(2)}, u32[]{:S(2)}) %collective-permute-start.6) | collective-permute-done | bytes 147488 | tf_op jit(solution)/shard_map/ppermute | solution.py:341
  18.4 2.6 %collective-permute-done.5 = bf16[4,48,384]{2,1,0:T(8,128)(2,1)S(1)} collective-permute-done((bf16[4,48,384]{2,1,0:T(8,128)(2,1)S(1)}, bf16[4,48,384]{2,1,0:T(8,128)(2,1)S(1)}, u32[]{:S(2)}, u32[]{:S(2)}) %collective-permute-start.5) | collective-permute-done | bytes 147488 | tf_op jit(solution)/shard_map/ppermute | solution.py:341
  21.0 4.4 %collective-permute-done.4 = bf16[4,48,384]{2,1,0:T(8,128)(2,1)S(1)} collective-permute-done((bf16[4,48,384]{2,1,0:T(8,128)(2,1)S(1)}, bf16[4,48,384]{2,1,0:T(8,128)(2,1)S(1)}, u32[]{:S(2)}, u32[]{:S(2)}) %collective-permute-start.4) | collective-permute-done | bytes 147488 | tf_op jit(solution)/shard_map/ppermute | solution.py:341
  25.4 0.1 pad_maximum_fusion.1
  25.5 0.0 copy-start.1
  25.5 0.0 copy-start.6
  25.5 2.6 %collective-permute-done.7.refs_5_ = bf16[3,80,384]{2,1,0:T(8,128)(2,1)S(1)} collective-permute-done((bf16[3,80,384]{2,1,0:T(8,128)(2,1)S(1)}, bf16[3,80,384]{2,1,0:T(8,128)(2,1)S(1)}, u32[]{:S(2)}, u32[]{:S(2)}) %collective-permute-start.7) | collective-permute-done | bytes 184352 | tf_op jit(solution)/shard_map/ppermute | solution.py:359
  28.1 0.0 collective-permute-done.8.refs_6_
  28.1 0.0 collective-permute-start.9
  28.1 2.0 %collective-permute-done.9 = bf16[16,48,384]{2,1,0:T(8,128)(2,1)S(1)} collective-permute-done((bf16[16,48,384]{2,1,0:T(8,128)(2,1)S(1)}, bf16[16,48,384]{2,1,0:T(8,128)(2,1)S(1)}, u32[]{:S(2)}, u32[]{:S(2)}) %collective-permute-start.9) | collective-permute-done | bytes 589856 | tf_op jit(solution)/shard_map/ppermute | solution.py:341
  30.1 0.1 pad_maximum_fusion.refs_1_
  30.3 0.0 copy-done.1
  30.3 4.3 %shard_map.60 = (bf16[384,384]{1,0:T(8,128)(2,1)S(1)}, bf16[384,384]{1,0:T(8,128)(2,1)S(1)}, bf16[384,384]{1,0:T(8,128)(2,1)S(1)}, bf16[576,384]{1,0:T(8,128)(2,...) custom-call(s32[4]{0:T(128)S(1)} %pad_add_fusion.refs_0_.scalars, ...), custom_call_target="tpu_custom_call" | custom-call | tf_op jit(solution)/shard_map/pallas_call | solution.py:327
  34.6 0.2 collective-permute-start.10
  34.8 3.5 %shard_map.61 = (bf16[576,384]{1,0:T(8,128)(2,1)S(1)}, f32[128,384]{1,0:T(8,128)S(1)}, f32[2,4,48,384]{3,2,1,0:T(8,128)S(1)}, bf16[2,4,48,384]{3,2,1,0:T(8,128)(2,1)}) custom-call(s32[4]{0:T(128)S(1)} %pad_add_fusion.refs_0_.scalars, bf16[384,384]{1,0:T(8,128)(2,1)S(1)} %get-tuple-element.42.wq, bf16[576,384]{1,0:T(8,128)(2,1)S(1)} %get-tuple-element.39.x, ...), custom_call_target="tpu_custom_call" | custom-call | tf_op jit(solution)/shard_map/pallas_call | solution.py:327
  38.3 0.4 collective-permute-start.13
  38.7 0.0 collective-permute-done.10
  38.7 0.3 copy-done.2
  39.0 2.5 %collective-permute-start.11 = (bf16[3,80,384]{2,1,0:T(8,128)(2,1)S(1)}, bf16[3,80,384]{2,1,0:T(8,128)(2,1)}, u32[]{:S(2)}, u32[]{:S(2)}) collective-permute-start(bf16[3,80,384]{2,1,0:T(8,128)(2,1)S(1)} %pad_maximum_fusion.3.mid), channel_id=1, source_target_pairs={{0,2},{2,0},{4,6},{6,4},{8,10},{10,8},{12,14},{14,12},{16,18},{18,... | collective-permute-start | bytes 552968 | tf_op jit(solution)/shard_map/ppermute | solution.py:359
  41.4 1.3 %collective-permute-start.12 = (bf16[3,80,384]{2,1,0:T(8,128)(2,1)S(1)}, bf16[3,80,384]{2,1,0:T(8,128)(2,1)}, u32[]{:S(2)}, u32[]{:S(2)}) collective-permute-start(bf16[3,80,384]{2,1,0:T(8,128)(2,1)S(1)} %pad_maximum_fusion.3.mid), channel_id=1, source_target_pairs={{2,4},{4,2},{6,8},{8,6},{10,12},{12,10},{14,16},{16,14},{18,20},{2... | collective-permute-start | bytes 552968 | tf_op jit(solution)/shard_map/ppermute | solution.py:359
  42.8 4.2 %collective-permute-done.11.near = bf16[3,80,384]{2,1,0:T(8,128)(2,1)} collective-permute-done((bf16[3,80,384]{2,1,0:T(8,128)(2,1)S(1)}, bf16[3,80,384]{2,1,0:T(8,128)(2,1)}, u32[]{:S(2)}, u32[]{:S(2)}) %collective-permute-start.11) | collective-permute-done | bytes 184352 | tf_op jit(solution)/shard_map/ppermute | solution.py:359
  47.0 0.0 collective-permute-done.12.far
  47.0 0.9 %copy-done.3 = f32[128,384]{1,0:T(8,128)S(1)} copy-done((f32[128,384]{1,0:T(8,128)S(1)}, f32[128,384]{1,0:T(8,128)}, u32[]{:S(2)}) %copy-start.3) | copy-done | bytes 196632
  48.0 3.1 %shard_map.62 = (bf16[128,384]{1,0:T(8,128)(2,1)S(1)}, bf16[128,384]{1,0:T(8,128)(2,1)S(1)}, f32[128,384]{1,0:T(8,128)S(1)}, f32[2,4,48,384]{3,2,1,0:T(8,128)S(1)}, bf16[2,4,48,384]{3,2,1,0:T(8,128)(2,1)S(1)}) custom-call(s32[4]{0:T(128)S(1)} %pad_add_fusion.refs_0_.scalars, bf16[576,384]{1,0:T(8,128)(2,1)S(1)} %get-tuple-element.39.x, ...), custom_call_target="tpu_custom_call" | custom-call | tf_op jit(solution)/shard_map/pallas_call | solution.py:327
  51.1 0.0 copy-start.7
  51.1 0.1 collective-permute-start.14
  51.1 0.0 collective-permute-done.13
  51.2 1.0 %convert_add_fusion.1 = f32[2,4,48,384]{3,2,1,0:T(8,128)S(1)} fusion(f32[2,4,48,384]{3,2,1,0:T(8,128)S(1)} %get-tuple-element.54, bf16[2,4,48,384]{3,2,1,0:T(8,128)(2,1)} %collective-permute-done.13), kind=kLoop, calls=%fused_computation.3 | loop fusion | flops 294912 | bytes 1474560 | tf_op jit(solution)/shard_map/add | solution.py:472
  52.3 0.4 collective-permute-done.14
  52.7 0.1 convert_add_fusion
  52.8 6.3 %collective-permute-start.17 = (bf16[4,48,384]{2,1,0:T(8,128)(2,1)S(1)}, bf16[4,48,384]{2,1,0:T(8,128)(2,1)S(1)}, u32[]{:S(2)}, u32[]{:S(2)}) collective-permute-start(bf16[4,48,384]{2,1,0:T(8,128)(2,1)S(1)} %pad_maximum_fusion.7), channel_id=1, source_target_pairs={{0,6},{1,7},{2,4},{3,5},{4,2},{5,3},{6,0},{7,1},{8,14},{9,15},{10,... | collective-permute-start | bytes 442376 | tf_op jit(solution)/shard_map/ppermute | solution.py:341
  59.2 0.3 collective-permute-start.16
  59.5 0.4 collective-permute-start.15
  60.0 3.6 %collective-permute-done.17 = bf16[4,48,384]{2,1,0:T(8,128)(2,1)S(1)} collective-permute-done((bf16[4,48,384]{2,1,0:T(8,128)(2,1)S(1)}, bf16[4,48,384]{2,1,0:T(8,128)(2,1)S(1)}, u32[]{:S(2)}, u32[]{:S(2)}) %collective-permute-start.17) | collective-permute-done | bytes 147488 | tf_op jit(solution)/shard_map/ppermute | solution.py:341
  63.7 2.8 %collective-permute-done.16 = bf16[4,48,384]{2,1,0:T(8,128)(2,1)S(1)} collective-permute-done((bf16[4,48,384]{2,1,0:T(8,128)(2,1)S(1)}, bf16[4,48,384]{2,1,0:T(8,128)(2,1)S(1)}, u32[]{:S(2)}, u32[]{:S(2)}) %collective-permute-start.16) | collective-permute-done | bytes 147488 | tf_op jit(solution)/shard_map/ppermute | solution.py:341
  66.5 0.0 collective-permute-done.15
  66.5 0.1 fusion.1
  66.7 4.0 %collective-permute-start.20 = (bf16[48,384]{1,0:T(8,128)(2,1)S(1)}, bf16[48,384]{1,0:T(8,128)(2,1)S(1)}, u32[]{:S(2)}, u32[]{:S(2)}) collective-permute-start(bf16[48,384]{1,0:T(8,128)(2,1)S(1)} %get-tuple-element.67), channel_id=1, source_target_pairs={{0,24},{1,25},{2,26},{3,27},{4,28},{5,29},{6,30},{7,31},{8,16},{9,... | collective-permute-start | bytes 110600 | tf_op jit(solution)/shard_map/ppermute | solution.py:341
  70.7 0.0 collective-permute-start.19
  70.7 0.6 collective-permute-start.18
  71.3 0.0 copy-done.5
  71.3 1.1 %shard_map.63 = bf16[8,16,384]{2,1,0:T(8,128)(2,1)} custom-call(bf16[8,16,384]{2,1,0:T(8,128)(2,1)S(1)} %copy-done.1, bf16[384,384]{1,0:T(8,128)(2,1)S(1)} %get-tuple-element.37.wk, bf16[384,384]{1,0:T(8,128)(2,1)S(1)} %get-tuple-element.38.wv, bf16[128,384]{1,0:T(8,128)(2,1)S(1)} %get-tuple-element.51.gk, bf16[128,384]{1,0:T(8,128)(2,1)S(1)} %copy-done.8, ...), custom_call_target="tpu_custom_call" | custom-call | tf_op jit(solution)/shard_map/pallas_call | solution.py:327
  72.4 0.3 collective-permute-done.20
  72.7 2.8 %collective-permute-done.19 = bf16[48,384]{1,0:T(8,128)(2,1)S(1)} collective-permute-done((bf16[48,384]{1,0:T(8,128)(2,1)S(1)}, bf16[48,384]{1,0:T(8,128)(2,1)S(1)}, u32[]{:S(2)}, u32[]{:S(2)}) %collective-permute-start.19) | collective-permute-done | bytes 36896 | tf_op jit(solution)/shard_map/ppermute | solution.py:341
  75.5 0.0 collective-permute-done.18
  75.6 0.6 reshape.28
  (25 shorter events, 0.4 us)
Async XLA Ops:
  1.4 8.2 %collective-permute-start.2 = (bf16[1,48,384]{2,1,0:T(8,128)(2,1)S(1)}, bf16[1,48,384]{2,1,0:T(8,128)(2,1)S(1)}, u32[]{:S(2)}, u32[]{:S(2)}) collective-permute-start(bf16[1,48,384]{2,1,0:T(8,128)(2,1)S(1)} %reshape.27), channel_id=1, source_target_pairs={{0,24},{1,25},{2,26},{3,27},{4,28},{5,29},{6,30},{7,31},{8,16},{9,... | collective-permute-start | bytes 110600 | tf_op jit(solution)/shard_map/ppermute | solution.py:341
  6.6 4.9 %collective-permute-start.1 = (bf16[1,48,384]{2,1,0:T(8,128)(2,1)S(1)}, bf16[1,48,384]{2,1,0:T(8,128)(2,1)S(1)}, u32[]{:S(2)}, u32[]{:S(2)}) collective-permute-start(bf16[1,48,384]{2,1,0:T(8,128)(2,1)S(1)} %reshape.27), channel_id=1, source_target_pairs={{0,16},{1,17},{2,18},{3,19},{4,20},{5,21},{6,22},{7,23},{8,24},{9,... | collective-permute-start | bytes 110600 | tf_op jit(solution)/shard_map/ppermute | solution.py:341
  6.6 4.9 %collective-permute-start = (bf16[1,48,384]{2,1,0:T(8,128)(2,1)S(1)}, bf16[1,48,384]{2,1,0:T(8,128)(2,1)S(1)}, u32[]{:S(2)}, u32[]{:S(2)}) collective-permute-start(bf16[1,48,384]{2,1,0:T(8,128)(2,1)S(1)} %reshape.27), channel_id=1, source_target_pairs={{0,8},{1,9},{2,10},{3,11},{4,12},{5,13},{6,14},{7,15},{8,0},{9,1},... | collective-permute-start | bytes 110600 | tf_op jit(solution)/shard_map/ppermute | solution.py:341
  7.3 0.9 %copy-start = (bf16[8,16,384]{2,1,0:T(8,128)(2,1)S(1)}, bf16[8,16,384]{2,1,0:T(8,128)(2,1)}, u32[]{:S(2)}) copy-start(bf16[8,16,384]{2,1,0:T(8,128)(2,1)} %tokens.1) | copy-start | bytes 294916
  8.2 0.7 copy-start.9
  9.6 1.9 %collective-permute-start.3 = (bf16[80,384]{1,0:T(8,128)(2,1)S(1)}, bf16[80,384]{1,0:T(8,128)(2,1)S(1)}, u32[]{:S(2)}, u32[]{:S(2)}) collective-permute-start(bf16[80,384]{1,0:T(8,128)(2,1)S(1)} %get-tuple-element.31), channel_id=1, source_target_pairs={{0,1},{1,0},{2,3},{3,2},{4,5},{5,4},{6,7},{7,6},{8,9},{9,8},{10,11... | collective-permute-start | bytes 184328 | tf_op jit(solution)/shard_map/ppermute | solution.py:353
  11.5 6.9 %collective-permute-start.6 = (bf16[4,48,384]{2,1,0:T(8,128)(2,1)S(1)}, bf16[4,48,384]{2,1,0:T(8,128)(2,1)S(1)}, u32[]{:S(2)}, u32[]{:S(2)}) collective-permute-start(bf16[4,48,384]{2,1,0:T(8,128)(2,1)S(1)} %pad_maximum_fusion.4), channel_id=1, source_target_pairs={{0,6},{1,7},{2,4},{3,5},{4,2},{5,3},{6,0},{7,1},{8,14},{9,15},{10,... | collective-permute-start | bytes 442376 | tf_op jit(solution)/shard_map/ppermute | solution.py:341
  14.0 6.9 %collective-permute-start.5 = (bf16[4,48,384]{2,1,0:T(8,128)(2,1)S(1)}, bf16[4,48,384]{2,1,0:T(8,128)(2,1)S(1)}, u32[]{:S(2)}, u32[]{:S(2)}) collective-permute-start(bf16[4,48,384]{2,1,0:T(8,128)(2,1)S(1)} %pad_maximum_fusion.4), channel_id=1, source_target_pairs={{0,4},{1,5},{2,6},{3,7},{4,0},{5,1},{6,2},{7,3},{8,12},{9,13},{10,... | collective-permute-start | bytes 442376 | tf_op jit(solution)/shard_map/ppermute | solution.py:341
  14.5 10.8 %collective-permute-start.4 = (bf16[4,48,384]{2,1,0:T(8,128)(2,1)S(1)}, bf16[4,48,384]{2,1,0:T(8,128)(2,1)S(1)}, u32[]{:S(2)}, u32[]{:S(2)}) collective-permute-start(bf16[4,48,384]{2,1,0:T(8,128)(2,1)S(1)} %pad_maximum_fusion.4), channel_id=1, source_target_pairs={{0,2},{1,3},{2,0},{3,1},{4,6},{5,7},{6,4},{7,5},{8,10},{9,11},{10,... | collective-permute-start | bytes 442376 | tf_op jit(solution)/shard_map/ppermute | solution.py:341
  15.1 13.1 %collective-permute-start.7 = (bf16[3,80,384]{2,1,0:T(8,128)(2,1)S(1)}, bf16[3,80,384]{2,1,0:T(8,128)(2,1)S(1)}, u32[]{:S(2)}, u32[]{:S(2)}) collective-permute-start(bf16[3,80,384]{2,1,0:T(8,128)(2,1)S(1)} %pad_maximum_fusion.2.refs_4_), channel_id=1, source_target_pairs={{0,2},{2,0},{4,6},{6,4},{8,10},{10,8},{12,14},{14,12},{16,18},{18,... | collective-permute-start | bytes 552968 | tf_op jit(solution)/shard_map/ppermute | solution.py:359
  16.6 11.6 %collective-permute-start.8 = (bf16[3,80,384]{2,1,0:T(8,128)(2,1)S(1)}, bf16[3,80,384]{2,1,0:T(8,128)(2,1)S(1)}, u32[]{:S(2)}, u32[]{:S(2)}) collective-permute-start(bf16[3,80,384]{2,1,0:T(8,128)(2,1)S(1)} %pad_maximum_fusion.2.refs_4_), channel_id=1, source_target_pairs={{2,4},{4,2},{6,8},{8,6},{10,12},{12,10},{14,16},{16,14},{18,20},{2... | collective-permute-start | bytes 552968 | tf_op jit(solution)/shard_map/ppermute | solution.py:359
  25.5 4.8 %copy-start.1 = (bf16[8,16,384]{2,1,0:T(8,128)(2,1)S(1)}, bf16[8,16,384]{2,1,0:T(8,128)(2,1)}, u32[]{:S(2)}) copy-start(bf16[8,16,384]{2,1,0:T(8,128)(2,1)} %tokens.1) | copy-start | bytes 294916
  25.5 4.8 %copy-start.6 = (bf16[8,16,384]{2,1,0:T(8,128)(2,1)S(1)}, bf16[8,16,384]{2,1,0:T(8,128)(2,1)}, u32[]{:S(2)}) copy-start(bf16[8,16,384]{2,1,0:T(8,128)(2,1)} %refs_3_.1) | copy-start | bytes 294916
  28.1 2.0 %collective-permute-start.9 = (bf16[16,48,384]{2,1,0:T(8,128)(2,1)S(1)}, bf16[16,48,384]{2,1,0:T(8,128)(2,1)S(1)}, u32[]{:S(2)}, u32[]{:S(2)}) collective-permute-start(bf16[16,48,384]{2,1,0:T(8,128)(2,1)S(1)} %pad_maximum_fusion.1), channel_id=1, source_target_pairs={{0,1},{1,0},{2,3},{3,2},{4,5},{5,4},{6,7},{7,6},{8,9},{9,8},{10,11... | collective-permute-start | bytes 1769480 | tf_op jit(solution)/shard_map/ppermute | solution.py:341
  34.6 4.1 %collective-permute-start.10 = (bf16[80,384]{1,0:T(8,128)(2,1)S(1)}, bf16[80,384]{1,0:T(8,128)(2,1)S(1)}, u32[]{:S(2)}, u32[]{:S(2)}) collective-permute-start(bf16[80,384]{1,0:T(8,128)(2,1)S(1)} %get-tuple-element.50), channel_id=1, source_target_pairs={{0,1},{1,0},{2,3},{3,2},{4,5},{5,4},{6,7},{7,6},{8,9},{9,8},{10,11... | collective-permute-start | bytes 184328 | tf_op jit(solution)/shard_map/ppermute | solution.py:353
  38.3 0.7 copy-start.2
  38.3 12.9 %collective-permute-start.13 = (bf16[2,4,48,384]{3,2,1,0:T(8,128)(2,1)}, bf16[2,4,48,384]{3,2,1,0:T(8,128)(2,1)}, u32[]{:S(2)}, u32[]{:S(2)}) collective-permute-start(bf16[2,4,48,384]{3,2,1,0:T(8,128)(2,1)} %get-tuple-element.55), channel_id=1, source_target_pairs={{0,1},{1,0},{2,3},{3,2},{4,5},{5,4},{6,7},{7,6},{8,9},{9,8},{10,11... | collective-permute-start | bytes 884744 | tf_op jit(solution)/shard_map/ppermute | solution.py:341
  39.0 8.1 %collective-permute-start.11 = (bf16[3,80,384]{2,1,0:T(8,128)(2,1)S(1)}, bf16[3,80,384]{2,1,0:T(8,128)(2,1)}, u32[]{:S(2)}, u32[]{:S(2)}) collective-permute-start(bf16[3,80,384]{2,1,0:T(8,128)(2,1)S(1)} %pad_maximum_fusion.3.mid), channel_id=1, source_target_pairs={{0,2},{2,0},{4,6},{6,4},{8,10},{10,8},{12,14},{14,12},{16,18},{18,... | collective-permute-start | bytes 552968 | tf_op jit(solution)/shard_map/ppermute | solution.py:359
  41.4 5.6 %collective-permute-start.12 = (bf16[3,80,384]{2,1,0:T(8,128)(2,1)S(1)}, bf16[3,80,384]{2,1,0:T(8,128)(2,1)}, u32[]{:S(2)}, u32[]{:S(2)}) collective-permute-start(bf16[3,80,384]{2,1,0:T(8,128)(2,1)S(1)} %pad_maximum_fusion.3.mid), channel_id=1, source_target_pairs={{2,4},{4,2},{6,8},{8,6},{10,12},{12,10},{14,16},{16,14},{18,20},{2... | collective-permute-start | bytes 552968 | tf_op jit(solution)/shard_map/ppermute | solution.py:359
  47.0 0.9 %copy-start.3 = (f32[128,384]{1,0:T(8,128)S(1)}, f32[128,384]{1,0:T(8,128)}, u32[]{:S(2)}) copy-start(f32[128,384]{1,0:T(8,128)} %copy-done.2) | copy-start | bytes 589828
  51.0 1.2 %copy-start.4 = (f32[128,384]{1,0:T(8,128)}, f32[128,384]{1,0:T(8,128)S(1)}, u32[]{:S(2)}) copy-start(f32[128,384]{1,0:T(8,128)S(1)} %get-tuple-element.53.gl) | copy-start | bytes 589828
  51.1 1.2 %copy-start.7 = (bf16[128,384]{1,0:T(8,128)(2,1)}, bf16[128,384]{1,0:T(8,128)(2,1)S(1)}, u32[]{:S(2)}) copy-start(bf16[128,384]{1,0:T(8,128)(2,1)S(1)} %get-tuple-element.52.gv) | copy-start | bytes 294916
  51.1 1.6 %collective-permute-start.14 = (bf16[2,4,48,384]{3,2,1,0:T(8,128)(2,1)S(1)}, bf16[2,4,48,384]{3,2,1,0:T(8,128)(2,1)S(1)}, u32[]{:S(2)}, u32[]{:S(2)}) collective-permute-start(bf16[2,4,48,384]{3,2,1,0:T(8,128)(2,1)S(1)} %get-tuple-element.57), channel_id=1, source_target_pairs={{0,1},{1,0},{2,3},{3,2},{4,5},{5,4},{6,7},{7,6},{8,9},{9,8},{10,11... | collective-permute-start | bytes 884744 | tf_op jit(solution)/shard_map/ppermute | solution.py:341
  52.8 10.8 %collective-permute-start.17 = (bf16[4,48,384]{2,1,0:T(8,128)(2,1)S(1)}, bf16[4,48,384]{2,1,0:T(8,128)(2,1)S(1)}, u32[]{:S(2)}, u32[]{:S(2)}) collective-permute-start(bf16[4,48,384]{2,1,0:T(8,128)(2,1)S(1)} %pad_maximum_fusion.7), channel_id=1, source_target_pairs={{0,6},{1,7},{2,4},{3,5},{4,2},{5,3},{6,0},{7,1},{8,14},{9,15},{10,... | collective-permute-start | bytes 442376 | tf_op jit(solution)/shard_map/ppermute | solution.py:341
  59.2 12.1 %copy-start.5 = (f32[128,384]{1,0:T(8,128)S(1)}, f32[128,384]{1,0:T(8,128)}, u32[]{:S(2)}) copy-start(f32[128,384]{1,0:T(8,128)} %copy-done.4) | copy-start | bytes 589828
  59.2 12.1 %copy-start.8 = (bf16[128,384]{1,0:T(8,128)(2,1)S(1)}, bf16[128,384]{1,0:T(8,128)(2,1)}, u32[]{:S(2)}) copy-start(bf16[128,384]{1,0:T(8,128)(2,1)} %copy-done.7) | copy-start | bytes 294916
  59.2 7.3 %collective-permute-start.16 = (bf16[4,48,384]{2,1,0:T(8,128)(2,1)S(1)}, bf16[4,48,384]{2,1,0:T(8,128)(2,1)S(1)}, u32[]{:S(2)}, u32[]{:S(2)}) collective-permute-start(bf16[4,48,384]{2,1,0:T(8,128)(2,1)S(1)} %pad_maximum_fusion.6), channel_id=1, source_target_pairs={{0,4},{1,5},{2,6},{3,7},{4,0},{5,1},{6,2},{7,3},{8,12},{9,13},{10,... | collective-permute-start | bytes 442376 | tf_op jit(solution)/shard_map/ppermute | solution.py:341
  59.5 7.0 %collective-permute-start.15 = (bf16[4,48,384]{2,1,0:T(8,128)(2,1)S(1)}, bf16[4,48,384]{2,1,0:T(8,128)(2,1)S(1)}, u32[]{:S(2)}, u32[]{:S(2)}) collective-permute-start(bf16[4,48,384]{2,1,0:T(8,128)(2,1)S(1)} %pad_maximum_fusion.5), channel_id=1, source_target_pairs={{0,2},{1,3},{2,0},{3,1},{4,6},{5,7},{6,4},{7,5},{8,10},{9,11},{10,... | collective-permute-start | bytes 442376 | tf_op jit(solution)/shard_map/ppermute | solution.py:341
  66.7 6.1 %collective-permute-start.20 = (bf16[48,384]{1,0:T(8,128)(2,1)S(1)}, bf16[48,384]{1,0:T(8,128)(2,1)S(1)}, u32[]{:S(2)}, u32[]{:S(2)}) collective-permute-start(bf16[48,384]{1,0:T(8,128)(2,1)S(1)} %get-tuple-element.67), channel_id=1, source_target_pairs={{0,24},{1,25},{2,26},{3,27},{4,28},{5,29},{6,30},{7,31},{8,16},{9,... | collective-permute-start | bytes 110600 | tf_op jit(solution)/shard_map/ppermute | solution.py:341
  70.7 4.9 %collective-permute-start.19 = (bf16[48,384]{1,0:T(8,128)(2,1)S(1)}, bf16[48,384]{1,0:T(8,128)(2,1)S(1)}, u32[]{:S(2)}, u32[]{:S(2)}) collective-permute-start(bf16[48,384]{1,0:T(8,128)(2,1)S(1)} %get-tuple-element.68), channel_id=1, source_target_pairs={{0,16},{1,17},{2,18},{3,19},{4,20},{5,21},{6,22},{7,23},{8,24},{9,... | collective-permute-start | bytes 110600 | tf_op jit(solution)/shard_map/ppermute | solution.py:341
  70.7 4.9 %collective-permute-start.18 = (bf16[48,384]{1,0:T(8,128)(2,1)S(1)}, bf16[48,384]{1,0:T(8,128)(2,1)S(1)}, u32[]{:S(2)}, u32[]{:S(2)}) collective-permute-start(bf16[48,384]{1,0:T(8,128)(2,1)S(1)} %get-tuple-element.66), channel_id=1, source_target_pairs={{0,8},{1,9},{2,10},{3,11},{4,12},{5,13},{6,14},{7,15},{8,0},{9,1},... | collective-permute-start | bytes 110600 | tf_op jit(solution)/shard_map/ppermute | solution.py:341

commit v2 on v1

--- a/solution.py
+++ b/solution.py
@@ -12,7 +12,7 @@
 HEADS = 6
 TILE = 8
 PER = TILE * TILE
-BLK = PER + 16
+BLK = PER + 8
 AXES = ("rows", "cols")
 
 norm_epsilon = 1e-05
@@ -68,7 +68,10 @@
 
 
 def head_normalise(raw, ones, width):
-    factor = lax.rsqrt(head_sums(raw * raw, ones) * (1.0 / width) + head_epsilon)
+    squares = (raw * raw).astype(BF16)
+    step = ones.shape[0]
+    sums = [dot(squares[:, p : p + step], ones) for p in range(0, raw.shape[1], step)]
+    factor = lax.rsqrt(jnp.concatenate(sums, axis=1) * (1.0 / width) + head_epsilon)
     return raw * factor, factor
 
 
@@ -90,8 +93,27 @@
     return jnp.where(lane < width, stacked[:half], stacked[half:])
 
 
-def strip_tiles(strips):
-    return [strip.at[g] for strip in strips for g in range(strip.shape[0])]
+def strip_tiles(strips, odd):
+    tiles = []
+    for n in range(3):
+        tiles += strips[0] if n == 0 else [strips[n].at[0], strips[n].at[1]]
+        for side in range(1, len(strips) // 3):
+            tiles.append(strips[3 * side + n].at[odd if side == 1 else 1 - odd])
+    return tiles
+
+
+def packed_tiles(v, n_tiles):
+    return [v.at[pl.ds(n_tiles * PER + t * BLK, BLK)] for t in range(2)]
+
+
+def pack_stats(stats, width):
+    blank = jnp.zeros((8, width - 2 * PER), F32)
+    return jnp.concatenate([stats[0:8], stats[8:16], blank], axis=1).astype(BF16)
+
+
+def unpack_stats(tile):
+    rows = tile[PER:BLK, 0 : 2 * PER].astype(F32)
+    return jnp.concatenate([rows[:, 0:PER], rows[:, PER:]], axis=0)
 
 
 def near_rows(groups, odd, n_tiles):
@@ -103,22 +125,18 @@
     return left, right
 
 
-def prep_kernel(scalars, tissue, tokens, low_out, send_a_out, send_b_out):
-    odd = scalars[0]
+def prep_kernel(tissue, tokens, low_out):
     normed, _ = normalise(tiles_of(tokens[...].astype(F32)))
     low = normed.astype(BF16)
     width = low.shape[1]
     for t in range(2):
         low_out[t, 0:PER, :] = low[t * PER : (t + 1) * PER]
         low_out[t, PER:BLK, :] = jnp.full((BLK - PER, width), tissue[0, t].astype(F32)).astype(BF16)
-    send_a_out[...] = low_out[1 - odd]
-    if send_b_out is not None:
-        send_b_out[...] = low_out[odd]
 
 
 def forward_kernel(groups, place, *refs):
-    scalars, wblk, tokens, teacher = refs[:4]
-    tiles = strip_tiles(refs[4:7])
+    scalars, first_half, second_half, tokens, teacher, *refs = refs
+    n_strips = 3 * (groups - 1)
     (
         wq_out,
         wk_out,
@@ -131,32 +149,46 @@
         near_out,
         stats_out,
         pack_out,
-        *sends_out,
         wo_scr,
-    ) = refs[7:]
+    ) = refs[n_strips:]
     odd, base = scalars[0], scalars[1]
-    n_blocks, per_block, model = wblk.shape
+    own_strip, *others = refs[:n_strips]
+    tiles = strip_tiles([[own_strip.at[0], own_strip.at[1]], *others], odd)
+    half, per_block, model = first_half.shape
+    n_blocks = 2 * half
     width = model // HEADS
     own = 2 * PER
     per_matrix = n_blocks // 4
-    for d in range(n_blocks):
-        whole = (wq_out, wk_out, wv_out, wo_scr)[d // per_matrix]
-        at = d % per_matrix * per_block
-        whole[at : at + per_block, :] = wblk[jnp.bitwise_xor(base, place[d])]
+    swapped = (base >= half).astype(jnp.int32)
+    for way in (0, 1):
+
+        @pl.when(swapped == way)
+        def _():
+            for d in range(n_blocks):
+                whole = (wq_out, wk_out, wv_out, wo_scr)[d // per_matrix]
+                at = d % per_matrix * per_block
+                source = first_half if (place[d] >= half) == way else second_half
+                whole[at : at + per_block, :] = source[jnp.bitwise_xor(base, place[d]) % half]
+
     n_tiles = 3 * groups
     flag_rows = []
-    for n, tile in enumerate(tiles):
-        x_out[n * PER : (n + 1) * PER, :] = tile[0:PER, :]
-        flag_rows.append(tile[PER:BLK, :].astype(F32)[0:1, 0:PER])
     ones = pair_ones(width)
-    x = x_out[...]
-    k_normal, _ = head_normalise(dot(x, wk_out[...]), ones, width)
-    keys = k_normal.astype(BF16)
+    key_parts, value_parts = [], []
+    for first, last in ((0, groups), (groups, n_tiles)):
+        for n in range(first, last):
+            x_out[n * PER : (n + 1) * PER, :] = tiles[n][0:PER, :]
+            flag_rows.append(tiles[n][PER:BLK, :].astype(F32)[0:1, 0:PER])
+        x = x_out[first * PER : last * PER, :]
+        if first == 0:
+            q_normal, _ = head_normalise(dot(x[0:own], wq_out[...]), ones, width)
+            queries = q_normal.astype(BF16)
+        k_normal, _ = head_normalise(dot(x, wk_out[...]), ones, width)
+        key_parts.append(k_normal.astype(BF16))
+        value_parts.append(dot(x, wv_out[...]).astype(BF16))
+    keys = jnp.concatenate(key_parts, axis=0)
+    values = jnp.concatenate(value_parts, axis=0)
     k_out[...] = keys
-    values = dot(x, wv_out[...]).astype(BF16)
-    v_out[...] = values
-    q_normal, _ = head_normalise(dot(x[0:own], wq_out[...]), ones, width)
-    queries = q_normal.astype(BF16)
+    v_out[0 : n_tiles * PER, :] = values
 
     flags = jnp.concatenate(flag_rows, axis=1)
     left, right = near_rows(groups, odd, n_tiles)
@@ -198,11 +230,8 @@
     for t in range(2):
         here = slice(t * PER, (t + 1) * PER)
         pack_out[t, 0:PER, :] = grad_mixed[here]
-        padded = jnp.concatenate([stats[:, here], jnp.zeros((16, model - PER), F32)], axis=1)
-        pack_out[t, PER:BLK, :] = padded.astype(BF16)
-    sends_out[0][...] = pack_out[1 - odd]
-    if len(sends_out) > 1:
-        sends_out[1][...] = pack_out[odd]
+        pack_out[t, PER:BLK, :] = pack_stats(stats[:, here], model)
+        packed_tiles(v_out, n_tiles)[t][...] = pack_out[t]
 
 
 def store_terms(fast, odd, grads, outs):
@@ -221,25 +250,31 @@
             send[m, b] = jnp.where(is_odd, even_part, odd_part).astype(BF16)
 
 
-def query_kernel(fast, scalars, wq, x, k, v, mixed, gout, near_in, stats_in, pack, q_out, gl_out, *outs):
+def halo_query_kernel(wq, x, q_out):
+    model = x.shape[1]
+    width = model // HEADS
+    q_normal, _ = head_normalise(dot(x[...], wq[...]), pair_ones(width), width)
+    q_out[...] = q_normal.astype(BF16)
+
+
+def query_kernel(fast, scalars, wq, x, k, v, mixed, gout, near_in, stats_in, *outs):
     core = scalars[2]
     model = wq.shape[0]
     width = model // HEADS
     own = 2 * PER
     n_tiles = near_in.shape[1] // PER
     ones = pair_ones(width)
-    q_normal, q_factor = head_normalise(dot(x[...], wq[...]), ones, width)
-    q_all = q_normal.astype(BF16)
-    q_out[...] = q_all
-    q_normal, q_factor, queries = q_normal[0:own], q_factor[0:own], q_all[0:own]
+    q_normal, q_factor = head_normalise(dot(x[0:own, :], wq[...]), ones, width)
+    queries = q_normal.astype(BF16)
     near = jnp.stack([near_in[0:1], near_in[1:2]] * 2)
     stats = stats_in[...].astype(BF16).astype(F32)
-    grad_mixed = jnp.concatenate([pack[t, 0:PER, :] for t in range(2)], axis=0)
+    gq_out, *outs = outs
+    grad_mixed = jnp.concatenate([pack[0:PER, :] for pack in packed_tiles(v, n_tiles)], axis=0)
     scale = 1.0 / math.sqrt(width)
     parts = []
     for p in range(HEADS // 2):
         lanes = slice(2 * width * p, 2 * width * (p + 1))
-        keys, values = k[:, lanes], v[:, lanes]
+        keys, values = k[:, lanes], v[0 : n_tiles * PER, lanes]
         scores = dot_nt(split_heads(queries[:, lanes], width), keys) * scale
         inverse = jnp.concatenate([stats[:, 2 * p : 2 * p + 1], stats[:, 2 * p + 1 : 2 * p + 2]], axis=0)
         at = HEADS + 2 * p
@@ -251,26 +286,33 @@
         parts.append(join_heads(dot(grad_scores, keys), width))
     grad_qn = jnp.concatenate(parts, axis=1)
     grad_query = head_back(q_normal, q_factor, grad_qn, ones, width).astype(BF16)
-    gl_out[...] = dot_nt(grad_query, wq[...])
+    gq_out[...] = grad_query
     grad_wq = dot_tn(x[0:own, :], grad_query)
     grad_wo = dot_tn(mixed[...], gout[...].astype(BF16))
     store_terms(fast, core, [grad_wq, grad_wo], outs)
 
 
-def key_kernel(groups, fast, scalars, x, k, v, q, wk, gl, mid, near, far, gk_out, gv_out, gl_out, *rest):
-    *outs, g_scr = rest
-    tiles = strip_tiles((mid, near, far))
-    gl_out[...] = gl[...]
+def key_kernel(groups, fast, scalars, x, k, v, wk, q, *refs):
+    n_strips = 3 * (groups - 1)
+    sources, refs = refs[: n_strips - 1], refs[n_strips - 1 :]
+    if fast:
+        kept, arrived, sums_out, *refs = refs
+        sums_out[...] = kept[...] + arrived[...].astype(F32)
+    *refs, g_scr = refs
+    gk_out, gv_out, *outs = refs
     odd, core = scalars[0], scalars[2]
-    model = q.shape[1]
+    model = x.shape[1]
     width = model // HEADS
     own = 2 * PER
     n_tiles = 3 * groups
     ones = pair_ones(width)
+    tiles = strip_tiles([packed_tiles(v, n_tiles), *sources], odd)
+    x_own = x[0:own, :]
+    k_normal, k_factor = head_normalise(dot(x_own, wk[...]), ones, width)
     stat_parts = []
     for n, tile in enumerate(tiles):
         g_scr[n * PER : (n + 1) * PER, :] = tile[0:PER, :]
-        stat_parts.append(tile[PER:BLK, :].astype(F32)[:, 0:PER])
+        stat_parts.append(unpack_stats(tile))
     stats = jnp.concatenate(stat_parts, axis=1)
     left, right = near_rows(groups, odd, n_tiles)
     flag = stats[2 * HEADS : 2 * HEADS + 1]
@@ -293,8 +335,6 @@
         key_parts.append(join_heads(dot(grad_scores, queries), width))
         value_parts.append(join_heads(dot(low, grads), width))
     grad_kn = jnp.concatenate(key_parts, axis=1)
-    x_own = x[0:own, :]
-    k_normal, k_factor = head_normalise(dot(x_own, wk[...]), ones, width)
     grad_key = head_back(k_normal, k_factor, grad_kn, ones, width).astype(BF16)
     grad_value = jnp.concatenate(value_parts, axis=1).astype(BF16)
     gk_out[...] = grad_key
@@ -302,9 +342,11 @@
     store_terms(fast, core, [dot_tn(x_own, grad_key), dot_tn(x_own, grad_value)], outs)
 
 
-def final_kernel(tokens, wk, wv, gk, gv, gl, gout, out):
+def final_kernel(tokens, wq, wk, wv, gq, gk, gv, gout, out):
     model = gk.shape[1]
-    grad_lowered = gl[...] + dot_nt(gk[...], wk[...]) + dot_nt(gv[...], wv[...])
+    grad_lowered = (
+        dot_nt(gq[...], wq[...]) + dot_nt(gk[...], wk[...]) + dot_nt(gv[...], wv[...])
+    )
     normed, inv_std = normalise(tiles_of(tokens[...].astype(F32)))
     grads = gout[...] + inv_std * (
         grad_lowered
@@ -315,8 +357,13 @@
     out[...] = jnp.concatenate(pieces, axis=1).astype(BF16)
 
 
+ANY = pl.BlockSpec(memory_space=pl.ANY)
 SMEM = pl.BlockSpec(memory_space=pltpu.SMEM)
 VMEM = pl.BlockSpec(memory_space=pltpu.VMEM)
+
+
+def in_hbm(value):
+    return pltpu.with_memory_space_constraint(value, pltpu.HBM)
 
 
 def call(kernel, in_specs, shapes, args, scratch=(), kept=0, held=()):
@@ -348,15 +395,19 @@
     return pairs
 
 
-def across(own, sides):
-    cols = lax.axis_size("cols")
-    parts = [lax.ppermute(v, "cols", side_pairs(cols, n))[None] for n, v in enumerate(sides)]
-    return jnp.concatenate([own] + parts, axis=0)
-
-
 def beside(strip):
     rows = lax.axis_size("rows")
-    return [lax.ppermute(strip, "rows", side_pairs(rows, n)) for n in range(2)]
+    near = lax.ppermute(strip, "rows", side_pairs(rows, 0))
+    return [strip, near, lax.ppermute(strip, "rows", side_pairs(rows, 1))]
+
+
+def across(strips):
+    cols = lax.axis_size("cols")
+    return [
+        lax.ppermute(strip, "cols", side_pairs(cols, n))
+        for n in range(1 if cols == 2 else 2)
+        for strip in strips
+    ]
 
 
 def layer(tokens, teacher, tissue, weights):
@@ -372,6 +423,7 @@
     odd = lax.axis_index("cols") % 2
     own = 2 * PER
     n_keys = 3 * groups * PER
+    n_strips = 3 * (groups - 1)
 
     def spot(d):
         return (d % 2) * (count // 2) + (d // 2 % spots) * 4 + d // per_matrix
@@ -382,47 +434,49 @@
         place, base = list(range(4)), jnp.int32(0)
     scalars = jnp.stack([odd, base, index % 2, index]).astype(jnp.int32)
 
-    tile_shape = ((BLK, model), BF16)
-    sends_shape = [tile_shape] * (groups - 2)
-    prep = prep_kernel if groups == 4 else lambda *refs: prep_kernel(*refs, None)
-    low, *sends = call(
-        prep, [SMEM, SMEM, VMEM], [((2, BLK, model), BF16)] + sends_shape, (scalars, tissue, tokens)
+    (low,) = call(
+        prep_kernel,
+        [SMEM, VMEM],
+        [((2, BLK, model), BF16)],
+        (
+            in_hbm(tissue),
+            in_hbm(tokens),
+        ),
     )
     if fast:
         wblk = weights.reshape(1, per_block, model)
         parts = [swap(wblk, count, per_matrix * step) for step in range(1, 4)]
         wblk = jnp.concatenate([wblk] + parts, axis=0)
-        mid = across(low, sends)
-        wblk, mid = lax.optimization_barrier((wblk, mid))
         parts = [swap(wblk, count, 2 * step) for step in range(1, spots)]
-        sides = beside(mid)
+        strips = beside(low)
         wblk = jnp.concatenate([wblk] + parts, axis=0)
-        wblk, sides = lax.optimization_barrier((wblk, sides))
-        wblk = jnp.concatenate([wblk, swap(wblk, count, 1)], axis=0)
+        halves = [wblk, swap(wblk, count, 1)]
+        strips = strips + across(strips)
     else:
-        mid = across(low, sends)
-        sides = beside(mid)
+        strips = beside(low)
+        strips = strips + across(strips)
         wblk = lax.all_gather(weights, AXES, axis=0, tiled=True).reshape(4, model, model)
-
-    wq, wk, wv, x, k, v, mixed, gout, near, stats, pack, *sends = call(
+        halves = [wblk[0:2], wblk[2:4]]
+
+    wq, wk, wv, x, k, v, mixed, gout, near, stats, pack = call(
         functools.partial(forward_kernel, groups, place),
-        [SMEM] + [VMEM] * 6,
+        [SMEM] + [VMEM] * (4 + n_strips),
         [((model, model), BF16)] * 3
-        + [((n_keys, model), BF16)] * 3
+        + [((n_keys, model), BF16)] * 2
+        + [((n_keys + 2 * BLK, model), BF16)]
         + [
             ((own, model), BF16),
             ((own, model), F32),
             ((2, n_keys), F32),
             ((own, own), F32),
             ((2, BLK, model), BF16),
-        ]
-        + sends_shape,
-        (scalars, wblk, tokens, teacher, mid, *sides),
+        ],
+        (scalars, *halves, tokens, in_hbm(teacher), *map(in_hbm, strips[:3]), *strips[3:]),
         scratch=[pltpu.VMEM((model, model), BF16)],
         kept=10,
     )
-    packs = across(pack, sends)
-    packs = [packs] + beside(packs)
+    packs = beside(pack)
+    packs = packs + across(packs)
 
     if fast:
         term_shapes = [
@@ -431,29 +485,37 @@
         ]
     else:
         term_shapes = [((2, model, model), F32)]
-    q, gl, *terms_qo = call(
+    gq, *terms_qo = call(
         functools.partial(query_kernel, fast),
-        [SMEM] + [VMEM] * 9,
-        [((n_keys, model), BF16), ((own, model), F32)] + term_shapes,
-        (scalars, wq, x, k, v, mixed, gout, near, stats, pack),
-        kept=4 if fast else 2,
+        [SMEM] + [VMEM] * 8,
+        [((own, model), BF16)] + term_shapes,
+        (scalars, wq, x, k, v, mixed, gout, near, stats),
+        kept=2,
         held=range(1, 9),
     )
-    gk, gv, gl, *terms_kv = call(
+    (q,) = call(
+        halo_query_kernel, [VMEM] * 2, [((n_keys, model), BF16)], (wq, x), kept=1, held=range(2)
+    )
+    more = []
+    if fast:
+        more = [terms_qo[0], swap(terms_qo[1], count, 1)]
+    results = call(
         functools.partial(key_kernel, groups, fast),
-        [SMEM] + [VMEM] * 9,
-        [((own, model), BF16), ((own, model), BF16), ((own, model), F32)] + term_shapes,
-        (scalars, x, k, v, q, wk, gl, *packs),
+        [SMEM] + [VMEM] * (4 + n_strips + len(more)),
+        term_shapes[: len(more) // 2] + [((own, model), BF16)] * 2 + term_shapes,
+        (scalars, x, k, v, wk, q, *packs[1:], *more),
         scratch=[pltpu.VMEM((n_keys, model), BF16)],
-        kept=5 if fast else 3,
-        held=range(1, 7),
-    )
+        kept=5 if fast else 2,
+        held=[*range(1, 6)] + ([5 + n_strips] if fast else []),
+    )
+    sums_qo, results = (results[0], results[1:]) if fast else (None, results)
+    gk, gv, *terms_kv = results
     (grads,) = call(
         final_kernel,
-        [VMEM] * 7,
+        [VMEM] * 8,
         [(tokens.shape, BF16)],
-        (tokens, wk, wv, gk, gv, gl, gout),
-        held=range(1, 7),
+        (tokens, wq, wk, wv, gq, gk, gv, gout),
+        held=range(1, 8),
     )
 
     n_tokens = tokens.shape[0] * rows * tokens.shape[1] * cols
@@ -468,11 +530,7 @@
     def pick(values, at, axis):
         return lax.dynamic_index_in_dim(values, at, axis, keepdims=False)
 
-    def with_core(keep, send):
-        return keep + swap(send, count, 1).astype(F32)
-
-    sums_qo = with_core(*terms_qo)
-    sums_kv = with_core(*terms_kv)
+    sums_kv = terms_kv[0] + swap(terms_kv[1], count, 1).astype(F32)
 
     def all_four(at):
         qo, kv = pick(sums_qo, at, 1), pick(sums_kv, at, 1)

time: 76.5 us -> 77.3 us (1.010)
  starting transfers between devices: 27.8 us -> 29.6 us
  Pallas kernels: 12.7 us -> 14.4 us
  other arithmetic: 1.64 us -> 0.31 us
  waiting for transfers between devices: 28.9 us -> 27.7 us
    ppermute x15, waiting for transfers between devices: 22 us -> 19.9 us  [swap(): return lax.ppermute(value, AXES, [(i, i ^ mask) for i in range(count)])]
    pallas_call x5 -> x6, Pallas kernels: 12.7 us -> 14.4 us  [call(): pl.pallas_call(kernel, out_shape=[pltpu.VMEM(s, t) if n < kept else jax.S...]
    ppermute x6 -> x10, starting transfers between devices: 6.25 us -> 7.31 us  [the longest x2 4.56 us: beside(): near = lax.ppermute(strip, 'rows', side_pairs(rows, 0))]
    add x2 -> x1, other arithmetic: 1.08 us -> 0.06 us  [layer(): sums_kv = terms_kv[0] + swap(terms_kv[1], count, 1).astype(F32)]
    ppermute x6 -> x10, waiting for transfers between devices: 6.88 us -> 7.79 us  [the longest x2 7.14 us: beside(): near = lax.ppermute(strip, 'rows', side_pairs(rows, 0))]
    unnamed x20 -> x33, local copies, waits for them, and re-layouts: 2.78 us -> 2.51 us
  transfers between devices with their start and end apart: 21 -> 25, of which waited for: 12 -> 16; matrix products, arithmetic and copies ran while one was open for 2% -> 0% of each run, Pallas kernels for 11% -> 4%
where the time goes in v2:
time: 77.3 us; the launch traced here: 77 us
  starting transfers between devices  29.6 us (38%)
  waiting for transfers between devices  27.7 us (36%)
  Pallas kernels  14.4 us (19%)
  local copies, waits for them, and re-layouts  4.13 us (5%)
  between operations  0.91 us (1%)
    ppermute x15, starting transfers between devices, swap(): return lax.ppermute(value, AXES, [(i, i ^ mask) for i in range(count)])  22.3 us
    ppermute x15, waiting for transfers between devices, swap(): return lax.ppermute(value, AXES, [(i, i ^ mask) for i in range(count)])  19.9 us
    pallas_call x6, Pallas kernels, call(): pl.pallas_call(kernel, out_shape=[pltpu.VMEM(s, t) if n < kept else jax.S...  14.4 us
    ppermute x2, waiting for transfers between devices, beside(): near = lax.ppermute(strip, 'rows', side_pairs(rows, 0))  7.14 us
    ppermute x2, starting transfers between devices, beside(): near = lax.ppermute(strip, 'rows', side_pairs(rows, 0))  4.56 us
    unnamed x33, local copies, waits for them, and re-layouts  2.51 us
  transfers between devices with their start and end apart: 25, of which 16 were waited for; matrix products, arithmetic and copies ran while one was open for 0% of the time, Pallas kernels for 4%

profile of v2, /device:TPU:0, one launch (start us, length us, event | category | flops | bytes accessed | tf_op | source)
XLA Modules:
  0.0 77.0 jit_solution(4301112436053503284)
XLA Ops:
  0.6 0.8 %reshape.27 = bf16[1,48,384]{2,1,0:T(8,128)(2,1)S(1)} reshape(bf16[18432]{0:T(1024)(128)(2,1)} %param.7) | data formatting | bytes 73728 | tf_op jit(solution)/shard_map/reshape | solution.py:447
  1.4 3.1 %collective-permute-start = (bf16[1,48,384]{2,1,0:T(8,128)(2,1)S(1)}, bf16[1,48,384]{2,1,0:T(8,128)(2,1)S(1)}, u32[]{:S(2)}, u32[]{:S(2)}) collective-permute-start(bf16[1,48,384]{2,1,0:T(8,128)(2,1)S(1)} %reshape.27), channel_id=1, source_target_pairs={{0,8},{1,9},{2,10},{3,11},{4,12},{5,13},{6,14},{7,15},{8,0},{9,1},... | collective-permute-start | bytes 110600 | tf_op jit(solution)/shard_map/ppermute | solution.py:388
  4.5 2.6 %collective-permute-start.1 = (bf16[1,48,384]{2,1,0:T(8,128)(2,1)S(1)}, bf16[1,48,384]{2,1,0:T(8,128)(2,1)S(1)}, u32[]{:S(2)}, u32[]{:S(2)}) collective-permute-start(bf16[1,48,384]{2,1,0:T(8,128)(2,1)S(1)} %reshape.27), channel_id=1, source_target_pairs={{0,16},{1,17},{2,18},{3,19},{4,20},{5,21},{6,22},{7,23},{8,24},{9,... | collective-permute-start | bytes 110600 | tf_op jit(solution)/shard_map/ppermute | solution.py:388
  7.1 0.0 collective-permute-start.2
  7.1 0.0 collective-permute-done
  7.2 2.9 %collective-permute-done.1 = bf16[1,48,384]{2,1,0:T(8,128)(2,1)S(1)} collective-permute-done((bf16[1,48,384]{2,1,0:T(8,128)(2,1)S(1)}, bf16[1,48,384]{2,1,0:T(8,128)(2,1)S(1)}, u32[]{:S(2)}, u32[]{:S(2)}) %collective-permute-start.1) | collective-permute-done | bytes 36896 | tf_op jit(solution)/shard_map/ppermute | solution.py:388
  10.1 2.8 %collective-permute-done.2 = bf16[1,48,384]{2,1,0:T(8,128)(2,1)S(1)} collective-permute-done((bf16[1,48,384]{2,1,0:T(8,128)(2,1)S(1)}, bf16[1,48,384]{2,1,0:T(8,128)(2,1)S(1)}, u32[]{:S(2)}, u32[]{:S(2)}) %collective-permute-start.2) | collective-permute-done | bytes 36896 | tf_op jit(solution)/shard_map/ppermute | solution.py:388
  12.9 1.6 %collective-permute-start.3 = (bf16[4,48,384]{2,1,0:T(8,128)(2,1)S(1)}, bf16[4,48,384]{2,1,0:T(8,128)(2,1)S(1)}, u32[]{:S(2)}, u32[]{:S(2)}) collective-permute-start(bf16[4,48,384]{2,1,0:T(8,128)(2,1)S(1)} %get-tuple-element.57), channel_id=1, source_target_pairs={{0,2},{1,3},{2,0},{3,1},{4,6},{5,7},{6,4},{7,5},{8,10},{9,11},{10,... | collective-permute-start | bytes 442376 | tf_op jit(solution)/shard_map/ppermute | solution.py:388
  14.5 1.5 %collective-permute-start.4 = (bf16[4,48,384]{2,1,0:T(8,128)(2,1)S(1)}, bf16[4,48,384]{2,1,0:T(8,128)(2,1)S(1)}, u32[]{:S(2)}, u32[]{:S(2)}) collective-permute-start(bf16[4,48,384]{2,1,0:T(8,128)(2,1)S(1)} %get-tuple-element.57), channel_id=1, source_target_pairs={{0,4},{1,5},{2,6},{3,7},{4,0},{5,1},{6,2},{7,3},{8,12},{9,13},{10,... | collective-permute-start | bytes 442376 | tf_op jit(solution)/shard_map/ppermute | solution.py:388
  16.0 0.5 collective-permute-start.5
  16.5 2.9 %collective-permute-done.3 = bf16[4,48,384]{2,1,0:T(8,128)(2,1)S(1)} collective-permute-done((bf16[4,48,384]{2,1,0:T(8,128)(2,1)S(1)}, bf16[4,48,384]{2,1,0:T(8,128)(2,1)S(1)}, u32[]{:S(2)}, u32[]{:S(2)}) %collective-permute-start.3) | collective-permute-done | bytes 147488 | tf_op jit(solution)/shard_map/ppermute | solution.py:388
  19.4 2.8 %collective-permute-done.4 = bf16[4,48,384]{2,1,0:T(8,128)(2,1)S(1)} collective-permute-done((bf16[4,48,384]{2,1,0:T(8,128)(2,1)S(1)}, bf16[4,48,384]{2,1,0:T(8,128)(2,1)S(1)}, u32[]{:S(2)}, u32[]{:S(2)}) %collective-permute-start.4) | collective-permute-done | bytes 147488 | tf_op jit(solution)/shard_map/ppermute | solution.py:388
  22.2 0.0 collective-permute-done.5
  22.2 0.1 collective-permute-start.6
  22.3 1.1 %shard_map.59.refs_5_ = bf16[2,72,384]{2,1,0:T(8,128)(2,1)S(1)} custom-call(s32[1,2]{1,0:T(1,128)} %tissue.1, bf16[8,16,384]{2,1,0:T(8,128)(2,1)} %tokens.3), custom_call_target="tpu_custom_call" | custom-call | tf_op jit(solution)/shard_map/pallas_call | solution.py:374
  23.4 0.0 copy-start
  23.4 0.4 collective-permute-start.7
  23.9 0.7 collective-permute-start.8
  24.5 0.3 collective-permute-start.9
  24.8 4.2 %collective-permute-done.7.refs_6_ = bf16[2,72,384]{2,1,0:T(8,128)(2,1)S(1)} collective-permute-done((bf16[2,72,384]{2,1,0:T(8,128)(2,1)S(1)}, bf16[2,72,384]{2,1,0:T(8,128)(2,1)S(1)}, u32[]{:S(2)}, u32[]{:S(2)}) %collective-permute-start.7) | collective-permute-done | bytes 110624 | tf_op jit(solution)/shard_map/ppermute | solution.py:400
  29.0 0.0 collective-permute-done.8.refs_7_
  29.0 0.5 collective-permute-start.11
  29.5 0.1 pad_add_fusion.refs_0_.scalars
  29.6 0.6 copy-done.4
  30.2 0.1 collective-permute-done.10.refs_9_
  30.3 0.2 collective-permute-done.11.refs_10_
  30.5 0.9 %copy-done.5 = bf16[2,72,384]{2,1,0:T(8,128)(2,1)S(1)} copy-done((bf16[2,72,384]{2,1,0:T(8,128)(2,1)S(1)}, bf16[2,72,384]{2,1,0:T(8,128)(2,1)}, u32[]{:S(2)}) %copy-start.5) | copy-done | bytes 110616
  31.4 5.4 %shard_map.60 = (bf16[384,384]{1,0:T(8,128)(2,1)S(1)}, bf16[384,384]{1,0:T(8,128)(2,1)S(1)}, bf16[384,384]{1,0:T(8,128)(2,1)S(1)}, bf16[576,384]{1,0:T(8,128)(2,...) custom-call(s32[4]{0:T(128)S(1)} %pad_add_fusion.refs_0_.scalars, ...), custom_call_target="tpu_custom_call" | custom-call | tf_op jit(solution)/shard_map/pallas_call | solution.py:374
  36.8 3.2 %shard_map.61 = (bf16[128,384]{1,0:T(8,128)(2,1)S(1)}, f32[2,4,48,384]{3,2,1,0:T(8,128)S(1)}, bf16[2,4,48,384]{3,2,1,0:T(8,128)(2,1)}) custom-call(s32[4]{0:T(128)S(1)} %pad_add_fusion.refs_0_.scalars, bf16[384,384]{1,0:T(8,128)(2,1)S(1)} %get-tuple-element.21.wq, bf16[576,384]{1,0:T(8,128)(2,1)S(1)} %get-tuple-element.24.x, ...), custom_call_target="tpu_custom_call" | custom-call | tf_op jit(solution)/shard_map/pallas_call | solution.py:374
  39.9 0.6 copy-done.6
  40.6 0.4 collective-permute-start.17
  40.9 4.1 %collective-permute-start.12 = (bf16[2,72,384]{2,1,0:T(8,128)(2,1)}, bf16[2,72,384]{2,1,0:T(8,128)(2,1)S(1)}, u32[]{:S(2)}, u32[]{:S(2)}) collective-permute-start(bf16[2,72,384]{2,1,0:T(8,128)(2,1)} %get-tuple-element.32), channel_id=1, source_target_pairs={{0,2},{2,0},{4,6},{6,4},{8,10},{10,8},{12,14},{14,12},{16,18},{18,... | collective-permute-start | bytes 331784 | tf_op jit(solution)/shard_map/ppermute | solution.py:400
  45.1 0.7 collective-permute-start.13
  45.7 0.1 collective-permute-start.14
  45.9 3.0 %collective-permute-done.12.refs_0_ = bf16[2,72,384]{2,1,0:T(8,128)(2,1)S(1)} collective-permute-done((bf16[2,72,384]{2,1,0:T(8,128)(2,1)}, bf16[2,72,384]{2,1,0:T(8,128)(2,1)S(1)}, u32[]{:S(2)}, u32[]{:S(2)}) %collective-permute-start.12) | collective-permute-done | bytes 110624 | tf_op jit(solution)/shard_map/ppermute | solution.py:400
  48.9 0.0 collective-permute-start.15
  48.9 0.0 collective-permute-done.13.refs_1_
  48.9 0.5 collective-permute-start.16
  49.4 0.7 shard_map.62.q
  50.1 0.0 collective-permute-done.14.refs_2_
  50.1 0.2 collective-permute-done.15.refs_3_
  50.3 0.2 collective-permute-done.16.refs_4_
  50.5 2.9 %shard_map.63 = (f32[2,4,48,384]{3,2,1,0:T(8,128)S(1)}, bf16[128,384]{1,0:T(8,128)(2,1)S(1)}, bf16[128,384]{1,0:T(8,128)(2,1)S(1)}, f32[2,4,48,384]{3,2,1,0:T(8,128)S(1)}, bf16[2,4,48,384]{3,2,1,0:T(8,128)(2,1)S(1)}) custom-call(s32[4]{0:T(128)S(1)} %pad_add_fusion.refs_0_.scalars, bf16[576,384]{1,0:T(8,128)(2,1)S(1)} %get-tuple-element.24.x, ...), custom_call_target="tpu_custom_call" | custom-call | tf_op jit(solution)/shard_map/pallas_call | solution.py:374
  53.4 0.4 collective-permute-start.18
  53.9 0.2 copy-done.8
  54.0 0.0 copy-done.10
  54.1 1.0 %collective-permute-done.18 = bf16[2,4,48,384]{3,2,1,0:T(8,128)(2,1)S(1)} collective-permute-done((bf16[2,4,48,384]{3,2,1,0:T(8,128)(2,1)S(1)}, bf16[2,4,48,384]{3,2,1,0:T(8,128)(2,1)S(1)}, u32[]{:S(2)}, u32[]{:S(2)}) %collective-permute-start.18) | collective-permute-done | bytes 294944 | tf_op jit(solution)/shard_map/ppermute | solution.py:388
  55.1 0.1 convert_add_fusion
  55.2 6.7 %collective-permute-start.21 = (bf16[4,48,384]{2,1,0:T(8,128)(2,1)S(1)}, bf16[4,48,384]{2,1,0:T(8,128)(2,1)S(1)}, u32[]{:S(2)}, u32[]{:S(2)}) collective-permute-start(bf16[4,48,384]{2,1,0:T(8,128)(2,1)S(1)} %pad_maximum_fusion.2), channel_id=1, source_target_pairs={{0,6},{1,7},{2,4},{3,5},{4,2},{5,3},{6,0},{7,1},{8,14},{9,15},{10,... | collective-permute-start | bytes 442376 | tf_op jit(solution)/shard_map/ppermute | solution.py:388
  61.9 0.2 collective-permute-start.20
  62.2 0.8 %collective-permute-start.19 = (bf16[4,48,384]{2,1,0:T(8,128)(2,1)S(1)}, bf16[4,48,384]{2,1,0:T(8,128)(2,1)S(1)}, u32[]{:S(2)}, u32[]{:S(2)}) collective-permute-start(bf16[4,48,384]{2,1,0:T(8,128)(2,1)S(1)} %pad_maximum_fusion), channel_id=1, source_target_pairs={{0,2},{1,3},{2,0},{3,1},{4,6},{5,7},{6,4},{7,5},{8,10},{9,11},{10,... | collective-permute-start | bytes 442376 | tf_op jit(solution)/shard_map/ppermute | solution.py:388
  63.0 3.4 %collective-permute-done.21 = bf16[4,48,384]{2,1,0:T(8,128)(2,1)S(1)} collective-permute-done((bf16[4,48,384]{2,1,0:T(8,128)(2,1)S(1)}, bf16[4,48,384]{2,1,0:T(8,128)(2,1)S(1)}, u32[]{:S(2)}, u32[]{:S(2)}) %collective-permute-start.21) | collective-permute-done | bytes 147488 | tf_op jit(solution)/shard_map/ppermute | solution.py:388
  66.4 2.8 %collective-permute-done.20 = bf16[4,48,384]{2,1,0:T(8,128)(2,1)S(1)} collective-permute-done((bf16[4,48,384]{2,1,0:T(8,128)(2,1)S(1)}, bf16[4,48,384]{2,1,0:T(8,128)(2,1)S(1)}, u32[]{:S(2)}, u32[]{:S(2)}) %collective-permute-start.20) | collective-permute-done | bytes 147488 | tf_op jit(solution)/shard_map/ppermute | solution.py:388
  69.2 0.6 collective-permute-done.19
  69.8 0.1 fusion.1
  69.9 0.0 copy-start.7
  70.0 0.3 collective-permute-start.24
  70.3 1.2 %collective-permute-start.23 = (bf16[48,384]{1,0:T(8,128)(2,1)S(1)}, bf16[48,384]{1,0:T(8,128)(2,1)S(1)}, u32[]{:S(2)}, u32[]{:S(2)}) collective-permute-start(bf16[48,384]{1,0:T(8,128)(2,1)S(1)} %get-tuple-element.50), channel_id=1, source_target_pairs={{0,16},{1,17},{2,18},{3,19},{4,20},{5,21},{6,22},{7,23},{8,24},{9,... | collective-permute-start | bytes 110600 | tf_op jit(solution)/shard_map/ppermute | solution.py:388
  71.5 3.0 %collective-permute-start.22 = (bf16[48,384]{1,0:T(8,128)(2,1)S(1)}, bf16[48,384]{1,0:T(8,128)(2,1)S(1)}, u32[]{:S(2)}, u32[]{:S(2)}) collective-permute-start(bf16[48,384]{1,0:T(8,128)(2,1)S(1)} %get-tuple-element.48), channel_id=1, source_target_pairs={{0,8},{1,9},{2,10},{3,11},{4,12},{5,13},{6,14},{7,15},{8,0},{9,1},... | collective-permute-start | bytes 110600 | tf_op jit(solution)/shard_map/ppermute | solution.py:388
  74.4 1.2 %shard_map.64 = bf16[8,16,384]{2,1,0:T(8,128)(2,1)} custom-call(bf16[8,16,384]{2,1,0:T(8,128)(2,1)S(1)} %copy-done, bf16[384,384]{1,0:T(8,128)(2,1)S(1)} %get-tuple-element.21.wq, bf16[384,384]{1,0:T(8,128)(2,1)S(1)} %get-tuple-element.22.wk, bf16[384,384]{1,0:T(8,128)(2,1)S(1)} %copy-done.3, bf16[128,384]{1,0:T(8,128)(2,1)S(1)} %copy-done.7, ...), custom_call_target="tpu_custom_call" | custom-call | tf_op jit(solution)/shard_map/pallas_call | solution.py:374
  75.6 0.2 collective-permute-done.24
  75.8 0.0 collective-permute-done.23
  75.8 0.6 collective-permute-done.22
  76.4 0.6 reshape.28
  (43 shorter events, 0.4 us)
Async XLA Ops:
  1.4 5.7 %collective-permute-start = (bf16[1,48,384]{2,1,0:T(8,128)(2,1)S(1)}, bf16[1,48,384]{2,1,0:T(8,128)(2,1)S(1)}, u32[]{:S(2)}, u32[]{:S(2)}) collective-permute-start(bf16[1,48,384]{2,1,0:T(8,128)(2,1)S(1)} %reshape.27), channel_id=1, source_target_pairs={{0,8},{1,9},{2,10},{3,11},{4,12},{5,13},{6,14},{7,15},{8,0},{9,1},... | collective-permute-start | bytes 110600 | tf_op jit(solution)/shard_map/ppermute | solution.py:388
  4.5 5.5 %collective-permute-start.1 = (bf16[1,48,384]{2,1,0:T(8,128)(2,1)S(1)}, bf16[1,48,384]{2,1,0:T(8,128)(2,1)S(1)}, u32[]{:S(2)}, u32[]{:S(2)}) collective-permute-start(bf16[1,48,384]{2,1,0:T(8,128)(2,1)S(1)} %reshape.27), channel_id=1, source_target_pairs={{0,16},{1,17},{2,18},{3,19},{4,20},{5,21},{6,22},{7,23},{8,24},{9,... | collective-permute-start | bytes 110600 | tf_op jit(solution)/shard_map/ppermute | solution.py:388
  7.1 5.8 %collective-permute-start.2 = (bf16[1,48,384]{2,1,0:T(8,128)(2,1)S(1)}, bf16[1,48,384]{2,1,0:T(8,128)(2,1)S(1)}, u32[]{:S(2)}, u32[]{:S(2)}) collective-permute-start(bf16[1,48,384]{2,1,0:T(8,128)(2,1)S(1)} %reshape.27), channel_id=1, source_target_pairs={{0,24},{1,25},{2,26},{3,27},{4,28},{5,29},{6,30},{7,31},{8,16},{9,... | collective-permute-start | bytes 110600 | tf_op jit(solution)/shard_map/ppermute | solution.py:388
  12.9 6.4 %collective-permute-start.3 = (bf16[4,48,384]{2,1,0:T(8,128)(2,1)S(1)}, bf16[4,48,384]{2,1,0:T(8,128)(2,1)S(1)}, u32[]{:S(2)}, u32[]{:S(2)}) collective-permute-start(bf16[4,48,384]{2,1,0:T(8,128)(2,1)S(1)} %get-tuple-element.57), channel_id=1, source_target_pairs={{0,2},{1,3},{2,0},{3,1},{4,6},{5,7},{6,4},{7,5},{8,10},{9,11},{10,... | collective-permute-start | bytes 442376 | tf_op jit(solution)/shard_map/ppermute | solution.py:388
  14.5 7.7 %collective-permute-start.4 = (bf16[4,48,384]{2,1,0:T(8,128)(2,1)S(1)}, bf16[4,48,384]{2,1,0:T(8,128)(2,1)S(1)}, u32[]{:S(2)}, u32[]{:S(2)}) collective-permute-start(bf16[4,48,384]{2,1,0:T(8,128)(2,1)S(1)} %get-tuple-element.57), channel_id=1, source_target_pairs={{0,4},{1,5},{2,6},{3,7},{4,0},{5,1},{6,2},{7,3},{8,12},{9,13},{10,... | collective-permute-start | bytes 442376 | tf_op jit(solution)/shard_map/ppermute | solution.py:388
  16.0 6.2 %collective-permute-start.5 = (bf16[4,48,384]{2,1,0:T(8,128)(2,1)S(1)}, bf16[4,48,384]{2,1,0:T(8,128)(2,1)S(1)}, u32[]{:S(2)}, u32[]{:S(2)}) collective-permute-start(bf16[4,48,384]{2,1,0:T(8,128)(2,1)S(1)} %get-tuple-element.57), channel_id=1, source_target_pairs={{0,6},{1,7},{2,4},{3,5},{4,2},{5,3},{6,0},{7,1},{8,14},{9,15},{10,... | collective-permute-start | bytes 442376 | tf_op jit(solution)/shard_map/ppermute | solution.py:388
  22.2 8.2 %collective-permute-start.6 = (bf16[16,48,384]{2,1,0:T(8,128)(2,1)S(1)}, bf16[16,48,384]{2,1,0:T(8,128)(2,1)S(1)}, u32[]{:S(2)}, u32[]{:S(2)}) collective-permute-start(bf16[16,48,384]{2,1,0:T(8,128)(2,1)S(1)} %constant_dynamic-update-slice_fusion.4.refs_1_), channel_id=1, source_target_pairs={{0,1},{1,0},{2,3},{3,2},{4,5},{5,4},{6,7},{7,6},{8,9},{9,8},{10,11... | collective-permute-start | bytes 1769480 | tf_op jit(solution)/shard_map/ppermute | solution.py:388
  23.4 7.0 %copy-start.1 = (bf16[2,72,384]{2,1,0:T(8,128)(2,1)}, bf16[2,72,384]{2,1,0:T(8,128)(2,1)S(1)}, u32[]{:S(2)}) copy-start(bf16[2,72,384]{2,1,0:T(8,128)(2,1)S(1)} %shard_map.59.refs_5_) | copy-start | bytes 331780
  23.4 7.0 %copy-start = (bf16[8,16,384]{2,1,0:T(8,128)(2,1)S(1)}, bf16[8,16,384]{2,1,0:T(8,128)(2,1)}, u32[]{:S(2)}) copy-start(bf16[8,16,384]{2,1,0:T(8,128)(2,1)} %tokens.3) | copy-start | bytes 294916
  23.4 5.5 %collective-permute-start.7 = (bf16[2,72,384]{2,1,0:T(8,128)(2,1)S(1)}, bf16[2,72,384]{2,1,0:T(8,128)(2,1)S(1)}, u32[]{:S(2)}, u32[]{:S(2)}) collective-permute-start(bf16[2,72,384]{2,1,0:T(8,128)(2,1)S(1)} %shard_map.59.refs_5_), channel_id=1, source_target_pairs={{0,2},{2,0},{4,6},{6,4},{8,10},{10,8},{12,14},{14,12},{16,18},{18,... | collective-permute-start | bytes 331784 | tf_op jit(solution)/shard_map/ppermute | solution.py:400
  23.9 5.1 %collective-permute-start.8 = (bf16[2,72,384]{2,1,0:T(8,128)(2,1)S(1)}, bf16[2,72,384]{2,1,0:T(8,128)(2,1)S(1)}, u32[]{:S(2)}, u32[]{:S(2)}) collective-permute-start(bf16[2,72,384]{2,1,0:T(8,128)(2,1)S(1)} %shard_map.59.refs_5_), channel_id=1, source_target_pairs={{2,4},{4,2},{6,8},{8,6},{10,12},{12,10},{14,16},{16,14},{18,20},{2... | collective-permute-start | bytes 331784 | tf_op jit(solution)/shard_map/ppermute | solution.py:401
  24.5 5.0 %collective-permute-start.9 = (bf16[2,72,384]{2,1,0:T(8,128)(2,1)S(1)}, bf16[2,72,384]{2,1,0:T(8,128)(2,1)S(1)}, u32[]{:S(2)}, u32[]{:S(2)}) collective-permute-start(bf16[2,72,384]{2,1,0:T(8,128)(2,1)S(1)} %shard_map.59.refs_5_), channel_id=1, source_target_pairs={{0,1},{1,0},{2,3},{3,2},{4,5},{5,4},{6,7},{7,6},{8,9},{9,8},{10,11... | collective-permute-start | bytes 331784 | tf_op jit(solution)/shard_map/ppermute | solution.py:407
  29.0 1.5 %copy-start.12 = (bf16[2,72,384]{2,1,0:T(8,128)(2,1)}, bf16[2,72,384]{2,1,0:T(8,128)(2,1)S(1)}, u32[]{:S(2)}) copy-start(bf16[2,72,384]{2,1,0:T(8,128)(2,1)S(1)} %collective-permute-done.7.refs_6_) | copy-start | bytes 331780
  29.0 1.3 %collective-permute-start.10 = (bf16[2,72,384]{2,1,0:T(8,128)(2,1)S(1)}, bf16[2,72,384]{2,1,0:T(8,128)(2,1)S(1)}, u32[]{:S(2)}, u32[]{:S(2)}) collective-permute-start(bf16[2,72,384]{2,1,0:T(8,128)(2,1)S(1)} %collective-permute-done.7.refs_6_), channel_id=1, source_target_pairs={{0,1},{1,0},{2,3},{3,2},{4,5},{5,4},{6,7},{7,6},{8,9},{9,8},{10,11... | collective-permute-start | bytes 331784 | tf_op jit(solution)/shard_map/ppermute | solution.py:407
  29.0 1.5 %copy-start.13 = (bf16[2,72,384]{2,1,0:T(8,128)(2,1)}, bf16[2,72,384]{2,1,0:T(8,128)(2,1)S(1)}, u32[]{:S(2)}) copy-start(bf16[2,72,384]{2,1,0:T(8,128)(2,1)S(1)} %collective-permute-done.8.refs_7_) | copy-start | bytes 331780
  29.0 1.5 %collective-permute-start.11 = (bf16[2,72,384]{2,1,0:T(8,128)(2,1)S(1)}, bf16[2,72,384]{2,1,0:T(8,128)(2,1)S(1)}, u32[]{:S(2)}, u32[]{:S(2)}) collective-permute-start(bf16[2,72,384]{2,1,0:T(8,128)(2,1)S(1)} %collective-permute-done.8.refs_7_), channel_id=1, source_target_pairs={{0,1},{1,0},{2,3},{3,2},{4,5},{5,4},{6,7},{7,6},{8,9},{9,8},{10,11... | collective-permute-start | bytes 331784 | tf_op jit(solution)/shard_map/ppermute | solution.py:407
  29.6 0.6 copy-start.4
  30.5 0.9 %copy-start.5 = (bf16[2,72,384]{2,1,0:T(8,128)(2,1)S(1)}, bf16[2,72,384]{2,1,0:T(8,128)(2,1)}, u32[]{:S(2)}) copy-start(bf16[2,72,384]{2,1,0:T(8,128)(2,1)} %copy-done.4) | copy-start | bytes 331780
  36.8 3.2 %copy-start.2 = (bf16[384,384]{1,0:T(8,128)(2,1)}, bf16[384,384]{1,0:T(8,128)(2,1)S(1)}, u32[]{:S(2)}) copy-start(bf16[384,384]{1,0:T(8,128)(2,1)S(1)} %get-tuple-element.23.wv) | copy-start | bytes 884740
  39.9 0.6 copy-start.6
  40.6 9.9 %collective-permute-start.17 = (bf16[2,4,48,384]{3,2,1,0:T(8,128)(2,1)}, bf16[2,4,48,384]{3,2,1,0:T(8,128)(2,1)S(1)}, u32[]{:S(2)}, u32[]{:S(2)}) collective-permute-start(bf16[2,4,48,384]{3,2,1,0:T(8,128)(2,1)} %get-tuple-element.34), channel_id=1, source_target_pairs={{0,1},{1,0},{2,3},{3,2},{4,5},{5,4},{6,7},{7,6},{8,9},{9,8},{10,11... | collective-permute-start | bytes 884744 | tf_op jit(solution)/shard_map/ppermute | solution.py:388
  40.9 7.9 %collective-permute-start.12 = (bf16[2,72,384]{2,1,0:T(8,128)(2,1)}, bf16[2,72,384]{2,1,0:T(8,128)(2,1)S(1)}, u32[]{:S(2)}, u32[]{:S(2)}) collective-permute-start(bf16[2,72,384]{2,1,0:T(8,128)(2,1)} %get-tuple-element.32), channel_id=1, source_target_pairs={{0,2},{2,0},{4,6},{6,4},{8,10},{10,8},{12,14},{14,12},{16,18},{18,... | collective-permute-start | bytes 331784 | tf_op jit(solution)/shard_map/ppermute | solution.py:400
  45.1 3.8 %collective-permute-start.13 = (bf16[2,72,384]{2,1,0:T(8,128)(2,1)}, bf16[2,72,384]{2,1,0:T(8,128)(2,1)S(1)}, u32[]{:S(2)}, u32[]{:S(2)}) collective-permute-start(bf16[2,72,384]{2,1,0:T(8,128)(2,1)} %get-tuple-element.32), channel_id=1, source_target_pairs={{2,4},{4,2},{6,8},{8,6},{10,12},{12,10},{14,16},{16,14},{18,20},{2... | collective-permute-start | bytes 331784 | tf_op jit(solution)/shard_map/ppermute | solution.py:401
  45.7 4.3 %collective-permute-start.14 = (bf16[2,72,384]{2,1,0:T(8,128)(2,1)}, bf16[2,72,384]{2,1,0:T(8,128)(2,1)S(1)}, u32[]{:S(2)}, u32[]{:S(2)}) collective-permute-start(bf16[2,72,384]{2,1,0:T(8,128)(2,1)} %get-tuple-element.32), channel_id=1, source_target_pairs={{0,1},{1,0},{2,3},{3,2},{4,5},{5,4},{6,7},{7,6},{8,9},{9,8},{10,11... | collective-permute-start | bytes 331784 | tf_op jit(solution)/shard_map/ppermute | solution.py:407
  48.9 1.5 %collective-permute-start.15 = (bf16[2,72,384]{2,1,0:T(8,128)(2,1)S(1)}, bf16[2,72,384]{2,1,0:T(8,128)(2,1)}, u32[]{:S(2)}, u32[]{:S(2)}) collective-permute-start(bf16[2,72,384]{2,1,0:T(8,128)(2,1)S(1)} %collective-permute-done.12.refs_0_), channel_id=1, source_target_pairs={{0,1},{1,0},{2,3},{3,2},{4,5},{5,4},{6,7},{7,6},{8,9},{9,8},{10,11... | collective-permute-start | bytes 331784 | tf_op jit(solution)/shard_map/ppermute | solution.py:407
  48.9 1.6 %collective-permute-start.16 = (bf16[2,72,384]{2,1,0:T(8,128)(2,1)S(1)}, bf16[2,72,384]{2,1,0:T(8,128)(2,1)}, u32[]{:S(2)}, u32[]{:S(2)}) collective-permute-start(bf16[2,72,384]{2,1,0:T(8,128)(2,1)S(1)} %collective-permute-done.13.refs_1_), channel_id=1, source_target_pairs={{0,1},{1,0},{2,3},{3,2},{4,5},{5,4},{6,7},{7,6},{8,9},{9,8},{10,11... | collective-permute-start | bytes 331784 | tf_op jit(solution)/shard_map/ppermute | solution.py:407
  53.4 0.6 copy-start.8
  53.4 0.7 copy-start.10
  53.4 1.6 %collective-permute-start.18 = (bf16[2,4,48,384]{3,2,1,0:T(8,128)(2,1)S(1)}, bf16[2,4,48,384]{3,2,1,0:T(8,128)(2,1)S(1)}, u32[]{:S(2)}, u32[]{:S(2)}) collective-permute-start(bf16[2,4,48,384]{3,2,1,0:T(8,128)(2,1)S(1)} %get-tuple-element.39), channel_id=1, source_target_pairs={{0,1},{1,0},{2,3},{3,2},{4,5},{5,4},{6,7},{7,6},{8,9},{9,8},{10,11... | collective-permute-start | bytes 884744 | tf_op jit(solution)/shard_map/ppermute | solution.py:388
  55.2 11.2 %collective-permute-start.21 = (bf16[4,48,384]{2,1,0:T(8,128)(2,1)S(1)}, bf16[4,48,384]{2,1,0:T(8,128)(2,1)S(1)}, u32[]{:S(2)}, u32[]{:S(2)}) collective-permute-start(bf16[4,48,384]{2,1,0:T(8,128)(2,1)S(1)} %pad_maximum_fusion.2), channel_id=1, source_target_pairs={{0,6},{1,7},{2,4},{3,5},{4,2},{5,3},{6,0},{7,1},{8,14},{9,15},{10,... | collective-permute-start | bytes 442376 | tf_op jit(solution)/shard_map/ppermute | solution.py:388
  61.9 7.3 %collective-permute-start.20 = (bf16[4,48,384]{2,1,0:T(8,128)(2,1)S(1)}, bf16[4,48,384]{2,1,0:T(8,128)(2,1)S(1)}, u32[]{:S(2)}, u32[]{:S(2)}) collective-permute-start(bf16[4,48,384]{2,1,0:T(8,128)(2,1)S(1)} %pad_maximum_fusion.1), channel_id=1, source_target_pairs={{0,4},{1,5},{2,6},{3,7},{4,0},{5,1},{6,2},{7,3},{8,12},{9,13},{10,... | collective-permute-start | bytes 442376 | tf_op jit(solution)/shard_map/ppermute | solution.py:388
  62.2 7.7 %collective-permute-start.19 = (bf16[4,48,384]{2,1,0:T(8,128)(2,1)S(1)}, bf16[4,48,384]{2,1,0:T(8,128)(2,1)S(1)}, u32[]{:S(2)}, u32[]{:S(2)}) collective-permute-start(bf16[4,48,384]{2,1,0:T(8,128)(2,1)S(1)} %pad_maximum_fusion), channel_id=1, source_target_pairs={{0,2},{1,3},{2,0},{3,1},{4,6},{5,7},{6,4},{7,5},{8,10},{9,11},{10,... | collective-permute-start | bytes 442376 | tf_op jit(solution)/shard_map/ppermute | solution.py:388
  69.8 4.6 %copy-start.3 = (bf16[384,384]{1,0:T(8,128)(2,1)S(1)}, bf16[384,384]{1,0:T(8,128)(2,1)}, u32[]{:S(2)}) copy-start(bf16[384,384]{1,0:T(8,128)(2,1)} %copy-done.2) | copy-start | bytes 884740
  69.8 4.6 %copy-start.11 = (bf16[128,384]{1,0:T(8,128)(2,1)S(1)}, bf16[128,384]{1,0:T(8,128)(2,1)}, u32[]{:S(2)}) copy-start(bf16[128,384]{1,0:T(8,128)(2,1)} %copy-done.10) | copy-start | bytes 294916
  69.9 4.5 %copy-start.7 = (bf16[128,384]{1,0:T(8,128)(2,1)S(1)}, bf16[128,384]{1,0:T(8,128)(2,1)}, u32[]{:S(2)}) copy-start(bf16[128,384]{1,0:T(8,128)(2,1)} %copy-done.6) | copy-start | bytes 294916
  69.9 4.5 %copy-start.9 = (bf16[128,384]{1,0:T(8,128)(2,1)S(1)}, bf16[128,384]{1,0:T(8,128)(2,1)}, u32[]{:S(2)}) copy-start(bf16[128,384]{1,0:T(8,128)(2,1)} %copy-done.8) | copy-start | bytes 294916
  70.0 5.8 %collective-permute-start.24 = (bf16[48,384]{1,0:T(8,128)(2,1)S(1)}, bf16[48,384]{1,0:T(8,128)(2,1)S(1)}, u32[]{:S(2)}, u32[]{:S(2)}) collective-permute-start(bf16[48,384]{1,0:T(8,128)(2,1)S(1)} %get-tuple-element.49), channel_id=1, source_target_pairs={{0,24},{1,25},{2,26},{3,27},{4,28},{5,29},{6,30},{7,31},{8,16},{9,... | collective-permute-start | bytes 110600 | tf_op jit(solution)/shard_map/ppermute | solution.py:388
  70.3 5.5 %collective-permute-start.23 = (bf16[48,384]{1,0:T(8,128)(2,1)S(1)}, bf16[48,384]{1,0:T(8,128)(2,1)S(1)}, u32[]{:S(2)}, u32[]{:S(2)}) collective-permute-start(bf16[48,384]{1,0:T(8,128)(2,1)S(1)} %get-tuple-element.50), channel_id=1, source_target_pairs={{0,16},{1,17},{2,18},{3,19},{4,20},{5,21},{6,22},{7,23},{8,24},{9,... | collective-permute-start | bytes 110600 | tf_op jit(solution)/shard_map/ppermute | solution.py:388
  71.5 4.9 %collective-permute-start.22 = (bf16[48,384]{1,0:T(8,128)(2,1)S(1)}, bf16[48,384]{1,0:T(8,128)(2,1)S(1)}, u32[]{:S(2)}, u32[]{:S(2)}) collective-permute-start(bf16[48,384]{1,0:T(8,128)(2,1)S(1)} %get-tuple-element.48), channel_id=1, source_target_pairs={{0,8},{1,9},{2,10},{3,11},{4,12},{5,13},{6,14},{7,15},{8,0},{9,1},... | collective-permute-start | bytes 110600 | tf_op jit(solution)/shard_map/ppermute | solution.py:388

commit v3 on v2

--- a/solution.py
+++ b/solution.py
@@ -102,8 +102,10 @@
     return tiles
 
 
-def packed_tiles(v, n_tiles):
-    return [v.at[pl.ds(n_tiles * PER + t * BLK, BLK)] for t in range(2)]
+def own_parts(mine):
+    own = 2 * PER
+    packs = [mine.at[pl.ds(3 * own + t * BLK, BLK)] for t in range(2)]
+    return [mine.at[pl.ds(n * own, own)] for n in range(3)] + [packs]
 
 
 def pack_stats(stats, width):
@@ -134,9 +136,27 @@
         low_out[t, PER:BLK, :] = jnp.full((BLK - PER, width), tissue[0, t].astype(F32)).astype(BF16)
 
 
-def forward_kernel(groups, place, *refs):
-    scalars, first_half, second_half, tokens, teacher, *refs = refs
+def pile_kernel(*refs):
+    *parts, out = refs
+    for n, part in enumerate(parts):
+        out[n] = part[0]
+
+
+def assemble(index, spots, parts, out):
+    z_count, per_block, _ = parts[0].shape
+    for p, part in enumerate(parts):
+        inner = jnp.bitwise_xor(index % (2 * spots), p)
+        at = pl.multiple_of(inner * per_block, 16)
+        for z in range(z_count):
+            matrix = jnp.bitwise_xor(index // (2 * spots), z)
+            out[matrix, pl.ds(at, per_block), :] = part[z]
+
+
+def forward_kernel(groups, spots, *refs):
+    scalars, tokens, teacher, *refs = refs
     n_strips = 3 * (groups - 1)
+    n_parts = max(1, 2 * spots)
+    parts, refs = refs[:n_parts], refs[n_parts:]
     (
         wq_out,
         wk_out,
@@ -148,47 +168,43 @@
         gout_out,
         near_out,
         stats_out,
+        mine_out,
         pack_out,
-        wo_scr,
+        w_scr,
+        teacher_scr,
+        sem,
     ) = refs[n_strips:]
-    odd, base = scalars[0], scalars[1]
+    copy = pltpu.make_async_copy(teacher, teacher_scr, sem)
+    copy.start()
+    odd, index = scalars[0], scalars[3]
     own_strip, *others = refs[:n_strips]
     tiles = strip_tiles([[own_strip.at[0], own_strip.at[1]], *others], odd)
-    half, per_block, model = first_half.shape
-    n_blocks = 2 * half
+    model = tokens.shape[2]
     width = model // HEADS
     own = 2 * PER
-    per_matrix = n_blocks // 4
-    swapped = (base >= half).astype(jnp.int32)
-    for way in (0, 1):
-
-        @pl.when(swapped == way)
-        def _():
-            for d in range(n_blocks):
-                whole = (wq_out, wk_out, wv_out, wo_scr)[d // per_matrix]
-                at = d % per_matrix * per_block
-                source = first_half if (place[d] >= half) == way else second_half
-                whole[at : at + per_block, :] = source[jnp.bitwise_xor(base, place[d]) % half]
-
+    if spots > 0:
+        assemble(index, spots, parts, w_scr)
+    else:
+        w_scr[...] = parts[0][...]
+    for n, whole in enumerate((wq_out, wk_out, wv_out)):
+        whole[...] = w_scr[n]
     n_tiles = 3 * groups
     flag_rows = []
     ones = pair_ones(width)
-    key_parts, value_parts = [], []
-    for first, last in ((0, groups), (groups, n_tiles)):
-        for n in range(first, last):
-            x_out[n * PER : (n + 1) * PER, :] = tiles[n][0:PER, :]
-            flag_rows.append(tiles[n][PER:BLK, :].astype(F32)[0:1, 0:PER])
-        x = x_out[first * PER : last * PER, :]
-        if first == 0:
-            q_normal, _ = head_normalise(dot(x[0:own], wq_out[...]), ones, width)
-            queries = q_normal.astype(BF16)
-        k_normal, _ = head_normalise(dot(x, wk_out[...]), ones, width)
-        key_parts.append(k_normal.astype(BF16))
-        value_parts.append(dot(x, wv_out[...]).astype(BF16))
-    keys = jnp.concatenate(key_parts, axis=0)
-    values = jnp.concatenate(value_parts, axis=0)
+    for n, tile in enumerate(tiles):
+        x_out[n * PER : (n + 1) * PER, :] = tile[0:PER, :]
+        flag_rows.append(tile[PER:BLK, :].astype(F32)[0:1, 0:PER])
+    x = x_out[...]
+    k_normal, _ = head_normalise(dot(x, wk_out[...]), ones, width)
+    keys = k_normal.astype(BF16)
+    values = dot(x, wv_out[...]).astype(BF16)
+    q_normal, _ = head_normalise(dot(x[0:own], wq_out[...]), ones, width)
+    queries = q_normal.astype(BF16)
     k_out[...] = keys
-    v_out[0 : n_tiles * PER, :] = values
+    v_out[...] = values
+    *own_outs, packs = own_parts(mine_out)
+    for own_out, source in zip(own_outs, (x_out, k_out, v_out), strict=True):
+        own_out[...] = source[0:own, :]
 
     flags = jnp.concatenate(flag_rows, axis=1)
     left, right = near_rows(groups, odd, n_tiles)
@@ -203,7 +219,7 @@
     mixed_parts, inverses = [], []
     for p in range(HEADS // 2):
         lanes = slice(2 * width * p, 2 * width * (p + 1))
-        scores = dot_nt(split_heads(queries[:, lanes], width), keys[:, lanes]) * scale
+        scores = dot_nt(split_heads(queries[:, lanes] * scale, width), keys[:, lanes])
         raised = jnp.exp(scores).reshape(4, PER, n_tiles * PER) * near
         total = jnp.sum(raised, axis=-1, keepdims=True) + rest
         inverse = (1.0 / total).astype(BF16).astype(F32)
@@ -213,9 +229,10 @@
         inverses += [inverse[0:own], inverse[own:]]
     mixed = (jnp.concatenate(mixed_parts, axis=1) * query_mask).astype(BF16)
     mixed_out[...] = mixed
-    w_o = wo_scr[...]
+    w_o = w_scr[3]
+    copy.wait()
     residual = tiles_of(tokens[...].astype(F32)) + dot(mixed, w_o)
-    grad_out = query_mask * (residual - tiles_of(teacher[...].astype(F32)))
+    grad_out = query_mask * (residual - tiles_of(teacher_scr[...].astype(F32)))
     gout_out[...] = grad_out
     grad_mixed = dot_nt(grad_out.astype(BF16), w_o).astype(BF16)
     delta = head_sums(grad_mixed.astype(F32) * mixed.astype(F32), ones)
@@ -231,7 +248,7 @@
         here = slice(t * PER, (t + 1) * PER)
         pack_out[t, 0:PER, :] = grad_mixed[here]
         pack_out[t, PER:BLK, :] = pack_stats(stats[:, here], model)
-        packed_tiles(v_out, n_tiles)[t][...] = pack_out[t]
+        packs[t][...] = pack_out[t]
 
 
 def store_terms(fast, odd, grads, outs):
@@ -246,7 +263,7 @@
             even_part = grad[2 * b * rows : (2 * b + 1) * rows]
             odd_part = grad[(2 * b + 1) * rows : (2 * b + 2) * rows]
             is_odd = odd == 1
-            keep[m, b] = jnp.where(is_odd, odd_part, even_part)
+            keep[m, b] = jnp.where(is_odd, odd_part, even_part).astype(BF16)
             send[m, b] = jnp.where(is_odd, even_part, odd_part).astype(BF16)
 
 
@@ -257,57 +274,57 @@
     q_out[...] = q_normal.astype(BF16)
 
 
-def query_kernel(fast, scalars, wq, x, k, v, mixed, gout, near_in, stats_in, *outs):
+def query_kernel(fast, scalars, wq, k, v, mixed, gout, near_in, stats_in, mine, *outs):
     core = scalars[2]
     model = wq.shape[0]
     width = model // HEADS
-    own = 2 * PER
     n_tiles = near_in.shape[1] // PER
     ones = pair_ones(width)
-    q_normal, q_factor = head_normalise(dot(x[0:own, :], wq[...]), ones, width)
+    x_own, _, _, packs = own_parts(mine)
+    q_normal, q_factor = head_normalise(dot(x_own[...], wq[...]), ones, width)
     queries = q_normal.astype(BF16)
     near = jnp.stack([near_in[0:1], near_in[1:2]] * 2)
     stats = stats_in[...].astype(BF16).astype(F32)
     gq_out, *outs = outs
-    grad_mixed = jnp.concatenate([pack[0:PER, :] for pack in packed_tiles(v, n_tiles)], axis=0)
+    grad_mixed = jnp.concatenate([pack[0:PER, :] for pack in packs], axis=0)
     scale = 1.0 / math.sqrt(width)
     parts = []
     for p in range(HEADS // 2):
         lanes = slice(2 * width * p, 2 * width * (p + 1))
-        keys, values = k[:, lanes], v[0 : n_tiles * PER, lanes]
-        scores = dot_nt(split_heads(queries[:, lanes], width), keys) * scale
+        keys, values = k[:, lanes], v[:, lanes]
+        scores = dot_nt(split_heads(queries[:, lanes] * scale, width), keys)
         inverse = jnp.concatenate([stats[:, 2 * p : 2 * p + 1], stats[:, 2 * p + 1 : 2 * p + 2]], axis=0)
         at = HEADS + 2 * p
         delta = jnp.concatenate([stats[:, at : at + 1], stats[:, at + 1 : at + 2]], axis=0)
         full = jnp.exp(scores).reshape(4, PER, n_tiles * PER) * near
         full = full.reshape(4 * PER, n_tiles * PER) * inverse
         grad_attn = dot_nt(split_heads(grad_mixed[:, lanes], width), values)
-        grad_scores = (full * (grad_attn - delta) * scale).astype(BF16)
-        parts.append(join_heads(dot(grad_scores, keys), width))
+        grad_scores = (full * (grad_attn - delta)).astype(BF16)
+        parts.append(join_heads(dot(grad_scores, keys), width) * scale)
     grad_qn = jnp.concatenate(parts, axis=1)
     grad_query = head_back(q_normal, q_factor, grad_qn, ones, width).astype(BF16)
     gq_out[...] = grad_query
-    grad_wq = dot_tn(x[0:own, :], grad_query)
+    grad_wq = dot_tn(x_own[...], grad_query)
     grad_wo = dot_tn(mixed[...], gout[...].astype(BF16))
     store_terms(fast, core, [grad_wq, grad_wo], outs)
 
 
-def key_kernel(groups, fast, scalars, x, k, v, wk, q, *refs):
+def key_kernel(groups, fast, scalars, mine, wk, q, *refs):
     n_strips = 3 * (groups - 1)
     sources, refs = refs[: n_strips - 1], refs[n_strips - 1 :]
     if fast:
         kept, arrived, sums_out, *refs = refs
-        sums_out[...] = kept[...] + arrived[...].astype(F32)
+        sums_out[...] = (kept[...].astype(F32) + arrived[...].astype(F32)).astype(BF16)
     *refs, g_scr = refs
     gk_out, gv_out, *outs = refs
     odd, core = scalars[0], scalars[2]
-    model = x.shape[1]
+    model = q.shape[1]
     width = model // HEADS
-    own = 2 * PER
     n_tiles = 3 * groups
     ones = pair_ones(width)
-    tiles = strip_tiles([packed_tiles(v, n_tiles), *sources], odd)
-    x_own = x[0:own, :]
+    x, k, v, packs = own_parts(mine)
+    tiles = strip_tiles([packs, *sources], odd)
+    x_own = x[...]
     k_normal, k_factor = head_normalise(dot(x_own, wk[...]), ones, width)
     stat_parts = []
     for n, tile in enumerate(tiles):
@@ -322,17 +339,17 @@
     for p in range(HEADS // 2):
         lanes = slice(2 * width * p, 2 * width * (p + 1))
         queries, grads = q[:, lanes], g_scr[:, lanes]
-        scores = dot_nt(split_heads(k[0:own, lanes], width), queries) * scale
+        scores = dot_nt(split_heads(k[:, lanes] * scale, width), queries)
         inv = [stats[2 * p + j : 2 * p + j + 1] for j in range(2)]
         rows = jnp.stack([inv[j] * near[t] for j in range(2) for t in range(2)])
         at = HEADS + 2 * p
         delta = jnp.stack([stats[at + j : at + j + 1] for j in range(2) for _ in range(2)])
         full = jnp.exp(scores).reshape(4, PER, n_tiles * PER) * rows
-        grad_attn = dot_nt(split_heads(v[0:own, lanes], width), grads)
+        grad_attn = dot_nt(split_heads(v[:, lanes], width), grads)
         grad_attn = grad_attn.reshape(4, PER, n_tiles * PER) - delta
-        grad_scores = (full * grad_attn * scale).reshape(4 * PER, n_tiles * PER).astype(BF16)
+        grad_scores = (full * grad_attn).reshape(4 * PER, n_tiles * PER).astype(BF16)
         low = full.reshape(4 * PER, n_tiles * PER).astype(BF16)
-        key_parts.append(join_heads(dot(grad_scores, queries), width))
+        key_parts.append(join_heads(dot(grad_scores, queries), width) * scale)
         value_parts.append(join_heads(dot(low, grads), width))
     grad_kn = jnp.concatenate(key_parts, axis=1)
     grad_key = head_back(k_normal, k_factor, grad_kn, ones, width).astype(BF16)
@@ -364,6 +381,10 @@
 
 def in_hbm(value):
     return pltpu.with_memory_space_constraint(value, pltpu.HBM)
+
+
+def in_vmem(value):
+    return pltpu.with_memory_space_constraint(value, pltpu.VMEM)
 
 
 def call(kernel, in_specs, shapes, args, scratch=(), kept=0, held=()):
@@ -425,14 +446,7 @@
     n_keys = 3 * groups * PER
     n_strips = 3 * (groups - 1)
 
-    def spot(d):
-        return (d % 2) * (count // 2) + (d // 2 % spots) * 4 + d // per_matrix
-
-    if fast:
-        place, base = [spot(d) for d in range(count)], spot(index)
-    else:
-        place, base = list(range(4)), jnp.int32(0)
-    scalars = jnp.stack([odd, base, index % 2, index]).astype(jnp.int32)
+    scalars = jnp.stack([odd, index % 2, index % 2, index]).astype(jnp.int32)
 
     (low,) = call(
         prep_kernel,
@@ -444,52 +458,60 @@
         ),
     )
     if fast:
-        wblk = weights.reshape(1, per_block, model)
-        parts = [swap(wblk, count, per_matrix * step) for step in range(1, 4)]
-        wblk = jnp.concatenate([wblk] + parts, axis=0)
-        parts = [swap(wblk, count, 2 * step) for step in range(1, spots)]
+        block = weights.reshape(1, per_block, model)
+        parts = [block] + [swap(block, count, per_matrix * step) for step in range(1, 4)]
+        (pile,) = call(
+            pile_kernel,
+            [VMEM] * 4,
+            [((4, per_block, model), BF16)],
+            parts,
+            kept=1,
+            held=range(1, 4),
+        )
+        piles = [pile] + [swap(pile, count, 2 * step) for step in range(1, spots)]
         strips = beside(low)
-        wblk = jnp.concatenate([wblk] + parts, axis=0)
-        halves = [wblk, swap(wblk, count, 1)]
+        wide = [swap(pile, count, 1) for pile in piles]
+        parts = [in_vmem(part) for pair in zip(piles, wide, strict=True) for part in pair]
         strips = strips + across(strips)
     else:
         strips = beside(low)
         strips = strips + across(strips)
-        wblk = lax.all_gather(weights, AXES, axis=0, tiled=True).reshape(4, model, model)
-        halves = [wblk[0:2], wblk[2:4]]
-
-    wq, wk, wv, x, k, v, mixed, gout, near, stats, pack = call(
-        functools.partial(forward_kernel, groups, place),
-        [SMEM] + [VMEM] * (4 + n_strips),
+        whole = lax.all_gather(weights, AXES, axis=0, tiled=True)
+        parts = [whole.reshape(4, model, model)]
+
+    wq, wk, wv, x, k, v, mixed, gout, near, stats, mine, pack = call(
+        functools.partial(forward_kernel, groups, spots if fast else 0),
+        [SMEM, VMEM, ANY] + [VMEM] * (len(parts) + n_strips),
         [((model, model), BF16)] * 3
-        + [((n_keys, model), BF16)] * 2
-        + [((n_keys + 2 * BLK, model), BF16)]
+        + [((n_keys, model), BF16)] * 3
         + [
             ((own, model), BF16),
             ((own, model), F32),
             ((2, n_keys), F32),
             ((own, own), F32),
+            ((3 * own + 2 * BLK, model), BF16),
             ((2, BLK, model), BF16),
         ],
-        (scalars, *halves, tokens, in_hbm(teacher), *map(in_hbm, strips[:3]), *strips[3:]),
-        scratch=[pltpu.VMEM((model, model), BF16)],
-        kept=10,
+        (scalars, tokens, in_hbm(teacher), *parts, *map(in_vmem, strips)),
+        scratch=[
+            pltpu.VMEM((4, model, model), BF16),
+            pltpu.VMEM(teacher.shape, BF16),
+            pltpu.SemaphoreType.DMA,
+        ],
+        kept=11,
     )
     packs = beside(pack)
     packs = packs + across(packs)
 
     if fast:
-        term_shapes = [
-            ((2, spots, per_block, model), F32),
-            ((2, spots, per_block, model), BF16),
-        ]
+        term_shapes = [((2, spots, per_block, model), BF16)] * 2
     else:
         term_shapes = [((2, model, model), F32)]
     gq, *terms_qo = call(
         functools.partial(query_kernel, fast),
         [SMEM] + [VMEM] * 8,
         [((own, model), BF16)] + term_shapes,
-        (scalars, wq, x, k, v, mixed, gout, near, stats),
+        (scalars, wq, k, v, mixed, gout, near, stats, mine),
         kept=2,
         held=range(1, 9),
     )
@@ -501,12 +523,12 @@
         more = [terms_qo[0], swap(terms_qo[1], count, 1)]
     results = call(
         functools.partial(key_kernel, groups, fast),
-        [SMEM] + [VMEM] * (4 + n_strips + len(more)),
+        [SMEM] + [VMEM] * (2 + n_strips + len(more)),
         term_shapes[: len(more) // 2] + [((own, model), BF16)] * 2 + term_shapes,
-        (scalars, x, k, v, wk, q, *packs[1:], *more),
+        (scalars, mine, wk, q, *map(in_vmem, packs[1:]), *more),
         scratch=[pltpu.VMEM((n_keys, model), BF16)],
         kept=5 if fast else 2,
-        held=[*range(1, 6)] + ([5 + n_strips] if fast else []),
+        held=[1, 2, 3] + ([3 + n_strips] if fast else []),
     )
     sums_qo, results = (results[0], results[1:]) if fast else (None, results)
     gk, gv, *terms_kv = results
@@ -530,16 +552,17 @@
     def pick(values, at, axis):
         return lax.dynamic_index_in_dim(values, at, axis, keepdims=False)
 
-    sums_kv = terms_kv[0] + swap(terms_kv[1], count, 1).astype(F32)
+    arrived = swap(terms_kv[1], count, 1).astype(F32)
+    sums_kv = (terms_kv[0].astype(F32) + arrived).astype(BF16)
 
     def all_four(at):
         qo, kv = pick(sums_qo, at, 1), pick(sums_kv, at, 1)
         return jnp.concatenate([qo[0:1], kv, qo[1:2]], axis=0)
 
     arrived = [
-        swap(all_four(here ^ step).astype(BF16), count, 2 * step) for step in range(1, spots)
+        swap(all_four(here ^ step), count, 2 * step) for step in range(1, spots)
     ]
-    pieces = all_four(here)
+    pieces = all_four(here).astype(F32)
     for part in arrived:
         pieces = pieces + part.astype(F32)
     arrived = [

time: 77.3 us -> 68.3 us (0.88)
  local copies, waits for them, and re-layouts: 4.13 us -> 0.78 us
  waiting for transfers between devices: 27.7 us -> 24.9 us
  Pallas kernels: 14.4 us -> 12.3 us
    ppermute x2, waiting for transfers between devices: 7.14 us -> 4.23 us  [beside(): near = lax.ppermute(strip, 'rows', side_pairs(rows, 0))]
    unnamed x33 -> x4, local copies, waits for them, and re-layouts: 2.51 us -> 0.01 us
    pallas_call x6 -> x7, Pallas kernels: 14.4 us -> 12.3 us  [call(): pl.pallas_call(kernel, out_shape=[pltpu.VMEM(s, t) if n < kept else jax.S...]
    ppermute x2, starting transfers between devices: 4.56 us -> 3.09 us  [beside(): near = lax.ppermute(strip, 'rows', side_pairs(rows, 0))]
    ppermute x15 -> x18, starting transfers between devices: 22.3 us -> 22.9 us  [swap(): return lax.ppermute(value, AXES, [(i, i ^ mask) for i in range(count)])]
    ppermute x15 -> x18, waiting for transfers between devices: 19.9 us -> 19.5 us  [swap(): return lax.ppermute(value, AXES, [(i, i ^ mask) for i in range(count)])]
  transfers between devices with their start and end apart: 25 -> 28, of which waited for: 16 -> 14; matrix products, arithmetic and copies ran while one was open for 0% -> 0% of each run, Pallas kernels for 4% -> 3%
where the time goes in v3:
time: 68.3 us; the launch traced here: 68.1 us
  starting transfers between devices  29 us (42%)
  waiting for transfers between devices  24.9 us (36%)
  Pallas kernels  12.3 us (18%)
  between operations  0.84 us (1%)
  local copies, waits for them, and re-layouts  0.78 us (1%)
    ppermute x18, starting transfers between devices, swap(): return lax.ppermute(value, AXES, [(i, i ^ mask) for i in range(count)])  22.9 us
    ppermute x18, waiting for transfers between devices, swap(): return lax.ppermute(value, AXES, [(i, i ^ mask) for i in range(count)])  19.5 us
    pallas_call x7, Pallas kernels, call(): pl.pallas_call(kernel, out_shape=[pltpu.VMEM(s, t) if n < kept else jax.S...  12.3 us
    ppermute x2, waiting for transfers between devices, beside(): near = lax.ppermute(strip, 'rows', side_pairs(rows, 0))  4.23 us
    ppermute x2, starting transfers between devices, beside(): near = lax.ppermute(strip, 'rows', side_pairs(rows, 0))  3.09 us
    ppermute x6, starting transfers between devices, across(): lax.ppermute(strip, 'cols', side_pairs(cols, n))  1.69 us
  transfers between devices with their start and end apart: 28, of which 14 were waited for; matrix products, arithmetic and copies ran while one was open for 0% of the time, Pallas kernels for 3%

profile of v3, /device:TPU:0, one launch (start us, length us, event | category | flops | bytes accessed | tf_op | source)
XLA Modules:
  0.0 68.1 jit_solution(4724100270860708457)
XLA Ops:
  0.6 1.1 %shard_map.60.refs_11_ = bf16[2,72,384]{2,1,0:T(8,128)(2,1)S(1)} custom-call(s32[1,2]{1,0:T(1,128)} %tissue.1, bf16[8,16,384]{2,1,0:T(8,128)(2,1)} %tokens.3), custom_call_target="tpu_custom_call" | custom-call | tf_op jit(solution)/shard_map/pallas_call | solution.py:395
  1.7 3.0 %collective-permute-start.10 = (bf16[2,72,384]{2,1,0:T(8,128)(2,1)S(1)}, bf16[2,72,384]{2,1,0:T(8,128)(2,1)S(1)}, u32[]{:S(2)}, u32[]{:S(2)}) collective-permute-start(bf16[2,72,384]{2,1,0:T(8,128)(2,1)S(1)} %shard_map.60.refs_11_), channel_id=1, source_target_pairs={{0,2},{2,0},{4,6},{6,4},{8,10},{10,8},{12,14},{14,12},{16,18},{18,... | collective-permute-start | bytes 331784 | tf_op jit(solution)/shard_map/ppermute | solution.py:421
  4.8 0.7 collective-permute-start.11
  5.5 4.3 %collective-permute-start = (bf16[1,48,384]{2,1,0:T(8,128)(2,1)S(1)}, bf16[1,48,384]{2,1,0:T(8,128)(2,1)S(1)}, u32[]{:S(2)}, u32[]{:S(2)}) collective-permute-start(bf16[1,48,384]{2,1,0:T(8,128)(2,1)S(1)} %reshape.21.refs_0_), channel_id=1, source_target_pairs={{0,8},{1,9},{2,10},{3,11},{4,12},{5,13},{6,14},{7,15},{8,0},{9,1},... | collective-permute-start | bytes 110600 | tf_op jit(solution)/shard_map/ppermute | solution.py:409
  9.7 2.6 %collective-permute-start.1 = (bf16[1,48,384]{2,1,0:T(8,128)(2,1)S(1)}, bf16[1,48,384]{2,1,0:T(8,128)(2,1)S(1)}, u32[]{:S(2)}, u32[]{:S(2)}) collective-permute-start(bf16[1,48,384]{2,1,0:T(8,128)(2,1)S(1)} %reshape.21.refs_0_), channel_id=1, source_target_pairs={{0,16},{1,17},{2,18},{3,19},{4,20},{5,21},{6,22},{7,23},{8,24},{9,... | collective-permute-start | bytes 110600 | tf_op jit(solution)/shard_map/ppermute | solution.py:409
  12.3 0.0 collective-permute-start.2
  12.3 1.0 %collective-permute-done.refs_1_ = bf16[1,48,384]{2,1,0:T(8,128)(2,1)S(1)} collective-permute-done((bf16[1,48,384]{2,1,0:T(8,128)(2,1)S(1)}, bf16[1,48,384]{2,1,0:T(8,128)(2,1)S(1)}, u32[]{:S(2)}, u32[]{:S(2)}) %collective-permute-start) | collective-permute-done | bytes 36896 | tf_op jit(solution)/shard_map/ppermute | solution.py:409
  13.3 1.6 %collective-permute-done.1.refs_2_ = bf16[1,48,384]{2,1,0:T(8,128)(2,1)S(1)} collective-permute-done((bf16[1,48,384]{2,1,0:T(8,128)(2,1)S(1)}, bf16[1,48,384]{2,1,0:T(8,128)(2,1)S(1)}, u32[]{:S(2)}, u32[]{:S(2)}) %collective-permute-start.1) | collective-permute-done | bytes 36896 | tf_op jit(solution)/shard_map/ppermute | solution.py:409
  14.9 3.2 %collective-permute-done.2.refs_3_ = bf16[1,48,384]{2,1,0:T(8,128)(2,1)S(1)} collective-permute-done((bf16[1,48,384]{2,1,0:T(8,128)(2,1)S(1)}, bf16[1,48,384]{2,1,0:T(8,128)(2,1)S(1)}, u32[]{:S(2)}, u32[]{:S(2)}) %collective-permute-start.2) | collective-permute-done | bytes 36896 | tf_op jit(solution)/shard_map/ppermute | solution.py:409
  18.1 1.7 %collective-permute-start.4 = (bf16[4,48,384]{2,1,0:T(8,128)(2,1)S(1)}, bf16[4,48,384]{2,1,0:T(8,128)(2,1)S(1)}, u32[]{:S(2)}, u32[]{:S(2)}) collective-permute-start(bf16[4,48,384]{2,1,0:T(8,128)(2,1)S(1)} %shard_map.59.refs_3_), channel_id=1, source_target_pairs={{0,2},{1,3},{2,0},{3,1},{4,6},{5,7},{6,4},{7,5},{8,10},{9,11},{10,... | collective-permute-start | bytes 442376 | tf_op jit(solution)/shard_map/ppermute | solution.py:409
  19.8 0.0 collective-permute-start.6
  19.8 1.9 %collective-permute-start.8 = (bf16[4,48,384]{2,1,0:T(8,128)(2,1)S(1)}, bf16[4,48,384]{2,1,0:T(8,128)(2,1)S(1)}, u32[]{:S(2)}, u32[]{:S(2)}) collective-permute-start(bf16[4,48,384]{2,1,0:T(8,128)(2,1)S(1)} %shard_map.59.refs_3_), channel_id=1, source_target_pairs={{0,6},{1,7},{2,4},{3,5},{4,2},{5,3},{6,0},{7,1},{8,14},{9,15},{10,... | collective-permute-start | bytes 442376 | tf_op jit(solution)/shard_map/ppermute | solution.py:409
  21.7 0.0 collective-permute-done.10.refs_12_
  21.7 0.0 collective-permute-start.3
  21.7 0.0 collective-permute-done.11.refs_13_
  21.7 0.5 collective-permute-start.12
  22.2 1.8 %collective-permute-done.4.refs_5_ = bf16[4,48,384]{2,1,0:T(8,128)(2,1)S(1)} collective-permute-done((bf16[4,48,384]{2,1,0:T(8,128)(2,1)S(1)}, bf16[4,48,384]{2,1,0:T(8,128)(2,1)S(1)}, u32[]{:S(2)}, u32[]{:S(2)}) %collective-permute-start.4) | collective-permute-done | bytes 147488 | tf_op jit(solution)/shard_map/ppermute | solution.py:409
  24.0 0.0 collective-permute-start.5
  24.0 2.5 %collective-permute-done.6.refs_7_ = bf16[4,48,384]{2,1,0:T(8,128)(2,1)S(1)} collective-permute-done((bf16[4,48,384]{2,1,0:T(8,128)(2,1)S(1)}, bf16[4,48,384]{2,1,0:T(8,128)(2,1)S(1)}, u32[]{:S(2)}, u32[]{:S(2)}) %collective-permute-start.6) | collective-permute-done | bytes 147488 | tf_op jit(solution)/shard_map/ppermute | solution.py:409
  26.5 0.0 collective-permute-start.7
  26.5 0.0 collective-permute-done.8.refs_9_
  26.5 0.5 collective-permute-start.9
  27.0 0.0 collective-permute-done.12.refs_14_
  27.0 0.1 collective-permute-start.13
  27.1 0.0 collective-permute-done.3.refs_4_
  27.1 0.4 collective-permute-start.14
  27.5 0.1 pad_add_fusion.refs_0_.scalars
  27.6 0.7 %collective-permute-done.13.refs_15_ = bf16[2,72,384]{2,1,0:T(8,128)(2,1)S(1)} collective-permute-done((bf16[2,72,384]{2,1,0:T(8,128)(2,1)S(1)}, bf16[2,72,384]{2,1,0:T(8,128)(2,1)S(1)}, u32[]{:S(2)}, u32[]{:S(2)}) %collective-permute-start.13) | collective-permute-done | bytes 110624 | tf_op jit(solution)/shard_map/ppermute | solution.py:428
  28.3 0.2 collective-permute-done.14.refs_16_
  28.5 0.0 collective-permute-done.5.refs_6_
  28.5 0.0 collective-permute-done.7.refs_8_
  28.5 0.0 collective-permute-done.9.refs_10_
  28.5 4.4 %shard_map.61 = (bf16[384,384]{1,0:T(8,128)(2,1)S(1)}, bf16[384,384]{1,0:T(8,128)(2,1)S(1)}, bf16[384,384]{1,0:T(8,128)(2,1)S(1)}, bf16[576,384]{1,0:T(8,128)(2,...) custom-call(s32[4]{0:T(128)S(1)} %pad_add_fusion.refs_0_.scalars, ...), custom_call_target="tpu_custom_call" | custom-call | tf_op jit(solution)/shard_map/pallas_call | solution.py:395
  32.9 2.4 %shard_map.62 = (bf16[128,384]{1,0:T(8,128)(2,1)S(1)}, bf16[2,4,48,384]{3,2,1,0:T(8,128)(2,1)S(1)}, bf16[2,4,48,384]{3,2,1,0:T(8,128)(2,1)S(1)}) custom-call(s32[4]{0:T(128)S(1)} %pad_add_fusion.refs_0_.scalars, bf16[384,384]{1,0:T(8,128)(2,1)S(1)} %get-tuple-element.22.wq, bf16[576,384]{1,0:T(8,128)(2,1)S(1)} %get-tuple-element.25.k, ...), custom_call_target="tpu_custom_call" | custom-call | tf_op jit(solution)/shard_map/pallas_call | solution.py:395
  35.3 0.4 collective-permute-start.20
  35.8 0.1 collective-permute-start.15
  35.8 0.7 collective-permute-start.16
  36.5 0.2 collective-permute-start.17
  36.6 4.2 %collective-permute-done.15.refs_0_ = bf16[2,72,384]{2,1,0:T(8,128)(2,1)S(1)} collective-permute-done((bf16[2,72,384]{2,1,0:T(8,128)(2,1)S(1)}, bf16[2,72,384]{2,1,0:T(8,128)(2,1)S(1)}, u32[]{:S(2)}, u32[]{:S(2)}) %collective-permute-start.15) | collective-permute-done | bytes 110624 | tf_op jit(solution)/shard_map/ppermute | solution.py:421
  40.9 0.0 collective-permute-start.18
  40.9 0.0 collective-permute-done.16.refs_1_
  40.9 0.5 collective-permute-start.19
  41.4 0.7 shard_map.63.q
  42.1 0.0 collective-permute-done.17.refs_2_
  42.1 0.1 collective-permute-done.18.refs_3_
  42.2 0.2 collective-permute-done.19.refs_4_
  42.3 2.5 %shard_map.64 = (bf16[2,4,48,384]{3,2,1,0:T(8,128)(2,1)S(1)}, bf16[128,384]{1,0:T(8,128)(2,1)S(1)}, bf16[128,384]{1,0:T(8,128)(2,1)S(1)}, bf16[2,4,48,384]{3,2,1,0:T(8,128)(2,1)S(1)}, bf16[2,4,48,384]{3,2,1,0:T(8,128)(2,1)S(1)}) custom-call(s32[4]{0:T(128)S(1)} %pad_add_fusion.refs_0_.scalars, bf16[528,384]{1,0:T(8,128)(2,1)S(1)} %get-tuple-element.31.mine, ...), custom_call_target="tpu_custom_call" | custom-call | tf_op jit(solution)/shard_map/pallas_call | solution.py:395
  44.9 0.4 collective-permute-start.21
  45.3 1.2 %collective-permute-done.21 = bf16[2,4,48,384]{3,2,1,0:T(8,128)(2,1)S(1)} collective-permute-done((bf16[2,4,48,384]{3,2,1,0:T(8,128)(2,1)S(1)}, bf16[2,4,48,384]{3,2,1,0:T(8,128)(2,1)S(1)}, u32[]{:S(2)}, u32[]{:S(2)}) %collective-permute-start.21) | collective-permute-done | bytes 294944 | tf_op jit(solution)/shard_map/ppermute | solution.py:409
  46.5 0.1 add_convert_fusion
  46.7 4.4 %collective-permute-start.22 = (bf16[4,48,384]{2,1,0:T(8,128)(2,1)S(1)}, bf16[4,48,384]{2,1,0:T(8,128)(2,1)S(1)}, u32[]{:S(2)}, u32[]{:S(2)}) collective-permute-start(bf16[4,48,384]{2,1,0:T(8,128)(2,1)S(1)} %pad_maximum_fusion), channel_id=1, source_target_pairs={{0,2},{1,3},{2,0},{3,1},{4,6},{5,7},{6,4},{7,5},{8,10},{9,11},{10,... | collective-permute-start | bytes 442376 | tf_op jit(solution)/shard_map/ppermute | solution.py:409
  51.2 2.2 %collective-permute-start.23 = (bf16[4,48,384]{2,1,0:T(8,128)(2,1)S(1)}, bf16[4,48,384]{2,1,0:T(8,128)(2,1)S(1)}, u32[]{:S(2)}, u32[]{:S(2)}) collective-permute-start(bf16[4,48,384]{2,1,0:T(8,128)(2,1)S(1)} %pad_maximum_fusion.1), channel_id=1, source_target_pairs={{0,4},{1,5},{2,6},{3,7},{4,0},{5,1},{6,2},{7,3},{8,12},{9,13},{10,... | collective-permute-start | bytes 442376 | tf_op jit(solution)/shard_map/ppermute | solution.py:409
  53.3 0.1 collective-permute-start.24
  53.5 1.9 %collective-permute-done.22 = bf16[4,48,384]{2,1,0:T(8,128)(2,1)S(1)} collective-permute-done((bf16[4,48,384]{2,1,0:T(8,128)(2,1)S(1)}, bf16[4,48,384]{2,1,0:T(8,128)(2,1)S(1)}, u32[]{:S(2)}, u32[]{:S(2)}) %collective-permute-start.22) | collective-permute-done | bytes 147488 | tf_op jit(solution)/shard_map/ppermute | solution.py:409
  55.4 5.0 %collective-permute-done.23 = bf16[4,48,384]{2,1,0:T(8,128)(2,1)S(1)} collective-permute-done((bf16[4,48,384]{2,1,0:T(8,128)(2,1)S(1)}, bf16[4,48,384]{2,1,0:T(8,128)(2,1)S(1)}, u32[]{:S(2)}, u32[]{:S(2)}) %collective-permute-start.23) | collective-permute-done | bytes 147488 | tf_op jit(solution)/shard_map/ppermute | solution.py:409
  60.4 0.1 convert_add_fusion
  60.5 0.1 collective-permute-start.25
  60.6 1.1 %collective-permute-start.26 = (bf16[48,384]{1,0:T(8,128)(2,1)S(1)}, bf16[48,384]{1,0:T(8,128)(2,1)S(1)}, u32[]{:S(2)}, u32[]{:S(2)}) collective-permute-start(bf16[48,384]{1,0:T(8,128)(2,1)S(1)} %get-tuple-element.44), channel_id=1, source_target_pairs={{0,16},{1,17},{2,18},{3,19},{4,20},{5,21},{6,22},{7,23},{8,24},{9,... | collective-permute-start | bytes 110600 | tf_op jit(solution)/shard_map/ppermute | solution.py:409
  61.7 3.2 %collective-permute-start.27 = (bf16[48,384]{1,0:T(8,128)(2,1)S(1)}, bf16[48,384]{1,0:T(8,128)(2,1)S(1)}, u32[]{:S(2)}, u32[]{:S(2)}) collective-permute-start(bf16[48,384]{1,0:T(8,128)(2,1)S(1)} %get-tuple-element.43), channel_id=1, source_target_pairs={{0,24},{1,25},{2,26},{3,27},{4,28},{5,29},{6,30},{7,31},{8,16},{9,... | collective-permute-start | bytes 110600 | tf_op jit(solution)/shard_map/ppermute | solution.py:409
  64.9 1.2 %shard_map.65 = bf16[8,16,384]{2,1,0:T(8,128)(2,1)} custom-call(bf16[8,16,384]{2,1,0:T(8,128)(2,1)S(1)} %copy-done, bf16[384,384]{1,0:T(8,128)(2,1)S(1)} %get-tuple-element.22.wq, bf16[384,384]{1,0:T(8,128)(2,1)S(1)} %get-tuple-element.23.wk, bf16[384,384]{1,0:T(8,128)(2,1)S(1)} %get-tuple-element.24.wv, bf16[128,384]{1,0:T(8,128)(2,1)S(1)} %get-tuple-element.32.gq, ...), custom_call_target="tpu_custom_call" | custom-call | tf_op jit(solution)/shard_map/pallas_call | solution.py:395
  66.1 0.0 collective-permute-done.25
  66.1 0.0 collective-permute-done.26
  66.1 1.3 %collective-permute-done.27 = bf16[48,384]{1,0:T(8,128)(2,1)S(1)} collective-permute-done((bf16[48,384]{1,0:T(8,128)(2,1)S(1)}, bf16[48,384]{1,0:T(8,128)(2,1)S(1)}, u32[]{:S(2)}, u32[]{:S(2)}) %collective-permute-start.27) | collective-permute-done | bytes 36896 | tf_op jit(solution)/shard_map/ppermute | solution.py:409
  67.5 0.6 reshape.22
  (15 shorter events, 0.3 us)
Async XLA Ops:
  0.6 4.8 %copy-start.1 = (bf16[18432]{0:T(1024)(128)(2,1)S(1)}, bf16[18432]{0:T(1024)(128)(2,1)}, u32[]{:S(2)}) copy-start(bf16[18432]{0:T(1024)(128)(2,1)} %param.7) | copy-start | bytes 110596
  1.7 19.9 %collective-permute-start.10 = (bf16[2,72,384]{2,1,0:T(8,128)(2,1)S(1)}, bf16[2,72,384]{2,1,0:T(8,128)(2,1)S(1)}, u32[]{:S(2)}, u32[]{:S(2)}) collective-permute-start(bf16[2,72,384]{2,1,0:T(8,128)(2,1)S(1)} %shard_map.60.refs_11_), channel_id=1, source_target_pairs={{0,2},{2,0},{4,6},{6,4},{8,10},{10,8},{12,14},{14,12},{16,18},{18,... | collective-permute-start | bytes 331784 | tf_op jit(solution)/shard_map/ppermute | solution.py:421
  4.8 16.9 %collective-permute-start.11 = (bf16[2,72,384]{2,1,0:T(8,128)(2,1)S(1)}, bf16[2,72,384]{2,1,0:T(8,128)(2,1)S(1)}, u32[]{:S(2)}, u32[]{:S(2)}) collective-permute-start(bf16[2,72,384]{2,1,0:T(8,128)(2,1)S(1)} %shard_map.60.refs_11_), channel_id=1, source_target_pairs={{2,4},{4,2},{6,8},{8,6},{10,12},{12,10},{14,16},{16,14},{18,20},{2... | collective-permute-start | bytes 331784 | tf_op jit(solution)/shard_map/ppermute | solution.py:422
  5.5 7.8 %collective-permute-start = (bf16[1,48,384]{2,1,0:T(8,128)(2,1)S(1)}, bf16[1,48,384]{2,1,0:T(8,128)(2,1)S(1)}, u32[]{:S(2)}, u32[]{:S(2)}) collective-permute-start(bf16[1,48,384]{2,1,0:T(8,128)(2,1)S(1)} %reshape.21.refs_0_), channel_id=1, source_target_pairs={{0,8},{1,9},{2,10},{3,11},{4,12},{5,13},{6,14},{7,15},{8,0},{9,1},... | collective-permute-start | bytes 110600 | tf_op jit(solution)/shard_map/ppermute | solution.py:409
  9.7 5.2 %collective-permute-start.1 = (bf16[1,48,384]{2,1,0:T(8,128)(2,1)S(1)}, bf16[1,48,384]{2,1,0:T(8,128)(2,1)S(1)}, u32[]{:S(2)}, u32[]{:S(2)}) collective-permute-start(bf16[1,48,384]{2,1,0:T(8,128)(2,1)S(1)} %reshape.21.refs_0_), channel_id=1, source_target_pairs={{0,16},{1,17},{2,18},{3,19},{4,20},{5,21},{6,22},{7,23},{8,24},{9,... | collective-permute-start | bytes 110600 | tf_op jit(solution)/shard_map/ppermute | solution.py:409
  12.3 5.8 %collective-permute-start.2 = (bf16[1,48,384]{2,1,0:T(8,128)(2,1)S(1)}, bf16[1,48,384]{2,1,0:T(8,128)(2,1)S(1)}, u32[]{:S(2)}, u32[]{:S(2)}) collective-permute-start(bf16[1,48,384]{2,1,0:T(8,128)(2,1)S(1)} %reshape.21.refs_0_), channel_id=1, source_target_pairs={{0,24},{1,25},{2,26},{3,27},{4,28},{5,29},{6,30},{7,31},{8,16},{9,... | collective-permute-start | bytes 110600 | tf_op jit(solution)/shard_map/ppermute | solution.py:409
  18.1 10.4 %copy-start = (bf16[8,16,384]{2,1,0:T(8,128)(2,1)S(1)}, bf16[8,16,384]{2,1,0:T(8,128)(2,1)}, u32[]{:S(2)}) copy-start(bf16[8,16,384]{2,1,0:T(8,128)(2,1)} %tokens.3) | copy-start | bytes 294916
  18.1 5.9 %collective-permute-start.4 = (bf16[4,48,384]{2,1,0:T(8,128)(2,1)S(1)}, bf16[4,48,384]{2,1,0:T(8,128)(2,1)S(1)}, u32[]{:S(2)}, u32[]{:S(2)}) collective-permute-start(bf16[4,48,384]{2,1,0:T(8,128)(2,1)S(1)} %shard_map.59.refs_3_), channel_id=1, source_target_pairs={{0,2},{1,3},{2,0},{3,1},{4,6},{5,7},{6,4},{7,5},{8,10},{9,11},{10,... | collective-permute-start | bytes 442376 | tf_op jit(solution)/shard_map/ppermute | solution.py:409
  19.8 6.7 %collective-permute-start.6 = (bf16[4,48,384]{2,1,0:T(8,128)(2,1)S(1)}, bf16[4,48,384]{2,1,0:T(8,128)(2,1)S(1)}, u32[]{:S(2)}, u32[]{:S(2)}) collective-permute-start(bf16[4,48,384]{2,1,0:T(8,128)(2,1)S(1)} %shard_map.59.refs_3_), channel_id=1, source_target_pairs={{0,4},{1,5},{2,6},{3,7},{4,0},{5,1},{6,2},{7,3},{8,12},{9,13},{10,... | collective-permute-start | bytes 442376 | tf_op jit(solution)/shard_map/ppermute | solution.py:409
  19.8 6.7 %collective-permute-start.8 = (bf16[4,48,384]{2,1,0:T(8,128)(2,1)S(1)}, bf16[4,48,384]{2,1,0:T(8,128)(2,1)S(1)}, u32[]{:S(2)}, u32[]{:S(2)}) collective-permute-start(bf16[4,48,384]{2,1,0:T(8,128)(2,1)S(1)} %shard_map.59.refs_3_), channel_id=1, source_target_pairs={{0,6},{1,7},{2,4},{3,5},{4,2},{5,3},{6,0},{7,1},{8,14},{9,15},{10,... | collective-permute-start | bytes 442376 | tf_op jit(solution)/shard_map/ppermute | solution.py:409
  21.7 5.4 %collective-permute-start.3 = (bf16[4,48,384]{2,1,0:T(8,128)(2,1)S(1)}, bf16[4,48,384]{2,1,0:T(8,128)(2,1)S(1)}, u32[]{:S(2)}, u32[]{:S(2)}) collective-permute-start(bf16[4,48,384]{2,1,0:T(8,128)(2,1)S(1)} %shard_map.59.refs_3_), channel_id=1, source_target_pairs={{0,1},{1,0},{2,3},{3,2},{4,5},{5,4},{6,7},{7,6},{8,9},{9,8},{10,11... | collective-permute-start | bytes 442376 | tf_op jit(solution)/shard_map/ppermute | solution.py:409
  21.7 5.3 %collective-permute-start.12 = (bf16[2,72,384]{2,1,0:T(8,128)(2,1)S(1)}, bf16[2,72,384]{2,1,0:T(8,128)(2,1)S(1)}, u32[]{:S(2)}, u32[]{:S(2)}) collective-permute-start(bf16[2,72,384]{2,1,0:T(8,128)(2,1)S(1)} %shard_map.60.refs_11_), channel_id=1, source_target_pairs={{0,1},{1,0},{2,3},{3,2},{4,5},{5,4},{6,7},{7,6},{8,9},{9,8},{10,11... | collective-permute-start | bytes 331784 | tf_op jit(solution)/shard_map/ppermute | solution.py:428
  24.0 4.5 %collective-permute-start.5 = (bf16[4,48,384]{2,1,0:T(8,128)(2,1)S(1)}, bf16[4,48,384]{2,1,0:T(8,128)(2,1)S(1)}, u32[]{:S(2)}, u32[]{:S(2)}) collective-permute-start(bf16[4,48,384]{2,1,0:T(8,128)(2,1)S(1)} %collective-permute-done.4.refs_5_), channel_id=1, source_target_pairs={{0,1},{1,0},{2,3},{3,2},{4,5},{5,4},{6,7},{7,6},{8,9},{9,8},{10,11... | collective-permute-start | bytes 442376 | tf_op jit(solution)/shard_map/ppermute | solution.py:409
  26.5 2.0 %collective-permute-start.7 = (bf16[4,48,384]{2,1,0:T(8,128)(2,1)S(1)}, bf16[4,48,384]{2,1,0:T(8,128)(2,1)S(1)}, u32[]{:S(2)}, u32[]{:S(2)}) collective-permute-start(bf16[4,48,384]{2,1,0:T(8,128)(2,1)S(1)} %collective-permute-done.6.refs_7_), channel_id=1, source_target_pairs={{0,1},{1,0},{2,3},{3,2},{4,5},{5,4},{6,7},{7,6},{8,9},{9,8},{10,11... | collective-permute-start | bytes 442376 | tf_op jit(solution)/shard_map/ppermute | solution.py:409
  26.5 2.0 %collective-permute-start.9 = (bf16[4,48,384]{2,1,0:T(8,128)(2,1)S(1)}, bf16[4,48,384]{2,1,0:T(8,128)(2,1)S(1)}, u32[]{:S(2)}, u32[]{:S(2)}) collective-permute-start(bf16[4,48,384]{2,1,0:T(8,128)(2,1)S(1)} %collective-permute-done.8.refs_9_), channel_id=1, source_target_pairs={{0,1},{1,0},{2,3},{3,2},{4,5},{5,4},{6,7},{7,6},{8,9},{9,8},{10,11... | collective-permute-start | bytes 442376 | tf_op jit(solution)/shard_map/ppermute | solution.py:409
  27.0 1.3 %collective-permute-start.13 = (bf16[2,72,384]{2,1,0:T(8,128)(2,1)S(1)}, bf16[2,72,384]{2,1,0:T(8,128)(2,1)S(1)}, u32[]{:S(2)}, u32[]{:S(2)}) collective-permute-start(bf16[2,72,384]{2,1,0:T(8,128)(2,1)S(1)} %collective-permute-done.10.refs_12_), channel_id=1, source_target_pairs={{0,1},{1,0},{2,3},{3,2},{4,5},{5,4},{6,7},{7,6},{8,9},{9,8},{10,11... | collective-permute-start | bytes 331784 | tf_op jit(solution)/shard_map/ppermute | solution.py:428
  27.1 1.4 %collective-permute-start.14 = (bf16[2,72,384]{2,1,0:T(8,128)(2,1)S(1)}, bf16[2,72,384]{2,1,0:T(8,128)(2,1)S(1)}, u32[]{:S(2)}, u32[]{:S(2)}) collective-permute-start(bf16[2,72,384]{2,1,0:T(8,128)(2,1)S(1)} %collective-permute-done.11.refs_13_), channel_id=1, source_target_pairs={{0,1},{1,0},{2,3},{3,2},{4,5},{5,4},{6,7},{7,6},{8,9},{9,8},{10,11... | collective-permute-start | bytes 331784 | tf_op jit(solution)/shard_map/ppermute | solution.py:428
  35.3 7.0 %collective-permute-start.20 = (bf16[2,4,48,384]{3,2,1,0:T(8,128)(2,1)S(1)}, bf16[2,4,48,384]{3,2,1,0:T(8,128)(2,1)S(1)}, u32[]{:S(2)}, u32[]{:S(2)}) collective-permute-start(bf16[2,4,48,384]{3,2,1,0:T(8,128)(2,1)S(1)} %get-tuple-element.36), channel_id=1, source_target_pairs={{0,1},{1,0},{2,3},{3,2},{4,5},{5,4},{6,7},{7,6},{8,9},{9,8},{10,11... | collective-permute-start | bytes 884744 | tf_op jit(solution)/shard_map/ppermute | solution.py:409
  35.8 5.1 %collective-permute-start.15 = (bf16[2,72,384]{2,1,0:T(8,128)(2,1)S(1)}, bf16[2,72,384]{2,1,0:T(8,128)(2,1)S(1)}, u32[]{:S(2)}, u32[]{:S(2)}) collective-permute-start(bf16[2,72,384]{2,1,0:T(8,128)(2,1)S(1)} %get-tuple-element.34), channel_id=1, source_target_pairs={{0,2},{2,0},{4,6},{6,4},{8,10},{10,8},{12,14},{14,12},{16,18},{18,... | collective-permute-start | bytes 331784 | tf_op jit(solution)/shard_map/ppermute | solution.py:421
  35.8 5.1 %collective-permute-start.16 = (bf16[2,72,384]{2,1,0:T(8,128)(2,1)S(1)}, bf16[2,72,384]{2,1,0:T(8,128)(2,1)S(1)}, u32[]{:S(2)}, u32[]{:S(2)}) collective-permute-start(bf16[2,72,384]{2,1,0:T(8,128)(2,1)S(1)} %get-tuple-element.34), channel_id=1, source_target_pairs={{2,4},{4,2},{6,8},{8,6},{10,12},{12,10},{14,16},{16,14},{18,20},{2... | collective-permute-start | bytes 331784 | tf_op jit(solution)/shard_map/ppermute | solution.py:422
  36.5 5.6 %collective-permute-start.17 = (bf16[2,72,384]{2,1,0:T(8,128)(2,1)S(1)}, bf16[2,72,384]{2,1,0:T(8,128)(2,1)S(1)}, u32[]{:S(2)}, u32[]{:S(2)}) collective-permute-start(bf16[2,72,384]{2,1,0:T(8,128)(2,1)S(1)} %get-tuple-element.34), channel_id=1, source_target_pairs={{0,1},{1,0},{2,3},{3,2},{4,5},{5,4},{6,7},{7,6},{8,9},{9,8},{10,11... | collective-permute-start | bytes 331784 | tf_op jit(solution)/shard_map/ppermute | solution.py:428
  40.9 1.3 %collective-permute-start.18 = (bf16[2,72,384]{2,1,0:T(8,128)(2,1)S(1)}, bf16[2,72,384]{2,1,0:T(8,128)(2,1)S(1)}, u32[]{:S(2)}, u32[]{:S(2)}) collective-permute-start(bf16[2,72,384]{2,1,0:T(8,128)(2,1)S(1)} %collective-permute-done.15.refs_0_), channel_id=1, source_target_pairs={{0,1},{1,0},{2,3},{3,2},{4,5},{5,4},{6,7},{7,6},{8,9},{9,8},{10,11... | collective-permute-start | bytes 331784 | tf_op jit(solution)/shard_map/ppermute | solution.py:428
  40.9 1.5 %collective-permute-start.19 = (bf16[2,72,384]{2,1,0:T(8,128)(2,1)S(1)}, bf16[2,72,384]{2,1,0:T(8,128)(2,1)S(1)}, u32[]{:S(2)}, u32[]{:S(2)}) collective-permute-start(bf16[2,72,384]{2,1,0:T(8,128)(2,1)S(1)} %collective-permute-done.16.refs_1_), channel_id=1, source_target_pairs={{0,1},{1,0},{2,3},{3,2},{4,5},{5,4},{6,7},{7,6},{8,9},{9,8},{10,11... | collective-permute-start | bytes 331784 | tf_op jit(solution)/shard_map/ppermute | solution.py:428
  44.9 1.6 %collective-permute-start.21 = (bf16[2,4,48,384]{3,2,1,0:T(8,128)(2,1)S(1)}, bf16[2,4,48,384]{3,2,1,0:T(8,128)(2,1)S(1)}, u32[]{:S(2)}, u32[]{:S(2)}) collective-permute-start(bf16[2,4,48,384]{3,2,1,0:T(8,128)(2,1)S(1)} %get-tuple-element.41), channel_id=1, source_target_pairs={{0,1},{1,0},{2,3},{3,2},{4,5},{5,4},{6,7},{7,6},{8,9},{9,8},{10,11... | collective-permute-start | bytes 884744 | tf_op jit(solution)/shard_map/ppermute | solution.py:409
  46.7 8.7 %collective-permute-start.22 = (bf16[4,48,384]{2,1,0:T(8,128)(2,1)S(1)}, bf16[4,48,384]{2,1,0:T(8,128)(2,1)S(1)}, u32[]{:S(2)}, u32[]{:S(2)}) collective-permute-start(bf16[4,48,384]{2,1,0:T(8,128)(2,1)S(1)} %pad_maximum_fusion), channel_id=1, source_target_pairs={{0,2},{1,3},{2,0},{3,1},{4,6},{5,7},{6,4},{7,5},{8,10},{9,11},{10,... | collective-permute-start | bytes 442376 | tf_op jit(solution)/shard_map/ppermute | solution.py:409
  51.2 9.2 %collective-permute-start.23 = (bf16[4,48,384]{2,1,0:T(8,128)(2,1)S(1)}, bf16[4,48,384]{2,1,0:T(8,128)(2,1)S(1)}, u32[]{:S(2)}, u32[]{:S(2)}) collective-permute-start(bf16[4,48,384]{2,1,0:T(8,128)(2,1)S(1)} %pad_maximum_fusion.1), channel_id=1, source_target_pairs={{0,4},{1,5},{2,6},{3,7},{4,0},{5,1},{6,2},{7,3},{8,12},{9,13},{10,... | collective-permute-start | bytes 442376 | tf_op jit(solution)/shard_map/ppermute | solution.py:409
  53.3 7.0 %collective-permute-start.24 = (bf16[4,48,384]{2,1,0:T(8,128)(2,1)S(1)}, bf16[4,48,384]{2,1,0:T(8,128)(2,1)S(1)}, u32[]{:S(2)}, u32[]{:S(2)}) collective-permute-start(bf16[4,48,384]{2,1,0:T(8,128)(2,1)S(1)} %pad_maximum_fusion.2), channel_id=1, source_target_pairs={{0,6},{1,7},{2,4},{3,5},{4,2},{5,3},{6,0},{7,1},{8,14},{9,15},{10,... | collective-permute-start | bytes 442376 | tf_op jit(solution)/shard_map/ppermute | solution.py:409
  60.5 5.6 %collective-permute-start.25 = (bf16[48,384]{1,0:T(8,128)(2,1)S(1)}, bf16[48,384]{1,0:T(8,128)(2,1)S(1)}, u32[]{:S(2)}, u32[]{:S(2)}) collective-permute-start(bf16[48,384]{1,0:T(8,128)(2,1)S(1)} %get-tuple-element.42), channel_id=1, source_target_pairs={{0,8},{1,9},{2,10},{3,11},{4,12},{5,13},{6,14},{7,15},{8,0},{9,1},... | collective-permute-start | bytes 110600 | tf_op jit(solution)/shard_map/ppermute | solution.py:409
  60.6 5.5 %collective-permute-start.26 = (bf16[48,384]{1,0:T(8,128)(2,1)S(1)}, bf16[48,384]{1,0:T(8,128)(2,1)S(1)}, u32[]{:S(2)}, u32[]{:S(2)}) collective-permute-start(bf16[48,384]{1,0:T(8,128)(2,1)S(1)} %get-tuple-element.44), channel_id=1, source_target_pairs={{0,16},{1,17},{2,18},{3,19},{4,20},{5,21},{6,22},{7,23},{8,24},{9,... | collective-permute-start | bytes 110600 | tf_op jit(solution)/shard_map/ppermute | solution.py:409
  61.7 5.8 %collective-permute-start.27 = (bf16[48,384]{1,0:T(8,128)(2,1)S(1)}, bf16[48,384]{1,0:T(8,128)(2,1)S(1)}, u32[]{:S(2)}, u32[]{:S(2)}) collective-permute-start(bf16[48,384]{1,0:T(8,128)(2,1)S(1)} %get-tuple-element.43), channel_id=1, source_target_pairs={{0,24},{1,25},{2,26},{3,27},{4,28},{5,29},{6,30},{7,31},{8,16},{9,... | collective-permute-start | bytes 110600 | tf_op jit(solution)/shard_map/ppermute | solution.py:409

commit v4 on v3

--- a/solution.py
+++ b/solution.py
@@ -267,11 +267,16 @@
             send[m, b] = jnp.where(is_odd, even_part, odd_part).astype(BF16)
 
 
-def halo_query_kernel(wq, x, q_out):
+def halo_query_kernel(wq, x, wk, *refs):
+    q_out, kn_out, kf_out, *sums = refs[-4:] if len(refs) > 3 else refs
     model = x.shape[1]
     width = model // HEADS
-    q_normal, _ = head_normalise(dot(x[...], wq[...]), pair_ones(width), width)
+    ones = pair_ones(width)
+    q_normal, _ = head_normalise(dot(x[...], wq[...]), ones, width)
     q_out[...] = q_normal.astype(BF16)
+    kn_out[...], kf_out[...] = head_normalise(dot(x[0 : 2 * PER, :], wk[...]), ones, width)
+    for sums_out in sums:
+        sums_out[...] = (refs[0][...].astype(F32) + refs[1][...].astype(F32)).astype(BF16)
 
 
 def query_kernel(fast, scalars, wq, k, v, mixed, gout, near_in, stats_in, mine, *outs):
@@ -309,12 +314,9 @@
     store_terms(fast, core, [grad_wq, grad_wo], outs)
 
 
-def key_kernel(groups, fast, scalars, mine, wk, q, *refs):
+def key_kernel(groups, fast, scalars, mine, q, kn, kf, *refs):
     n_strips = 3 * (groups - 1)
     sources, refs = refs[: n_strips - 1], refs[n_strips - 1 :]
-    if fast:
-        kept, arrived, sums_out, *refs = refs
-        sums_out[...] = (kept[...].astype(F32) + arrived[...].astype(F32)).astype(BF16)
     *refs, g_scr = refs
     gk_out, gv_out, *outs = refs
     odd, core = scalars[0], scalars[2]
@@ -325,7 +327,6 @@
     x, k, v, packs = own_parts(mine)
     tiles = strip_tiles([packs, *sources], odd)
     x_own = x[...]
-    k_normal, k_factor = head_normalise(dot(x_own, wk[...]), ones, width)
     stat_parts = []
     for n, tile in enumerate(tiles):
         g_scr[n * PER : (n + 1) * PER, :] = tile[0:PER, :]
@@ -352,7 +353,7 @@
         key_parts.append(join_heads(dot(grad_scores, queries), width) * scale)
         value_parts.append(join_heads(dot(low, grads), width))
     grad_kn = jnp.concatenate(key_parts, axis=1)
-    grad_key = head_back(k_normal, k_factor, grad_kn, ones, width).astype(BF16)
+    grad_key = head_back(kn[...], kf[...], grad_kn, ones, width).astype(BF16)
     grad_value = jnp.concatenate(value_parts, axis=1).astype(BF16)
     gk_out[...] = grad_key
     gv_out[...] = grad_value
@@ -424,11 +425,11 @@
 
 def across(strips):
     cols = lax.axis_size("cols")
-    return [
-        lax.ppermute(strip, "cols", side_pairs(cols, n))
-        for n in range(1 if cols == 2 else 2)
-        for strip in strips
-    ]
+    sides = []
+    for n in range(1 if cols == 2 else 2):
+        for strip in strips:
+            sides.append(lax.ppermute(strip, "cols", side_pairs(cols, n)))
+    return sides
 
 
 def layer(tokens, teacher, tissue, weights):
@@ -470,7 +471,9 @@
         )
         piles = [pile] + [swap(pile, count, 2 * step) for step in range(1, spots)]
         strips = beside(low)
-        wide = [swap(pile, count, 1) for pile in piles]
+        wide = []
+        for pile in piles:
+            wide.append(swap(pile, count, 1))
         parts = [in_vmem(part) for pair in zip(piles, wide, strict=True) for part in pair]
         strips = strips + across(strips)
     else:
@@ -515,23 +518,26 @@
         kept=2,
         held=range(1, 9),
     )
-    (q,) = call(
-        halo_query_kernel, [VMEM] * 2, [((n_keys, model), BF16)], (wq, x), kept=1, held=range(2)
-    )
     more = []
     if fast:
         more = [terms_qo[0], swap(terms_qo[1], count, 1)]
-    results = call(
+    q, kn, kf, *sums_qo = call(
+        halo_query_kernel,
+        [VMEM] * (3 + len(more)),
+        [((n_keys, model), BF16)] + [((own, model), F32)] * 2 + term_shapes[: len(more) // 2],
+        (wq, x, wk, *more),
+        kept=4 if fast else 3,
+        held=range(4 if fast else 3),
+    )
+    gk, gv, *terms_kv = call(
         functools.partial(key_kernel, groups, fast),
-        [SMEM] + [VMEM] * (2 + n_strips + len(more)),
-        term_shapes[: len(more) // 2] + [((own, model), BF16)] * 2 + term_shapes,
-        (scalars, mine, wk, q, *map(in_vmem, packs[1:]), *more),
+        [SMEM] + [VMEM] * (3 + n_strips),
+        [((own, model), BF16)] * 2 + term_shapes,
+        (scalars, mine, q, kn, kf, *map(in_vmem, packs[1:])),
         scratch=[pltpu.VMEM((n_keys, model), BF16)],
-        kept=5 if fast else 2,
-        held=[1, 2, 3] + ([3 + n_strips] if fast else []),
-    )
-    sums_qo, results = (results[0], results[1:]) if fast else (None, results)
-    gk, gv, *terms_kv = results
+        kept=4 if fast else 2,
+        held=range(1, 5),
+    )
     (grads,) = call(
         final_kernel,
         [VMEM] * 8,
@@ -555,16 +561,16 @@
     arrived = swap(terms_kv[1], count, 1).astype(F32)
     sums_kv = (terms_kv[0].astype(F32) + arrived).astype(BF16)
 
-    def all_four(at):
-        qo, kv = pick(sums_qo, at, 1), pick(sums_kv, at, 1)
-        return jnp.concatenate([qo[0:1], kv, qo[1:2]], axis=0)
-
-    arrived = [
-        swap(all_four(here ^ step), count, 2 * step) for step in range(1, spots)
-    ]
-    pieces = all_four(here).astype(F32)
-    for part in arrived:
-        pieces = pieces + part.astype(F32)
+    def within_matrix(sums):
+        arrived = [swap(pick(sums, here ^ step, 1), count, 2 * step) for step in range(1, spots)]
+        total = pick(sums, here, 1).astype(F32)
+        for part in arrived:
+            total = total + part.astype(F32)
+        return total
+
+    total_qo = within_matrix(sums_qo[0])
+    total_kv = within_matrix(sums_kv)
+    pieces = jnp.concatenate([total_qo[0:1], total_kv, total_qo[1:2]], axis=0)
     arrived = [
         swap(pick(pieces, mine ^ step, 0).astype(BF16), count, per_matrix * step)
         for step in range(1, 4)

time: 68.3 us -> 68.1 us (level)
  waiting for transfers between devices: 24.9 us -> 21 us
  starting transfers between devices: 29 us -> 32.8 us
    ppermute x18 -> x21, starting transfers between devices: 22.9 us -> 26.7 us  [swap(): return lax.ppermute(value, AXES, [(i, i ^ mask) for i in range(count)])]
    ppermute x18 -> x21, waiting for transfers between devices: 19.5 us -> 15.9 us  [swap(): return lax.ppermute(value, AXES, [(i, i ^ mask) for i in range(count)])]
  transfers between devices with their start and end apart: 28 -> 31, of which waited for: 14 -> 12; matrix products, arithmetic and copies ran while one was open for 0% -> 0% of each run, Pallas kernels for 3% -> 3%
where the time goes in v4:
time: 68.1 us; the launch traced here: 68 us
  starting transfers between devices  32.8 us (48%)
  waiting for transfers between devices  21 us (31%)
  Pallas kernels  12.3 us (18%)
  between operations  0.82 us (1%)
  local copies, waits for them, and re-layouts  0.78 us (1%)
    ppermute x21, starting transfers between devices, swap(): return lax.ppermute(value, AXES, [(i, i ^ mask) for i in range(count)])  26.7 us
    ppermute x21, waiting for transfers between devices, swap(): return lax.ppermute(value, AXES, [(i, i ^ mask) for i in range(count)])  15.9 us
    pallas_call x7, Pallas kernels, call(): pl.pallas_call(kernel, out_shape=[pltpu.VMEM(s, t) if n < kept else jax.S...  12.3 us
    ppermute x2, waiting for transfers between devices, beside(): near = lax.ppermute(strip, 'rows', side_pairs(rows, 0))  4.23 us
    ppermute x2, starting transfers between devices, beside(): near = lax.ppermute(strip, 'rows', side_pairs(rows, 0))  3.09 us
    ppermute x6, starting transfers between devices, across(): sides.append(lax.ppermute(strip, 'cols', side_pairs(cols, n)))  1.69 us
  transfers between devices with their start and end apart: 31, of which 12 were waited for; matrix products, arithmetic and copies ran while one was open for 0% of the time, Pallas kernels for 3%

profile of v4, /device:TPU:0, one launch (start us, length us, event | category | flops | bytes accessed | tf_op | source)
XLA Modules:
  0.0 68.0 jit_solution(9549163153144209784)
XLA Ops:
  0.6 1.1 %shard_map.60.refs_11_ = bf16[2,72,384]{2,1,0:T(8,128)(2,1)S(1)} custom-call(s32[1,2]{1,0:T(1,128)} %tissue.1, bf16[8,16,384]{2,1,0:T(8,128)(2,1)} %tokens.3), custom_call_target="tpu_custom_call" | custom-call | tf_op jit(solution)/shard_map/pallas_call | solution.py:396
  1.7 3.0 %collective-permute-start.10 = (bf16[2,72,384]{2,1,0:T(8,128)(2,1)S(1)}, bf16[2,72,384]{2,1,0:T(8,128)(2,1)S(1)}, u32[]{:S(2)}, u32[]{:S(2)}) collective-permute-start(bf16[2,72,384]{2,1,0:T(8,128)(2,1)S(1)} %shard_map.60.refs_11_), channel_id=1, source_target_pairs={{0,2},{2,0},{4,6},{6,4},{8,10},{10,8},{12,14},{14,12},{16,18},{18,... | collective-permute-start | bytes 331784 | tf_op jit(solution)/shard_map/ppermute | solution.py:422
  4.8 0.7 collective-permute-start.11
  5.5 4.3 %collective-permute-start = (bf16[1,48,384]{2,1,0:T(8,128)(2,1)S(1)}, bf16[1,48,384]{2,1,0:T(8,128)(2,1)S(1)}, u32[]{:S(2)}, u32[]{:S(2)}) collective-permute-start(bf16[1,48,384]{2,1,0:T(8,128)(2,1)S(1)} %reshape.17.refs_0_), channel_id=1, source_target_pairs={{0,8},{1,9},{2,10},{3,11},{4,12},{5,13},{6,14},{7,15},{8,0},{9,1},... | collective-permute-start | bytes 110600 | tf_op jit(solution)/shard_map/ppermute | solution.py:410
  9.7 2.6 %collective-permute-start.1 = (bf16[1,48,384]{2,1,0:T(8,128)(2,1)S(1)}, bf16[1,48,384]{2,1,0:T(8,128)(2,1)S(1)}, u32[]{:S(2)}, u32[]{:S(2)}) collective-permute-start(bf16[1,48,384]{2,1,0:T(8,128)(2,1)S(1)} %reshape.17.refs_0_), channel_id=1, source_target_pairs={{0,16},{1,17},{2,18},{3,19},{4,20},{5,21},{6,22},{7,23},{8,24},{9,... | collective-permute-start | bytes 110600 | tf_op jit(solution)/shard_map/ppermute | solution.py:410
  12.3 0.0 collective-permute-start.2
  12.3 1.0 %collective-permute-done.refs_1_ = bf16[1,48,384]{2,1,0:T(8,128)(2,1)S(1)} collective-permute-done((bf16[1,48,384]{2,1,0:T(8,128)(2,1)S(1)}, bf16[1,48,384]{2,1,0:T(8,128)(2,1)S(1)}, u32[]{:S(2)}, u32[]{:S(2)}) %collective-permute-start) | collective-permute-done | bytes 36896 | tf_op jit(solution)/shard_map/ppermute | solution.py:410
  13.3 1.6 %collective-permute-done.1.refs_2_ = bf16[1,48,384]{2,1,0:T(8,128)(2,1)S(1)} collective-permute-done((bf16[1,48,384]{2,1,0:T(8,128)(2,1)S(1)}, bf16[1,48,384]{2,1,0:T(8,128)(2,1)S(1)}, u32[]{:S(2)}, u32[]{:S(2)}) %collective-permute-start.1) | collective-permute-done | bytes 36896 | tf_op jit(solution)/shard_map/ppermute | solution.py:410
  14.9 3.2 %collective-permute-done.2.refs_3_ = bf16[1,48,384]{2,1,0:T(8,128)(2,1)S(1)} collective-permute-done((bf16[1,48,384]{2,1,0:T(8,128)(2,1)S(1)}, bf16[1,48,384]{2,1,0:T(8,128)(2,1)S(1)}, u32[]{:S(2)}, u32[]{:S(2)}) %collective-permute-start.2) | collective-permute-done | bytes 36896 | tf_op jit(solution)/shard_map/ppermute | solution.py:410
  18.1 1.7 %collective-permute-start.4 = (bf16[4,48,384]{2,1,0:T(8,128)(2,1)S(1)}, bf16[4,48,384]{2,1,0:T(8,128)(2,1)S(1)}, u32[]{:S(2)}, u32[]{:S(2)}) collective-permute-start(bf16[4,48,384]{2,1,0:T(8,128)(2,1)S(1)} %shard_map.59.refs_3_), channel_id=1, source_target_pairs={{0,2},{1,3},{2,0},{3,1},{4,6},{5,7},{6,4},{7,5},{8,10},{9,11},{10,... | collective-permute-start | bytes 442376 | tf_op jit(solution)/shard_map/ppermute | solution.py:410
  19.8 0.0 collective-permute-start.6
  19.8 1.9 %collective-permute-start.8 = (bf16[4,48,384]{2,1,0:T(8,128)(2,1)S(1)}, bf16[4,48,384]{2,1,0:T(8,128)(2,1)S(1)}, u32[]{:S(2)}, u32[]{:S(2)}) collective-permute-start(bf16[4,48,384]{2,1,0:T(8,128)(2,1)S(1)} %shard_map.59.refs_3_), channel_id=1, source_target_pairs={{0,6},{1,7},{2,4},{3,5},{4,2},{5,3},{6,0},{7,1},{8,14},{9,15},{10,... | collective-permute-start | bytes 442376 | tf_op jit(solution)/shard_map/ppermute | solution.py:410
  21.7 0.0 collective-permute-done.10.refs_12_
  21.7 0.0 collective-permute-start.3
  21.7 0.0 collective-permute-done.11.refs_13_
  21.7 0.5 collective-permute-start.12
  22.2 1.8 %collective-permute-done.4.refs_5_ = bf16[4,48,384]{2,1,0:T(8,128)(2,1)S(1)} collective-permute-done((bf16[4,48,384]{2,1,0:T(8,128)(2,1)S(1)}, bf16[4,48,384]{2,1,0:T(8,128)(2,1)S(1)}, u32[]{:S(2)}, u32[]{:S(2)}) %collective-permute-start.4) | collective-permute-done | bytes 147488 | tf_op jit(solution)/shard_map/ppermute | solution.py:410
  24.0 0.0 collective-permute-start.5
  24.0 2.5 %collective-permute-done.6.refs_7_ = bf16[4,48,384]{2,1,0:T(8,128)(2,1)S(1)} collective-permute-done((bf16[4,48,384]{2,1,0:T(8,128)(2,1)S(1)}, bf16[4,48,384]{2,1,0:T(8,128)(2,1)S(1)}, u32[]{:S(2)}, u32[]{:S(2)}) %collective-permute-start.6) | collective-permute-done | bytes 147488 | tf_op jit(solution)/shard_map/ppermute | solution.py:410
  26.5 0.5 collective-permute-start.9
  27.0 0.1 collective-permute-start.13
  27.1 0.4 collective-permute-start.14
  27.5 0.1 pad_add_fusion.refs_0_.scalars
  27.6 0.7 %collective-permute-done.13.refs_15_ = bf16[2,72,384]{2,1,0:T(8,128)(2,1)S(1)} collective-permute-done((bf16[2,72,384]{2,1,0:T(8,128)(2,1)S(1)}, bf16[2,72,384]{2,1,0:T(8,128)(2,1)S(1)}, u32[]{:S(2)}, u32[]{:S(2)}) %collective-permute-start.13) | collective-permute-done | bytes 110624 | tf_op jit(solution)/shard_map/ppermute | solution.py:431
  28.3 0.2 collective-permute-done.14.refs_16_
  28.5 0.0 collective-permute-done.7.refs_8_
  28.5 0.0 collective-permute-done.9.refs_10_
  28.5 4.4 %shard_map.61 = (bf16[384,384]{1,0:T(8,128)(2,1)S(1)}, bf16[384,384]{1,0:T(8,128)(2,1)S(1)}, bf16[384,384]{1,0:T(8,128)(2,1)S(1)}, bf16[576,384]{1,0:T(8,128)(2,...) custom-call(s32[4]{0:T(128)S(1)} %pad_add_fusion.refs_0_.scalars, ...), custom_call_target="tpu_custom_call" | custom-call | tf_op jit(solution)/shard_map/pallas_call | solution.py:396
  32.9 2.4 %shard_map.62 = (bf16[128,384]{1,0:T(8,128)(2,1)S(1)}, bf16[2,4,48,384]{3,2,1,0:T(8,128)(2,1)S(1)}, bf16[2,4,48,384]{3,2,1,0:T(8,128)(2,1)S(1)}) custom-call(s32[4]{0:T(128)S(1)} %pad_add_fusion.refs_0_.scalars, bf16[384,384]{1,0:T(8,128)(2,1)S(1)} %get-tuple-element.25.wq, bf16[576,384]{1,0:T(8,128)(2,1)S(1)} %get-tuple-element.28.k, ...), custom_call_target="tpu_custom_call" | custom-call | tf_op jit(solution)/shard_map/pallas_call | solution.py:396
  35.3 0.4 collective-permute-start.15
  35.8 0.1 collective-permute-start.16
  35.8 0.7 collective-permute-start.17
  36.5 0.2 collective-permute-start.18
  36.6 4.2 %collective-permute-done.16.refs_0_ = bf16[2,72,384]{2,1,0:T(8,128)(2,1)S(1)} collective-permute-done((bf16[2,72,384]{2,1,0:T(8,128)(2,1)S(1)}, bf16[2,72,384]{2,1,0:T(8,128)(2,1)S(1)}, u32[]{:S(2)}, u32[]{:S(2)}) %collective-permute-start.16) | collective-permute-done | bytes 110624 | tf_op jit(solution)/shard_map/ppermute | solution.py:422
  40.9 0.0 collective-permute-done.17.refs_1_
  40.9 0.5 collective-permute-start.20
  41.4 0.0 collective-permute-done.15.refs_1_
  41.4 0.9 %shard_map.63 = (bf16[576,384]{1,0:T(8,128)(2,1)S(1)}, f32[128,384]{1,0:T(8,128)S(1)}, f32[128,384]{1,0:T(8,128)S(1)}, bf16[2,4,48,384]{3,2,1,0:T(8,128)(2,1)S(1)}) custom-call(bf16[384,384]{1,0:T(8,128)(2,1)S(1)} %get-tuple-element.25.wq, bf16[576,384]{1,0:T(8,128)(2,1)S(1)} %get-tuple-element.36.x, bf16[384,384]{1,0:T(8,128)(2,1)S(1)} %get-tuple-element.26.wk, ...), custom_call_target="tpu_custom_call" | custom-call | tf_op jit(solution)/shard_map/pallas_call | solution.py:396
  42.3 0.0 collective-permute-done.18.refs_2_
  42.3 0.0 collective-permute-done.19.refs_3_
  42.3 0.0 collective-permute-done.20.refs_4_
  42.3 2.3 %shard_map.64 = (bf16[128,384]{1,0:T(8,128)(2,1)S(1)}, bf16[128,384]{1,0:T(8,128)(2,1)S(1)}, bf16[2,4,48,384]{3,2,1,0:T(8,128)(2,1)S(1)}, bf16[2,4,48,384]{3,2,1,0:T(8,128)(2,1)S(1)}) custom-call(s32[4]{0:T(128)S(1)} %pad_add_fusion.refs_0_.scalars, bf16[528,384]{1,0:T(8,128)(2,1)S(1)} %get-tuple-element.34.mine, bf16[576,384]{1,0:T(8,128)(2,1)S(1)} %get-tuple-element.39.q, ...), custom_call_target="tpu_custom_call" | custom-call | tf_op jit(solution)/shard_map/pallas_call | solution.py:396
  44.6 0.4 collective-permute-start.24
  45.1 4.2 %collective-permute-start.21 = (bf16[2,48,384]{2,1,0:T(8,128)(2,1)S(1)}, bf16[2,48,384]{2,1,0:T(8,128)(2,1)S(1)}, u32[]{:S(2)}, u32[]{:S(2)}) collective-permute-start(bf16[2,48,384]{2,1,0:T(8,128)(2,1)S(1)} %get-tuple-element.54), channel_id=1, source_target_pairs={{0,2},{1,3},{2,0},{3,1},{4,6},{5,7},{6,4},{7,5},{8,10},{9,11},{10,... | collective-permute-start | bytes 221192 | tf_op jit(solution)/shard_map/ppermute | solution.py:410
  49.3 2.1 %collective-permute-start.22 = (bf16[2,48,384]{2,1,0:T(8,128)(2,1)S(1)}, bf16[2,48,384]{2,1,0:T(8,128)(2,1)S(1)}, u32[]{:S(2)}, u32[]{:S(2)}) collective-permute-start(bf16[2,48,384]{2,1,0:T(8,128)(2,1)S(1)} %get-tuple-element.56), channel_id=1, source_target_pairs={{0,4},{1,5},{2,6},{3,7},{4,0},{5,1},{6,2},{7,3},{8,12},{9,13},{10,... | collective-permute-start | bytes 221192 | tf_op jit(solution)/shard_map/ppermute | solution.py:410
  51.4 0.0 collective-permute-start.23
  51.4 0.0 collective-permute-done.24
  51.4 0.1 add_convert_fusion
  51.5 1.5 %collective-permute-start.25 = (bf16[2,48,384]{2,1,0:T(8,128)(2,1)S(1)}, bf16[2,48,384]{2,1,0:T(8,128)(2,1)S(1)}, u32[]{:S(2)}, u32[]{:S(2)}) collective-permute-start(bf16[2,48,384]{2,1,0:T(8,128)(2,1)S(1)} %get-tuple-element.51), channel_id=1, source_target_pairs={{0,2},{1,3},{2,0},{3,1},{4,6},{5,7},{6,4},{7,5},{8,10},{9,11},{10,... | collective-permute-start | bytes 221192 | tf_op jit(solution)/shard_map/ppermute | solution.py:410
  53.1 2.0 %collective-permute-start.26 = (bf16[2,48,384]{2,1,0:T(8,128)(2,1)S(1)}, bf16[2,48,384]{2,1,0:T(8,128)(2,1)S(1)}, u32[]{:S(2)}, u32[]{:S(2)}) collective-permute-start(bf16[2,48,384]{2,1,0:T(8,128)(2,1)S(1)} %get-tuple-element.53), channel_id=1, source_target_pairs={{0,4},{1,5},{2,6},{3,7},{4,0},{5,1},{6,2},{7,3},{8,12},{9,13},{10,... | collective-permute-start | bytes 221192 | tf_op jit(solution)/shard_map/ppermute | solution.py:410
  55.1 0.6 collective-permute-start.27
  55.7 0.0 collective-permute-done.22
  55.7 1.4 %collective-permute-done.23 = bf16[2,48,384]{2,1,0:T(8,128)(2,1)S(1)} collective-permute-done((bf16[2,48,384]{2,1,0:T(8,128)(2,1)S(1)}, bf16[2,48,384]{2,1,0:T(8,128)(2,1)S(1)}, u32[]{:S(2)}, u32[]{:S(2)}) %collective-permute-start.23) | collective-permute-done | bytes 73760 | tf_op jit(solution)/shard_map/ppermute | solution.py:410
  57.1 0.0 collective-permute-done.25
  57.1 1.1 %collective-permute-done.26 = bf16[2,48,384]{2,1,0:T(8,128)(2,1)S(1)} collective-permute-done((bf16[2,48,384]{2,1,0:T(8,128)(2,1)S(1)}, bf16[2,48,384]{2,1,0:T(8,128)(2,1)S(1)}, u32[]{:S(2)}, u32[]{:S(2)}) %collective-permute-start.26) | collective-permute-done | bytes 73760 | tf_op jit(solution)/shard_map/ppermute | solution.py:410
  58.2 2.2 %collective-permute-done.27 = bf16[2,48,384]{2,1,0:T(8,128)(2,1)S(1)} collective-permute-done((bf16[2,48,384]{2,1,0:T(8,128)(2,1)S(1)}, bf16[2,48,384]{2,1,0:T(8,128)(2,1)S(1)}, u32[]{:S(2)}, u32[]{:S(2)}) %collective-permute-start.27) | collective-permute-done | bytes 73760 | tf_op jit(solution)/shard_map/ppermute | solution.py:410
  60.3 0.1 fusion.1
  60.5 0.1 collective-permute-start.28
  60.6 0.1 collective-permute-start.29
  60.7 4.3 %collective-permute-start.30 = (bf16[48,384]{1,0:T(8,128)(2,1)S(1)}, bf16[48,384]{1,0:T(8,128)(2,1)S(1)}, u32[]{:S(2)}, u32[]{:S(2)}) collective-permute-start(bf16[48,384]{1,0:T(8,128)(2,1)S(1)} %get-tuple-element.49), channel_id=1, source_target_pairs={{0,24},{1,25},{2,26},{3,27},{4,28},{5,29},{6,30},{7,31},{8,16},{9,... | collective-permute-start | bytes 110600 | tf_op jit(solution)/shard_map/ppermute | solution.py:410
  65.0 1.2 %shard_map.65 = bf16[8,16,384]{2,1,0:T(8,128)(2,1)} custom-call(bf16[8,16,384]{2,1,0:T(8,128)(2,1)S(1)} %copy-done, bf16[384,384]{1,0:T(8,128)(2,1)S(1)} %get-tuple-element.25.wq, bf16[384,384]{1,0:T(8,128)(2,1)S(1)} %get-tuple-element.26.wk, bf16[384,384]{1,0:T(8,128)(2,1)S(1)} %get-tuple-element.27.wv, bf16[128,384]{1,0:T(8,128)(2,1)S(1)} %get-tuple-element.35.gq, ...), custom_call_target="tpu_custom_call" | custom-call | tf_op jit(solution)/shard_map/pallas_call | solution.py:396
  66.1 0.0 collective-permute-done.28
  66.1 1.2 %collective-permute-done.30 = bf16[48,384]{1,0:T(8,128)(2,1)S(1)} collective-permute-done((bf16[48,384]{1,0:T(8,128)(2,1)S(1)}, bf16[48,384]{1,0:T(8,128)(2,1)S(1)}, u32[]{:S(2)}, u32[]{:S(2)}) %collective-permute-start.30) | collective-permute-done | bytes 36896 | tf_op jit(solution)/shard_map/ppermute | solution.py:410
  67.3 0.6 reshape.18
  (20 shorter events, 0.2 us)
Async XLA Ops:
  0.6 4.8 %copy-start.1 = (bf16[18432]{0:T(1024)(128)(2,1)S(1)}, bf16[18432]{0:T(1024)(128)(2,1)}, u32[]{:S(2)}) copy-start(bf16[18432]{0:T(1024)(128)(2,1)} %param.7) | copy-start | bytes 110596
  1.7 19.9 %collective-permute-start.10 = (bf16[2,72,384]{2,1,0:T(8,128)(2,1)S(1)}, bf16[2,72,384]{2,1,0:T(8,128)(2,1)S(1)}, u32[]{:S(2)}, u32[]{:S(2)}) collective-permute-start(bf16[2,72,384]{2,1,0:T(8,128)(2,1)S(1)} %shard_map.60.refs_11_), channel_id=1, source_target_pairs={{0,2},{2,0},{4,6},{6,4},{8,10},{10,8},{12,14},{14,12},{16,18},{18,... | collective-permute-start | bytes 331784 | tf_op jit(solution)/shard_map/ppermute | solution.py:422
  4.8 16.9 %collective-permute-start.11 = (bf16[2,72,384]{2,1,0:T(8,128)(2,1)S(1)}, bf16[2,72,384]{2,1,0:T(8,128)(2,1)S(1)}, u32[]{:S(2)}, u32[]{:S(2)}) collective-permute-start(bf16[2,72,384]{2,1,0:T(8,128)(2,1)S(1)} %shard_map.60.refs_11_), channel_id=1, source_target_pairs={{2,4},{4,2},{6,8},{8,6},{10,12},{12,10},{14,16},{16,14},{18,20},{2... | collective-permute-start | bytes 331784 | tf_op jit(solution)/shard_map/ppermute | solution.py:423
  5.5 7.8 %collective-permute-start = (bf16[1,48,384]{2,1,0:T(8,128)(2,1)S(1)}, bf16[1,48,384]{2,1,0:T(8,128)(2,1)S(1)}, u32[]{:S(2)}, u32[]{:S(2)}) collective-permute-start(bf16[1,48,384]{2,1,0:T(8,128)(2,1)S(1)} %reshape.17.refs_0_), channel_id=1, source_target_pairs={{0,8},{1,9},{2,10},{3,11},{4,12},{5,13},{6,14},{7,15},{8,0},{9,1},... | collective-permute-start | bytes 110600 | tf_op jit(solution)/shard_map/ppermute | solution.py:410
  9.7 5.2 %collective-permute-start.1 = (bf16[1,48,384]{2,1,0:T(8,128)(2,1)S(1)}, bf16[1,48,384]{2,1,0:T(8,128)(2,1)S(1)}, u32[]{:S(2)}, u32[]{:S(2)}) collective-permute-start(bf16[1,48,384]{2,1,0:T(8,128)(2,1)S(1)} %reshape.17.refs_0_), channel_id=1, source_target_pairs={{0,16},{1,17},{2,18},{3,19},{4,20},{5,21},{6,22},{7,23},{8,24},{9,... | collective-permute-start | bytes 110600 | tf_op jit(solution)/shard_map/ppermute | solution.py:410
  12.3 5.8 %collective-permute-start.2 = (bf16[1,48,384]{2,1,0:T(8,128)(2,1)S(1)}, bf16[1,48,384]{2,1,0:T(8,128)(2,1)S(1)}, u32[]{:S(2)}, u32[]{:S(2)}) collective-permute-start(bf16[1,48,384]{2,1,0:T(8,128)(2,1)S(1)} %reshape.17.refs_0_), channel_id=1, source_target_pairs={{0,24},{1,25},{2,26},{3,27},{4,28},{5,29},{6,30},{7,31},{8,16},{9,... | collective-permute-start | bytes 110600 | tf_op jit(solution)/shard_map/ppermute | solution.py:410
  18.1 10.4 %copy-start = (bf16[8,16,384]{2,1,0:T(8,128)(2,1)S(1)}, bf16[8,16,384]{2,1,0:T(8,128)(2,1)}, u32[]{:S(2)}) copy-start(bf16[8,16,384]{2,1,0:T(8,128)(2,1)} %tokens.3) | copy-start | bytes 294916
  18.1 5.9 %collective-permute-start.4 = (bf16[4,48,384]{2,1,0:T(8,128)(2,1)S(1)}, bf16[4,48,384]{2,1,0:T(8,128)(2,1)S(1)}, u32[]{:S(2)}, u32[]{:S(2)}) collective-permute-start(bf16[4,48,384]{2,1,0:T(8,128)(2,1)S(1)} %shard_map.59.refs_3_), channel_id=1, source_target_pairs={{0,2},{1,3},{2,0},{3,1},{4,6},{5,7},{6,4},{7,5},{8,10},{9,11},{10,... | collective-permute-start | bytes 442376 | tf_op jit(solution)/shard_map/ppermute | solution.py:410
  19.8 6.7 %collective-permute-start.6 = (bf16[4,48,384]{2,1,0:T(8,128)(2,1)S(1)}, bf16[4,48,384]{2,1,0:T(8,128)(2,1)S(1)}, u32[]{:S(2)}, u32[]{:S(2)}) collective-permute-start(bf16[4,48,384]{2,1,0:T(8,128)(2,1)S(1)} %shard_map.59.refs_3_), channel_id=1, source_target_pairs={{0,4},{1,5},{2,6},{3,7},{4,0},{5,1},{6,2},{7,3},{8,12},{9,13},{10,... | collective-permute-start | bytes 442376 | tf_op jit(solution)/shard_map/ppermute | solution.py:410
  19.8 6.7 %collective-permute-start.8 = (bf16[4,48,384]{2,1,0:T(8,128)(2,1)S(1)}, bf16[4,48,384]{2,1,0:T(8,128)(2,1)S(1)}, u32[]{:S(2)}, u32[]{:S(2)}) collective-permute-start(bf16[4,48,384]{2,1,0:T(8,128)(2,1)S(1)} %shard_map.59.refs_3_), channel_id=1, source_target_pairs={{0,6},{1,7},{2,4},{3,5},{4,2},{5,3},{6,0},{7,1},{8,14},{9,15},{10,... | collective-permute-start | bytes 442376 | tf_op jit(solution)/shard_map/ppermute | solution.py:410
  21.7 5.4 %collective-permute-start.3 = (bf16[4,48,384]{2,1,0:T(8,128)(2,1)S(1)}, bf16[4,48,384]{2,1,0:T(8,128)(2,1)S(1)}, u32[]{:S(2)}, u32[]{:S(2)}) collective-permute-start(bf16[4,48,384]{2,1,0:T(8,128)(2,1)S(1)} %shard_map.59.refs_3_), channel_id=1, source_target_pairs={{0,1},{1,0},{2,3},{3,2},{4,5},{5,4},{6,7},{7,6},{8,9},{9,8},{10,11... | collective-permute-start | bytes 442376 | tf_op jit(solution)/shard_map/ppermute | solution.py:410
  21.7 5.3 %collective-permute-start.12 = (bf16[2,72,384]{2,1,0:T(8,128)(2,1)S(1)}, bf16[2,72,384]{2,1,0:T(8,128)(2,1)S(1)}, u32[]{:S(2)}, u32[]{:S(2)}) collective-permute-start(bf16[2,72,384]{2,1,0:T(8,128)(2,1)S(1)} %shard_map.60.refs_11_), channel_id=1, source_target_pairs={{0,1},{1,0},{2,3},{3,2},{4,5},{5,4},{6,7},{7,6},{8,9},{9,8},{10,11... | collective-permute-start | bytes 331784 | tf_op jit(solution)/shard_map/ppermute | solution.py:431
  24.0 4.5 %collective-permute-start.5 = (bf16[4,48,384]{2,1,0:T(8,128)(2,1)S(1)}, bf16[4,48,384]{2,1,0:T(8,128)(2,1)S(1)}, u32[]{:S(2)}, u32[]{:S(2)}) collective-permute-start(bf16[4,48,384]{2,1,0:T(8,128)(2,1)S(1)} %collective-permute-done.4.refs_5_), channel_id=1, source_target_pairs={{0,1},{1,0},{2,3},{3,2},{4,5},{5,4},{6,7},{7,6},{8,9},{9,8},{10,11... | collective-permute-start | bytes 442376 | tf_op jit(solution)/shard_map/ppermute | solution.py:410
  26.5 2.0 %collective-permute-start.7 = (bf16[4,48,384]{2,1,0:T(8,128)(2,1)S(1)}, bf16[4,48,384]{2,1,0:T(8,128)(2,1)S(1)}, u32[]{:S(2)}, u32[]{:S(2)}) collective-permute-start(bf16[4,48,384]{2,1,0:T(8,128)(2,1)S(1)} %collective-permute-done.6.refs_7_), channel_id=1, source_target_pairs={{0,1},{1,0},{2,3},{3,2},{4,5},{5,4},{6,7},{7,6},{8,9},{9,8},{10,11... | collective-permute-start | bytes 442376 | tf_op jit(solution)/shard_map/ppermute | solution.py:410
  26.5 2.0 %collective-permute-start.9 = (bf16[4,48,384]{2,1,0:T(8,128)(2,1)S(1)}, bf16[4,48,384]{2,1,0:T(8,128)(2,1)S(1)}, u32[]{:S(2)}, u32[]{:S(2)}) collective-permute-start(bf16[4,48,384]{2,1,0:T(8,128)(2,1)S(1)} %collective-permute-done.8.refs_9_), channel_id=1, source_target_pairs={{0,1},{1,0},{2,3},{3,2},{4,5},{5,4},{6,7},{7,6},{8,9},{9,8},{10,11... | collective-permute-start | bytes 442376 | tf_op jit(solution)/shard_map/ppermute | solution.py:410
  27.0 1.3 %collective-permute-start.13 = (bf16[2,72,384]{2,1,0:T(8,128)(2,1)S(1)}, bf16[2,72,384]{2,1,0:T(8,128)(2,1)S(1)}, u32[]{:S(2)}, u32[]{:S(2)}) collective-permute-start(bf16[2,72,384]{2,1,0:T(8,128)(2,1)S(1)} %collective-permute-done.10.refs_12_), channel_id=1, source_target_pairs={{0,1},{1,0},{2,3},{3,2},{4,5},{5,4},{6,7},{7,6},{8,9},{9,8},{10,11... | collective-permute-start | bytes 331784 | tf_op jit(solution)/shard_map/ppermute | solution.py:431
  27.1 1.4 %collective-permute-start.14 = (bf16[2,72,384]{2,1,0:T(8,128)(2,1)S(1)}, bf16[2,72,384]{2,1,0:T(8,128)(2,1)S(1)}, u32[]{:S(2)}, u32[]{:S(2)}) collective-permute-start(bf16[2,72,384]{2,1,0:T(8,128)(2,1)S(1)} %collective-permute-done.11.refs_13_), channel_id=1, source_target_pairs={{0,1},{1,0},{2,3},{3,2},{4,5},{5,4},{6,7},{7,6},{8,9},{9,8},{10,11... | collective-permute-start | bytes 331784 | tf_op jit(solution)/shard_map/ppermute | solution.py:431
  35.3 6.1 %collective-permute-start.15 = (bf16[2,4,48,384]{3,2,1,0:T(8,128)(2,1)S(1)}, bf16[2,4,48,384]{3,2,1,0:T(8,128)(2,1)S(1)}, u32[]{:S(2)}, u32[]{:S(2)}) collective-permute-start(bf16[2,4,48,384]{3,2,1,0:T(8,128)(2,1)S(1)} %get-tuple-element.38), channel_id=1, source_target_pairs={{0,1},{1,0},{2,3},{3,2},{4,5},{5,4},{6,7},{7,6},{8,9},{9,8},{10,11... | collective-permute-start | bytes 884744 | tf_op jit(solution)/shard_map/ppermute | solution.py:410
  35.8 5.1 %collective-permute-start.16 = (bf16[2,72,384]{2,1,0:T(8,128)(2,1)S(1)}, bf16[2,72,384]{2,1,0:T(8,128)(2,1)S(1)}, u32[]{:S(2)}, u32[]{:S(2)}) collective-permute-start(bf16[2,72,384]{2,1,0:T(8,128)(2,1)S(1)} %get-tuple-element.42), channel_id=1, source_target_pairs={{0,2},{2,0},{4,6},{6,4},{8,10},{10,8},{12,14},{14,12},{16,18},{18,... | collective-permute-start | bytes 331784 | tf_op jit(solution)/shard_map/ppermute | solution.py:422
  35.8 5.1 %collective-permute-start.17 = (bf16[2,72,384]{2,1,0:T(8,128)(2,1)S(1)}, bf16[2,72,384]{2,1,0:T(8,128)(2,1)S(1)}, u32[]{:S(2)}, u32[]{:S(2)}) collective-permute-start(bf16[2,72,384]{2,1,0:T(8,128)(2,1)S(1)} %get-tuple-element.42), channel_id=1, source_target_pairs={{2,4},{4,2},{6,8},{8,6},{10,12},{12,10},{14,16},{16,14},{18,20},{2... | collective-permute-start | bytes 331784 | tf_op jit(solution)/shard_map/ppermute | solution.py:423
  36.5 5.8 %collective-permute-start.18 = (bf16[2,72,384]{2,1,0:T(8,128)(2,1)S(1)}, bf16[2,72,384]{2,1,0:T(8,128)(2,1)S(1)}, u32[]{:S(2)}, u32[]{:S(2)}) collective-permute-start(bf16[2,72,384]{2,1,0:T(8,128)(2,1)S(1)} %get-tuple-element.42), channel_id=1, source_target_pairs={{0,1},{1,0},{2,3},{3,2},{4,5},{5,4},{6,7},{7,6},{8,9},{9,8},{10,11... | collective-permute-start | bytes 331784 | tf_op jit(solution)/shard_map/ppermute | solution.py:431
  40.9 1.5 %collective-permute-start.19 = (bf16[2,72,384]{2,1,0:T(8,128)(2,1)S(1)}, bf16[2,72,384]{2,1,0:T(8,128)(2,1)S(1)}, u32[]{:S(2)}, u32[]{:S(2)}) collective-permute-start(bf16[2,72,384]{2,1,0:T(8,128)(2,1)S(1)} %collective-permute-done.16.refs_0_), channel_id=1, source_target_pairs={{0,1},{1,0},{2,3},{3,2},{4,5},{5,4},{6,7},{7,6},{8,9},{9,8},{10,11... | collective-permute-start | bytes 331784 | tf_op jit(solution)/shard_map/ppermute | solution.py:431
  40.9 1.5 %collective-permute-start.20 = (bf16[2,72,384]{2,1,0:T(8,128)(2,1)S(1)}, bf16[2,72,384]{2,1,0:T(8,128)(2,1)S(1)}, u32[]{:S(2)}, u32[]{:S(2)}) collective-permute-start(bf16[2,72,384]{2,1,0:T(8,128)(2,1)S(1)} %collective-permute-done.17.refs_1_), channel_id=1, source_target_pairs={{0,1},{1,0},{2,3},{3,2},{4,5},{5,4},{6,7},{7,6},{8,9},{9,8},{10,11... | collective-permute-start | bytes 331784 | tf_op jit(solution)/shard_map/ppermute | solution.py:431
  44.6 6.8 %collective-permute-start.24 = (bf16[2,4,48,384]{3,2,1,0:T(8,128)(2,1)S(1)}, bf16[2,4,48,384]{3,2,1,0:T(8,128)(2,1)S(1)}, u32[]{:S(2)}, u32[]{:S(2)}) collective-permute-start(bf16[2,4,48,384]{3,2,1,0:T(8,128)(2,1)S(1)} %get-tuple-element.47), channel_id=1, source_target_pairs={{0,1},{1,0},{2,3},{3,2},{4,5},{5,4},{6,7},{7,6},{8,9},{9,8},{10,11... | collective-permute-start | bytes 884744 | tf_op jit(solution)/shard_map/ppermute | solution.py:410
  45.1 10.0 %collective-permute-start.21 = (bf16[2,48,384]{2,1,0:T(8,128)(2,1)S(1)}, bf16[2,48,384]{2,1,0:T(8,128)(2,1)S(1)}, u32[]{:S(2)}, u32[]{:S(2)}) collective-permute-start(bf16[2,48,384]{2,1,0:T(8,128)(2,1)S(1)} %get-tuple-element.54), channel_id=1, source_target_pairs={{0,2},{1,3},{2,0},{3,1},{4,6},{5,7},{6,4},{7,5},{8,10},{9,11},{10,... | collective-permute-start | bytes 221192 | tf_op jit(solution)/shard_map/ppermute | solution.py:410
  49.3 6.4 %collective-permute-start.22 = (bf16[2,48,384]{2,1,0:T(8,128)(2,1)S(1)}, bf16[2,48,384]{2,1,0:T(8,128)(2,1)S(1)}, u32[]{:S(2)}, u32[]{:S(2)}) collective-permute-start(bf16[2,48,384]{2,1,0:T(8,128)(2,1)S(1)} %get-tuple-element.56), channel_id=1, source_target_pairs={{0,4},{1,5},{2,6},{3,7},{4,0},{5,1},{6,2},{7,3},{8,12},{9,13},{10,... | collective-permute-start | bytes 221192 | tf_op jit(solution)/shard_map/ppermute | solution.py:410
  51.4 5.7 %collective-permute-start.23 = (bf16[2,48,384]{2,1,0:T(8,128)(2,1)S(1)}, bf16[2,48,384]{2,1,0:T(8,128)(2,1)S(1)}, u32[]{:S(2)}, u32[]{:S(2)}) collective-permute-start(bf16[2,48,384]{2,1,0:T(8,128)(2,1)S(1)} %get-tuple-element.55), channel_id=1, source_target_pairs={{0,6},{1,7},{2,4},{3,5},{4,2},{5,3},{6,0},{7,1},{8,14},{9,15},{10,... | collective-permute-start | bytes 221192 | tf_op jit(solution)/shard_map/ppermute | solution.py:410
  51.5 5.5 %collective-permute-start.25 = (bf16[2,48,384]{2,1,0:T(8,128)(2,1)S(1)}, bf16[2,48,384]{2,1,0:T(8,128)(2,1)S(1)}, u32[]{:S(2)}, u32[]{:S(2)}) collective-permute-start(bf16[2,48,384]{2,1,0:T(8,128)(2,1)S(1)} %get-tuple-element.51), channel_id=1, source_target_pairs={{0,2},{1,3},{2,0},{3,1},{4,6},{5,7},{6,4},{7,5},{8,10},{9,11},{10,... | collective-permute-start | bytes 221192 | tf_op jit(solution)/shard_map/ppermute | solution.py:410
  53.1 5.1 %collective-permute-start.26 = (bf16[2,48,384]{2,1,0:T(8,128)(2,1)S(1)}, bf16[2,48,384]{2,1,0:T(8,128)(2,1)S(1)}, u32[]{:S(2)}, u32[]{:S(2)}) collective-permute-start(bf16[2,48,384]{2,1,0:T(8,128)(2,1)S(1)} %get-tuple-element.53), channel_id=1, source_target_pairs={{0,4},{1,5},{2,6},{3,7},{4,0},{5,1},{6,2},{7,3},{8,12},{9,13},{10,... | collective-permute-start | bytes 221192 | tf_op jit(solution)/shard_map/ppermute | solution.py:410
  55.1 5.3 %collective-permute-start.27 = (bf16[2,48,384]{2,1,0:T(8,128)(2,1)S(1)}, bf16[2,48,384]{2,1,0:T(8,128)(2,1)S(1)}, u32[]{:S(2)}, u32[]{:S(2)}) collective-permute-start(bf16[2,48,384]{2,1,0:T(8,128)(2,1)S(1)} %get-tuple-element.52), channel_id=1, source_target_pairs={{0,6},{1,7},{2,4},{3,5},{4,2},{5,3},{6,0},{7,1},{8,14},{9,15},{10,... | collective-permute-start | bytes 221192 | tf_op jit(solution)/shard_map/ppermute | solution.py:410
  60.5 5.6 %collective-permute-start.28 = (bf16[48,384]{1,0:T(8,128)(2,1)S(1)}, bf16[48,384]{1,0:T(8,128)(2,1)S(1)}, u32[]{:S(2)}, u32[]{:S(2)}) collective-permute-start(bf16[48,384]{1,0:T(8,128)(2,1)S(1)} %get-tuple-element.48), channel_id=1, source_target_pairs={{0,8},{1,9},{2,10},{3,11},{4,12},{5,13},{6,14},{7,15},{8,0},{9,1},... | collective-permute-start | bytes 110600 | tf_op jit(solution)/shard_map/ppermute | solution.py:410
  60.6 5.5 %collective-permute-start.29 = (bf16[48,384]{1,0:T(8,128)(2,1)S(1)}, bf16[48,384]{1,0:T(8,128)(2,1)S(1)}, u32[]{:S(2)}, u32[]{:S(2)}) collective-permute-start(bf16[48,384]{1,0:T(8,128)(2,1)S(1)} %get-tuple-element.50), channel_id=1, source_target_pairs={{0,16},{1,17},{2,18},{3,19},{4,20},{5,21},{6,22},{7,23},{8,24},{9,... | collective-permute-start | bytes 110600 | tf_op jit(solution)/shard_map/ppermute | solution.py:410
  60.7 6.6 %collective-permute-start.30 = (bf16[48,384]{1,0:T(8,128)(2,1)S(1)}, bf16[48,384]{1,0:T(8,128)(2,1)S(1)}, u32[]{:S(2)}, u32[]{:S(2)}) collective-permute-start(bf16[48,384]{1,0:T(8,128)(2,1)S(1)} %get-tuple-element.49), channel_id=1, source_target_pairs={{0,24},{1,25},{2,26},{3,27},{4,28},{5,29},{6,30},{7,31},{8,16},{9,... | collective-permute-start | bytes 110600 | tf_op jit(solution)/shard_map/ppermute | solution.py:410

commit v5 on v4

--- a/solution.py
+++ b/solution.py
@@ -223,9 +223,9 @@
         raised = jnp.exp(scores).reshape(4, PER, n_tiles * PER) * near
         total = jnp.sum(raised, axis=-1, keepdims=True) + rest
         inverse = (1.0 / total).astype(BF16).astype(F32)
-        low = (raised * inverse).reshape(4 * PER, n_tiles * PER).astype(BF16)
-        mixed_parts.append(join_heads(dot(low, values[:, lanes]), width))
+        low = raised.reshape(4 * PER, n_tiles * PER).astype(BF16)
         inverse = inverse.reshape(4 * PER, 1)
+        mixed_parts.append(join_heads(dot(low, values[:, lanes]) * inverse, width))
         inverses += [inverse[0:own], inverse[own:]]
     mixed = (jnp.concatenate(mixed_parts, axis=1) * query_mask).astype(BF16)
     mixed_out[...] = mixed
@@ -302,10 +302,10 @@
         at = HEADS + 2 * p
         delta = jnp.concatenate([stats[:, at : at + 1], stats[:, at + 1 : at + 2]], axis=0)
         full = jnp.exp(scores).reshape(4, PER, n_tiles * PER) * near
-        full = full.reshape(4 * PER, n_tiles * PER) * inverse
+        full = full.reshape(4 * PER, n_tiles * PER)
         grad_attn = dot_nt(split_heads(grad_mixed[:, lanes], width), values)
         grad_scores = (full * (grad_attn - delta)).astype(BF16)
-        parts.append(join_heads(dot(grad_scores, keys), width) * scale)
+        parts.append(join_heads(dot(grad_scores, keys) * (inverse * scale), width))
     grad_qn = jnp.concatenate(parts, axis=1)
     grad_query = head_back(q_normal, q_factor, grad_qn, ones, width).astype(BF16)
     gq_out[...] = grad_query

time: 68.1 us -> 67.4 us (0.990)
  Pallas kernels: 12.3 us -> 11.5 us
    pallas_call x7, Pallas kernels: 12.3 us -> 11.5 us  [call(): pl.pallas_call(kernel, out_shape=[pltpu.VMEM(s, t) if n < kept else jax.S...]
where the time goes in v5:
time: 67.4 us; the launch traced here: 67.2 us
  starting transfers between devices  32.8 us (49%)
  waiting for transfers between devices  21.1 us (31%)
  Pallas kernels  11.5 us (17%)
  between operations  0.82 us (1%)
  local copies, waits for them, and re-layouts  0.78 us (1%)
    ppermute x21, starting transfers between devices, swap(): return lax.ppermute(value, AXES, [(i, i ^ mask) for i in range(count)])  26.7 us
    ppermute x21, waiting for transfers between devices, swap(): return lax.ppermute(value, AXES, [(i, i ^ mask) for i in range(count)])  15.9 us
    pallas_call x7, Pallas kernels, call(): pl.pallas_call(kernel, out_shape=[pltpu.VMEM(s, t) if n < kept else jax.S...  11.5 us
    ppermute x2, waiting for transfers between devices, beside(): near = lax.ppermute(strip, 'rows', side_pairs(rows, 0))  4.23 us
    ppermute x2, starting transfers between devices, beside(): near = lax.ppermute(strip, 'rows', side_pairs(rows, 0))  3.1 us
    ppermute x6, starting transfers between devices, across(): sides.append(lax.ppermute(strip, 'cols', side_pairs(cols, n)))  1.68 us
  transfers between devices with their start and end apart: 31, of which 12 were waited for; matrix products, arithmetic and copies ran while one was open for 0% of the time, Pallas kernels for 3%

profile of v5, /device:TPU:0, one launch (start us, length us, event | category | flops | bytes accessed | tf_op | source)
XLA Modules:
  0.0 67.2 jit_solution(5186874423027789029)
XLA Ops:
  0.6 1.1 %shard_map.60.refs_11_ = bf16[2,72,384]{2,1,0:T(8,128)(2,1)S(1)} custom-call(s32[1,2]{1,0:T(1,128)} %tissue.1, bf16[8,16,384]{2,1,0:T(8,128)(2,1)} %tokens.3), custom_call_target="tpu_custom_call" | custom-call | tf_op jit(solution)/shard_map/pallas_call | solution.py:396
  1.7 3.0 %collective-permute-start.10 = (bf16[2,72,384]{2,1,0:T(8,128)(2,1)S(1)}, bf16[2,72,384]{2,1,0:T(8,128)(2,1)S(1)}, u32[]{:S(2)}, u32[]{:S(2)}) collective-permute-start(bf16[2,72,384]{2,1,0:T(8,128)(2,1)S(1)} %shard_map.60.refs_11_), channel_id=1, source_target_pairs={{0,2},{2,0},{4,6},{6,4},{8,10},{10,8},{12,14},{14,12},{16,18},{18,... | collective-permute-start | bytes 331784 | tf_op jit(solution)/shard_map/ppermute | solution.py:422
  4.8 0.7 collective-permute-start.11
  5.5 4.3 %collective-permute-start = (bf16[1,48,384]{2,1,0:T(8,128)(2,1)S(1)}, bf16[1,48,384]{2,1,0:T(8,128)(2,1)S(1)}, u32[]{:S(2)}, u32[]{:S(2)}) collective-permute-start(bf16[1,48,384]{2,1,0:T(8,128)(2,1)S(1)} %reshape.17.refs_0_), channel_id=1, source_target_pairs={{0,8},{1,9},{2,10},{3,11},{4,12},{5,13},{6,14},{7,15},{8,0},{9,1},... | collective-permute-start | bytes 110600 | tf_op jit(solution)/shard_map/ppermute | solution.py:410
  9.7 2.6 %collective-permute-start.1 = (bf16[1,48,384]{2,1,0:T(8,128)(2,1)S(1)}, bf16[1,48,384]{2,1,0:T(8,128)(2,1)S(1)}, u32[]{:S(2)}, u32[]{:S(2)}) collective-permute-start(bf16[1,48,384]{2,1,0:T(8,128)(2,1)S(1)} %reshape.17.refs_0_), channel_id=1, source_target_pairs={{0,16},{1,17},{2,18},{3,19},{4,20},{5,21},{6,22},{7,23},{8,24},{9,... | collective-permute-start | bytes 110600 | tf_op jit(solution)/shard_map/ppermute | solution.py:410
  12.3 0.0 collective-permute-start.2
  12.3 1.0 %collective-permute-done.refs_1_ = bf16[1,48,384]{2,1,0:T(8,128)(2,1)S(1)} collective-permute-done((bf16[1,48,384]{2,1,0:T(8,128)(2,1)S(1)}, bf16[1,48,384]{2,1,0:T(8,128)(2,1)S(1)}, u32[]{:S(2)}, u32[]{:S(2)}) %collective-permute-start) | collective-permute-done | bytes 36896 | tf_op jit(solution)/shard_map/ppermute | solution.py:410
  13.3 1.6 %collective-permute-done.1.refs_2_ = bf16[1,48,384]{2,1,0:T(8,128)(2,1)S(1)} collective-permute-done((bf16[1,48,384]{2,1,0:T(8,128)(2,1)S(1)}, bf16[1,48,384]{2,1,0:T(8,128)(2,1)S(1)}, u32[]{:S(2)}, u32[]{:S(2)}) %collective-permute-start.1) | collective-permute-done | bytes 36896 | tf_op jit(solution)/shard_map/ppermute | solution.py:410
  14.9 3.2 %collective-permute-done.2.refs_3_ = bf16[1,48,384]{2,1,0:T(8,128)(2,1)S(1)} collective-permute-done((bf16[1,48,384]{2,1,0:T(8,128)(2,1)S(1)}, bf16[1,48,384]{2,1,0:T(8,128)(2,1)S(1)}, u32[]{:S(2)}, u32[]{:S(2)}) %collective-permute-start.2) | collective-permute-done | bytes 36896 | tf_op jit(solution)/shard_map/ppermute | solution.py:410
  18.1 1.7 %collective-permute-start.4 = (bf16[4,48,384]{2,1,0:T(8,128)(2,1)S(1)}, bf16[4,48,384]{2,1,0:T(8,128)(2,1)S(1)}, u32[]{:S(2)}, u32[]{:S(2)}) collective-permute-start(bf16[4,48,384]{2,1,0:T(8,128)(2,1)S(1)} %shard_map.59.refs_3_), channel_id=1, source_target_pairs={{0,2},{1,3},{2,0},{3,1},{4,6},{5,7},{6,4},{7,5},{8,10},{9,11},{10,... | collective-permute-start | bytes 442376 | tf_op jit(solution)/shard_map/ppermute | solution.py:410
  19.8 0.0 collective-permute-start.6
  19.8 1.9 %collective-permute-start.8 = (bf16[4,48,384]{2,1,0:T(8,128)(2,1)S(1)}, bf16[4,48,384]{2,1,0:T(8,128)(2,1)S(1)}, u32[]{:S(2)}, u32[]{:S(2)}) collective-permute-start(bf16[4,48,384]{2,1,0:T(8,128)(2,1)S(1)} %shard_map.59.refs_3_), channel_id=1, source_target_pairs={{0,6},{1,7},{2,4},{3,5},{4,2},{5,3},{6,0},{7,1},{8,14},{9,15},{10,... | collective-permute-start | bytes 442376 | tf_op jit(solution)/shard_map/ppermute | solution.py:410
  21.7 0.0 collective-permute-done.10.refs_12_
  21.7 0.0 collective-permute-start.3
  21.7 0.0 collective-permute-done.11.refs_13_
  21.7 0.5 collective-permute-start.12
  22.2 1.8 %collective-permute-done.4.refs_5_ = bf16[4,48,384]{2,1,0:T(8,128)(2,1)S(1)} collective-permute-done((bf16[4,48,384]{2,1,0:T(8,128)(2,1)S(1)}, bf16[4,48,384]{2,1,0:T(8,128)(2,1)S(1)}, u32[]{:S(2)}, u32[]{:S(2)}) %collective-permute-start.4) | collective-permute-done | bytes 147488 | tf_op jit(solution)/shard_map/ppermute | solution.py:410
  24.0 0.0 collective-permute-start.5
  24.0 2.5 %collective-permute-done.6.refs_7_ = bf16[4,48,384]{2,1,0:T(8,128)(2,1)S(1)} collective-permute-done((bf16[4,48,384]{2,1,0:T(8,128)(2,1)S(1)}, bf16[4,48,384]{2,1,0:T(8,128)(2,1)S(1)}, u32[]{:S(2)}, u32[]{:S(2)}) %collective-permute-start.6) | collective-permute-done | bytes 147488 | tf_op jit(solution)/shard_map/ppermute | solution.py:410
  26.5 0.0 collective-permute-start.7
  26.5 0.5 collective-permute-start.9
  27.0 0.1 collective-permute-start.13
  27.1 0.4 collective-permute-start.14
  27.5 0.1 pad_add_fusion.refs_0_.scalars
  27.6 0.7 %collective-permute-done.13.refs_15_ = bf16[2,72,384]{2,1,0:T(8,128)(2,1)S(1)} collective-permute-done((bf16[2,72,384]{2,1,0:T(8,128)(2,1)S(1)}, bf16[2,72,384]{2,1,0:T(8,128)(2,1)S(1)}, u32[]{:S(2)}, u32[]{:S(2)}) %collective-permute-start.13) | collective-permute-done | bytes 110624 | tf_op jit(solution)/shard_map/ppermute | solution.py:431
  28.3 0.2 collective-permute-done.14.refs_16_
  28.5 0.0 collective-permute-done.7.refs_8_
  28.5 0.0 collective-permute-done.9.refs_10_
  28.5 3.6 %shard_map.61 = (bf16[384,384]{1,0:T(8,128)(2,1)S(1)}, bf16[384,384]{1,0:T(8,128)(2,1)S(1)}, bf16[384,384]{1,0:T(8,128)(2,1)S(1)}, bf16[576,384]{1,0:T(8,128)(2,...) custom-call(s32[4]{0:T(128)S(1)} %pad_add_fusion.refs_0_.scalars, ...), custom_call_target="tpu_custom_call" | custom-call | tf_op jit(solution)/shard_map/pallas_call | solution.py:396
  32.1 2.4 %shard_map.62 = (bf16[128,384]{1,0:T(8,128)(2,1)S(1)}, bf16[2,4,48,384]{3,2,1,0:T(8,128)(2,1)S(1)}, bf16[2,4,48,384]{3,2,1,0:T(8,128)(2,1)S(1)}) custom-call(s32[4]{0:T(128)S(1)} %pad_add_fusion.refs_0_.scalars, bf16[384,384]{1,0:T(8,128)(2,1)S(1)} %get-tuple-element.25.wq, bf16[576,384]{1,0:T(8,128)(2,1)S(1)} %get-tuple-element.28.k, ...), custom_call_target="tpu_custom_call" | custom-call | tf_op jit(solution)/shard_map/pallas_call | solution.py:396
  34.6 0.4 collective-permute-start.15
  35.0 0.1 collective-permute-start.16
  35.1 0.7 collective-permute-start.17
  35.7 0.2 collective-permute-start.18
  35.9 4.2 %collective-permute-done.16.refs_0_ = bf16[2,72,384]{2,1,0:T(8,128)(2,1)S(1)} collective-permute-done((bf16[2,72,384]{2,1,0:T(8,128)(2,1)S(1)}, bf16[2,72,384]{2,1,0:T(8,128)(2,1)S(1)}, u32[]{:S(2)}, u32[]{:S(2)}) %collective-permute-start.16) | collective-permute-done | bytes 110624 | tf_op jit(solution)/shard_map/ppermute | solution.py:422
  40.1 0.0 collective-permute-start.19
  40.1 0.0 collective-permute-done.17.refs_1_
  40.1 0.5 collective-permute-start.20
  40.6 0.0 collective-permute-done.15.refs_1_
  40.6 0.9 %shard_map.63 = (bf16[576,384]{1,0:T(8,128)(2,1)S(1)}, f32[128,384]{1,0:T(8,128)S(1)}, f32[128,384]{1,0:T(8,128)S(1)}, bf16[2,4,48,384]{3,2,1,0:T(8,128)(2,1)S(1)}) custom-call(bf16[384,384]{1,0:T(8,128)(2,1)S(1)} %get-tuple-element.25.wq, bf16[576,384]{1,0:T(8,128)(2,1)S(1)} %get-tuple-element.36.x, bf16[384,384]{1,0:T(8,128)(2,1)S(1)} %get-tuple-element.26.wk, ...), custom_call_target="tpu_custom_call" | custom-call | tf_op jit(solution)/shard_map/pallas_call | solution.py:396
  41.6 0.0 collective-permute-done.20.refs_4_
  41.6 2.3 %shard_map.64 = (bf16[128,384]{1,0:T(8,128)(2,1)S(1)}, bf16[128,384]{1,0:T(8,128)(2,1)S(1)}, bf16[2,4,48,384]{3,2,1,0:T(8,128)(2,1)S(1)}, bf16[2,4,48,384]{3,2,1,0:T(8,128)(2,1)S(1)}) custom-call(s32[4]{0:T(128)S(1)} %pad_add_fusion.refs_0_.scalars, bf16[528,384]{1,0:T(8,128)(2,1)S(1)} %get-tuple-element.34.mine, bf16[576,384]{1,0:T(8,128)(2,1)S(1)} %get-tuple-element.39.q, ...), custom_call_target="tpu_custom_call" | custom-call | tf_op jit(solution)/shard_map/pallas_call | solution.py:396
  43.9 0.4 collective-permute-start.24
  44.3 4.2 %collective-permute-start.21 = (bf16[2,48,384]{2,1,0:T(8,128)(2,1)S(1)}, bf16[2,48,384]{2,1,0:T(8,128)(2,1)S(1)}, u32[]{:S(2)}, u32[]{:S(2)}) collective-permute-start(bf16[2,48,384]{2,1,0:T(8,128)(2,1)S(1)} %get-tuple-element.54), channel_id=1, source_target_pairs={{0,2},{1,3},{2,0},{3,1},{4,6},{5,7},{6,4},{7,5},{8,10},{9,11},{10,... | collective-permute-start | bytes 221192 | tf_op jit(solution)/shard_map/ppermute | solution.py:410
  48.6 2.1 %collective-permute-start.22 = (bf16[2,48,384]{2,1,0:T(8,128)(2,1)S(1)}, bf16[2,48,384]{2,1,0:T(8,128)(2,1)S(1)}, u32[]{:S(2)}, u32[]{:S(2)}) collective-permute-start(bf16[2,48,384]{2,1,0:T(8,128)(2,1)S(1)} %get-tuple-element.56), channel_id=1, source_target_pairs={{0,4},{1,5},{2,6},{3,7},{4,0},{5,1},{6,2},{7,3},{8,12},{9,13},{10,... | collective-permute-start | bytes 221192 | tf_op jit(solution)/shard_map/ppermute | solution.py:410
  50.7 0.0 collective-permute-done.24
  50.7 0.1 add_convert_fusion
  50.8 1.5 %collective-permute-start.25 = (bf16[2,48,384]{2,1,0:T(8,128)(2,1)S(1)}, bf16[2,48,384]{2,1,0:T(8,128)(2,1)S(1)}, u32[]{:S(2)}, u32[]{:S(2)}) collective-permute-start(bf16[2,48,384]{2,1,0:T(8,128)(2,1)S(1)} %get-tuple-element.51), channel_id=1, source_target_pairs={{0,2},{1,3},{2,0},{3,1},{4,6},{5,7},{6,4},{7,5},{8,10},{9,11},{10,... | collective-permute-start | bytes 221192 | tf_op jit(solution)/shard_map/ppermute | solution.py:410
  52.3 2.0 %collective-permute-start.26 = (bf16[2,48,384]{2,1,0:T(8,128)(2,1)S(1)}, bf16[2,48,384]{2,1,0:T(8,128)(2,1)S(1)}, u32[]{:S(2)}, u32[]{:S(2)}) collective-permute-start(bf16[2,48,384]{2,1,0:T(8,128)(2,1)S(1)} %get-tuple-element.53), channel_id=1, source_target_pairs={{0,4},{1,5},{2,6},{3,7},{4,0},{5,1},{6,2},{7,3},{8,12},{9,13},{10,... | collective-permute-start | bytes 221192 | tf_op jit(solution)/shard_map/ppermute | solution.py:410
  54.3 0.0 collective-permute-done.21
  54.4 0.6 collective-permute-start.27
  55.0 1.4 %collective-permute-done.23 = bf16[2,48,384]{2,1,0:T(8,128)(2,1)S(1)} collective-permute-done((bf16[2,48,384]{2,1,0:T(8,128)(2,1)S(1)}, bf16[2,48,384]{2,1,0:T(8,128)(2,1)S(1)}, u32[]{:S(2)}, u32[]{:S(2)}) %collective-permute-start.23) | collective-permute-done | bytes 73760 | tf_op jit(solution)/shard_map/ppermute | solution.py:410
  56.3 0.0 collective-permute-done.25
  56.3 1.1 %collective-permute-done.26 = bf16[2,48,384]{2,1,0:T(8,128)(2,1)S(1)} collective-permute-done((bf16[2,48,384]{2,1,0:T(8,128)(2,1)S(1)}, bf16[2,48,384]{2,1,0:T(8,128)(2,1)S(1)}, u32[]{:S(2)}, u32[]{:S(2)}) %collective-permute-start.26) | collective-permute-done | bytes 73760 | tf_op jit(solution)/shard_map/ppermute | solution.py:410
  57.4 2.2 %collective-permute-done.27 = bf16[2,48,384]{2,1,0:T(8,128)(2,1)S(1)} collective-permute-done((bf16[2,48,384]{2,1,0:T(8,128)(2,1)S(1)}, bf16[2,48,384]{2,1,0:T(8,128)(2,1)S(1)}, u32[]{:S(2)}, u32[]{:S(2)}) %collective-permute-start.27) | collective-permute-done | bytes 73760 | tf_op jit(solution)/shard_map/ppermute | solution.py:410
  59.6 0.1 fusion.1
  59.8 0.1 collective-permute-start.28
  59.8 0.1 collective-permute-start.29
  59.9 4.3 %collective-permute-start.30 = (bf16[48,384]{1,0:T(8,128)(2,1)S(1)}, bf16[48,384]{1,0:T(8,128)(2,1)S(1)}, u32[]{:S(2)}, u32[]{:S(2)}) collective-permute-start(bf16[48,384]{1,0:T(8,128)(2,1)S(1)} %get-tuple-element.49), channel_id=1, source_target_pairs={{0,24},{1,25},{2,26},{3,27},{4,28},{5,29},{6,30},{7,31},{8,16},{9,... | collective-permute-start | bytes 110600 | tf_op jit(solution)/shard_map/ppermute | solution.py:410
  64.2 1.2 %shard_map.65 = bf16[8,16,384]{2,1,0:T(8,128)(2,1)} custom-call(bf16[8,16,384]{2,1,0:T(8,128)(2,1)S(1)} %copy-done, bf16[384,384]{1,0:T(8,128)(2,1)S(1)} %get-tuple-element.25.wq, bf16[384,384]{1,0:T(8,128)(2,1)S(1)} %get-tuple-element.26.wk, bf16[384,384]{1,0:T(8,128)(2,1)S(1)} %get-tuple-element.27.wv, bf16[128,384]{1,0:T(8,128)(2,1)S(1)} %get-tuple-element.35.gq, ...), custom_call_target="tpu_custom_call" | custom-call | tf_op jit(solution)/shard_map/pallas_call | solution.py:396
  65.4 0.0 collective-permute-done.28
  65.4 0.0 collective-permute-done.29
  65.4 1.2 %collective-permute-done.30 = bf16[48,384]{1,0:T(8,128)(2,1)S(1)} collective-permute-done((bf16[48,384]{1,0:T(8,128)(2,1)S(1)}, bf16[48,384]{1,0:T(8,128)(2,1)S(1)}, u32[]{:S(2)}, u32[]{:S(2)}) %collective-permute-start.30) | collective-permute-done | bytes 36896 | tf_op jit(solution)/shard_map/ppermute | solution.py:410
  66.6 0.6 reshape.18
  (20 shorter events, 0.2 us)
Async XLA Ops:
  0.6 4.8 %copy-start.1 = (bf16[18432]{0:T(1024)(128)(2,1)S(1)}, bf16[18432]{0:T(1024)(128)(2,1)}, u32[]{:S(2)}) copy-start(bf16[18432]{0:T(1024)(128)(2,1)} %param.7) | copy-start | bytes 110596
  1.7 19.9 %collective-permute-start.10 = (bf16[2,72,384]{2,1,0:T(8,128)(2,1)S(1)}, bf16[2,72,384]{2,1,0:T(8,128)(2,1)S(1)}, u32[]{:S(2)}, u32[]{:S(2)}) collective-permute-start(bf16[2,72,384]{2,1,0:T(8,128)(2,1)S(1)} %shard_map.60.refs_11_), channel_id=1, source_target_pairs={{0,2},{2,0},{4,6},{6,4},{8,10},{10,8},{12,14},{14,12},{16,18},{18,... | collective-permute-start | bytes 331784 | tf_op jit(solution)/shard_map/ppermute | solution.py:422
  4.8 16.9 %collective-permute-start.11 = (bf16[2,72,384]{2,1,0:T(8,128)(2,1)S(1)}, bf16[2,72,384]{2,1,0:T(8,128)(2,1)S(1)}, u32[]{:S(2)}, u32[]{:S(2)}) collective-permute-start(bf16[2,72,384]{2,1,0:T(8,128)(2,1)S(1)} %shard_map.60.refs_11_), channel_id=1, source_target_pairs={{2,4},{4,2},{6,8},{8,6},{10,12},{12,10},{14,16},{16,14},{18,20},{2... | collective-permute-start | bytes 331784 | tf_op jit(solution)/shard_map/ppermute | solution.py:423
  5.5 7.8 %collective-permute-start = (bf16[1,48,384]{2,1,0:T(8,128)(2,1)S(1)}, bf16[1,48,384]{2,1,0:T(8,128)(2,1)S(1)}, u32[]{:S(2)}, u32[]{:S(2)}) collective-permute-start(bf16[1,48,384]{2,1,0:T(8,128)(2,1)S(1)} %reshape.17.refs_0_), channel_id=1, source_target_pairs={{0,8},{1,9},{2,10},{3,11},{4,12},{5,13},{6,14},{7,15},{8,0},{9,1},... | collective-permute-start | bytes 110600 | tf_op jit(solution)/shard_map/ppermute | solution.py:410
  9.7 5.2 %collective-permute-start.1 = (bf16[1,48,384]{2,1,0:T(8,128)(2,1)S(1)}, bf16[1,48,384]{2,1,0:T(8,128)(2,1)S(1)}, u32[]{:S(2)}, u32[]{:S(2)}) collective-permute-start(bf16[1,48,384]{2,1,0:T(8,128)(2,1)S(1)} %reshape.17.refs_0_), channel_id=1, source_target_pairs={{0,16},{1,17},{2,18},{3,19},{4,20},{5,21},{6,22},{7,23},{8,24},{9,... | collective-permute-start | bytes 110600 | tf_op jit(solution)/shard_map/ppermute | solution.py:410
  12.3 5.8 %collective-permute-start.2 = (bf16[1,48,384]{2,1,0:T(8,128)(2,1)S(1)}, bf16[1,48,384]{2,1,0:T(8,128)(2,1)S(1)}, u32[]{:S(2)}, u32[]{:S(2)}) collective-permute-start(bf16[1,48,384]{2,1,0:T(8,128)(2,1)S(1)} %reshape.17.refs_0_), channel_id=1, source_target_pairs={{0,24},{1,25},{2,26},{3,27},{4,28},{5,29},{6,30},{7,31},{8,16},{9,... | collective-permute-start | bytes 110600 | tf_op jit(solution)/shard_map/ppermute | solution.py:410
  18.1 10.4 %copy-start = (bf16[8,16,384]{2,1,0:T(8,128)(2,1)S(1)}, bf16[8,16,384]{2,1,0:T(8,128)(2,1)}, u32[]{:S(2)}) copy-start(bf16[8,16,384]{2,1,0:T(8,128)(2,1)} %tokens.3) | copy-start | bytes 294916
  18.1 5.9 %collective-permute-start.4 = (bf16[4,48,384]{2,1,0:T(8,128)(2,1)S(1)}, bf16[4,48,384]{2,1,0:T(8,128)(2,1)S(1)}, u32[]{:S(2)}, u32[]{:S(2)}) collective-permute-start(bf16[4,48,384]{2,1,0:T(8,128)(2,1)S(1)} %shard_map.59.refs_3_), channel_id=1, source_target_pairs={{0,2},{1,3},{2,0},{3,1},{4,6},{5,7},{6,4},{7,5},{8,10},{9,11},{10,... | collective-permute-start | bytes 442376 | tf_op jit(solution)/shard_map/ppermute | solution.py:410
  19.8 6.7 %collective-permute-start.6 = (bf16[4,48,384]{2,1,0:T(8,128)(2,1)S(1)}, bf16[4,48,384]{2,1,0:T(8,128)(2,1)S(1)}, u32[]{:S(2)}, u32[]{:S(2)}) collective-permute-start(bf16[4,48,384]{2,1,0:T(8,128)(2,1)S(1)} %shard_map.59.refs_3_), channel_id=1, source_target_pairs={{0,4},{1,5},{2,6},{3,7},{4,0},{5,1},{6,2},{7,3},{8,12},{9,13},{10,... | collective-permute-start | bytes 442376 | tf_op jit(solution)/shard_map/ppermute | solution.py:410
  19.8 6.7 %collective-permute-start.8 = (bf16[4,48,384]{2,1,0:T(8,128)(2,1)S(1)}, bf16[4,48,384]{2,1,0:T(8,128)(2,1)S(1)}, u32[]{:S(2)}, u32[]{:S(2)}) collective-permute-start(bf16[4,48,384]{2,1,0:T(8,128)(2,1)S(1)} %shard_map.59.refs_3_), channel_id=1, source_target_pairs={{0,6},{1,7},{2,4},{3,5},{4,2},{5,3},{6,0},{7,1},{8,14},{9,15},{10,... | collective-permute-start | bytes 442376 | tf_op jit(solution)/shard_map/ppermute | solution.py:410
  21.7 5.4 %collective-permute-start.3 = (bf16[4,48,384]{2,1,0:T(8,128)(2,1)S(1)}, bf16[4,48,384]{2,1,0:T(8,128)(2,1)S(1)}, u32[]{:S(2)}, u32[]{:S(2)}) collective-permute-start(bf16[4,48,384]{2,1,0:T(8,128)(2,1)S(1)} %shard_map.59.refs_3_), channel_id=1, source_target_pairs={{0,1},{1,0},{2,3},{3,2},{4,5},{5,4},{6,7},{7,6},{8,9},{9,8},{10,11... | collective-permute-start | bytes 442376 | tf_op jit(solution)/shard_map/ppermute | solution.py:410
  21.7 5.3 %collective-permute-start.12 = (bf16[2,72,384]{2,1,0:T(8,128)(2,1)S(1)}, bf16[2,72,384]{2,1,0:T(8,128)(2,1)S(1)}, u32[]{:S(2)}, u32[]{:S(2)}) collective-permute-start(bf16[2,72,384]{2,1,0:T(8,128)(2,1)S(1)} %shard_map.60.refs_11_), channel_id=1, source_target_pairs={{0,1},{1,0},{2,3},{3,2},{4,5},{5,4},{6,7},{7,6},{8,9},{9,8},{10,11... | collective-permute-start | bytes 331784 | tf_op jit(solution)/shard_map/ppermute | solution.py:431
  24.0 4.5 %collective-permute-start.5 = (bf16[4,48,384]{2,1,0:T(8,128)(2,1)S(1)}, bf16[4,48,384]{2,1,0:T(8,128)(2,1)S(1)}, u32[]{:S(2)}, u32[]{:S(2)}) collective-permute-start(bf16[4,48,384]{2,1,0:T(8,128)(2,1)S(1)} %collective-permute-done.4.refs_5_), channel_id=1, source_target_pairs={{0,1},{1,0},{2,3},{3,2},{4,5},{5,4},{6,7},{7,6},{8,9},{9,8},{10,11... | collective-permute-start | bytes 442376 | tf_op jit(solution)/shard_map/ppermute | solution.py:410
  26.5 2.0 %collective-permute-start.7 = (bf16[4,48,384]{2,1,0:T(8,128)(2,1)S(1)}, bf16[4,48,384]{2,1,0:T(8,128)(2,1)S(1)}, u32[]{:S(2)}, u32[]{:S(2)}) collective-permute-start(bf16[4,48,384]{2,1,0:T(8,128)(2,1)S(1)} %collective-permute-done.6.refs_7_), channel_id=1, source_target_pairs={{0,1},{1,0},{2,3},{3,2},{4,5},{5,4},{6,7},{7,6},{8,9},{9,8},{10,11... | collective-permute-start | bytes 442376 | tf_op jit(solution)/shard_map/ppermute | solution.py:410
  26.5 2.0 %collective-permute-start.9 = (bf16[4,48,384]{2,1,0:T(8,128)(2,1)S(1)}, bf16[4,48,384]{2,1,0:T(8,128)(2,1)S(1)}, u32[]{:S(2)}, u32[]{:S(2)}) collective-permute-start(bf16[4,48,384]{2,1,0:T(8,128)(2,1)S(1)} %collective-permute-done.8.refs_9_), channel_id=1, source_target_pairs={{0,1},{1,0},{2,3},{3,2},{4,5},{5,4},{6,7},{7,6},{8,9},{9,8},{10,11... | collective-permute-start | bytes 442376 | tf_op jit(solution)/shard_map/ppermute | solution.py:410
  27.0 1.3 %collective-permute-start.13 = (bf16[2,72,384]{2,1,0:T(8,128)(2,1)S(1)}, bf16[2,72,384]{2,1,0:T(8,128)(2,1)S(1)}, u32[]{:S(2)}, u32[]{:S(2)}) collective-permute-start(bf16[2,72,384]{2,1,0:T(8,128)(2,1)S(1)} %collective-permute-done.10.refs_12_), channel_id=1, source_target_pairs={{0,1},{1,0},{2,3},{3,2},{4,5},{5,4},{6,7},{7,6},{8,9},{9,8},{10,11... | collective-permute-start | bytes 331784 | tf_op jit(solution)/shard_map/ppermute | solution.py:431
  27.1 1.4 %collective-permute-start.14 = (bf16[2,72,384]{2,1,0:T(8,128)(2,1)S(1)}, bf16[2,72,384]{2,1,0:T(8,128)(2,1)S(1)}, u32[]{:S(2)}, u32[]{:S(2)}) collective-permute-start(bf16[2,72,384]{2,1,0:T(8,128)(2,1)S(1)} %collective-permute-done.11.refs_13_), channel_id=1, source_target_pairs={{0,1},{1,0},{2,3},{3,2},{4,5},{5,4},{6,7},{7,6},{8,9},{9,8},{10,11... | collective-permute-start | bytes 331784 | tf_op jit(solution)/shard_map/ppermute | solution.py:431
  34.6 6.1 %collective-permute-start.15 = (bf16[2,4,48,384]{3,2,1,0:T(8,128)(2,1)S(1)}, bf16[2,4,48,384]{3,2,1,0:T(8,128)(2,1)S(1)}, u32[]{:S(2)}, u32[]{:S(2)}) collective-permute-start(bf16[2,4,48,384]{3,2,1,0:T(8,128)(2,1)S(1)} %get-tuple-element.38), channel_id=1, source_target_pairs={{0,1},{1,0},{2,3},{3,2},{4,5},{5,4},{6,7},{7,6},{8,9},{9,8},{10,11... | collective-permute-start | bytes 884744 | tf_op jit(solution)/shard_map/ppermute | solution.py:410
  35.0 5.1 %collective-permute-start.16 = (bf16[2,72,384]{2,1,0:T(8,128)(2,1)S(1)}, bf16[2,72,384]{2,1,0:T(8,128)(2,1)S(1)}, u32[]{:S(2)}, u32[]{:S(2)}) collective-permute-start(bf16[2,72,384]{2,1,0:T(8,128)(2,1)S(1)} %get-tuple-element.42), channel_id=1, source_target_pairs={{0,2},{2,0},{4,6},{6,4},{8,10},{10,8},{12,14},{14,12},{16,18},{18,... | collective-permute-start | bytes 331784 | tf_op jit(solution)/shard_map/ppermute | solution.py:422
  35.1 5.1 %collective-permute-start.17 = (bf16[2,72,384]{2,1,0:T(8,128)(2,1)S(1)}, bf16[2,72,384]{2,1,0:T(8,128)(2,1)S(1)}, u32[]{:S(2)}, u32[]{:S(2)}) collective-permute-start(bf16[2,72,384]{2,1,0:T(8,128)(2,1)S(1)} %get-tuple-element.42), channel_id=1, source_target_pairs={{2,4},{4,2},{6,8},{8,6},{10,12},{12,10},{14,16},{16,14},{18,20},{2... | collective-permute-start | bytes 331784 | tf_op jit(solution)/shard_map/ppermute | solution.py:423
  35.7 5.8 %collective-permute-start.18 = (bf16[2,72,384]{2,1,0:T(8,128)(2,1)S(1)}, bf16[2,72,384]{2,1,0:T(8,128)(2,1)S(1)}, u32[]{:S(2)}, u32[]{:S(2)}) collective-permute-start(bf16[2,72,384]{2,1,0:T(8,128)(2,1)S(1)} %get-tuple-element.42), channel_id=1, source_target_pairs={{0,1},{1,0},{2,3},{3,2},{4,5},{5,4},{6,7},{7,6},{8,9},{9,8},{10,11... | collective-permute-start | bytes 331784 | tf_op jit(solution)/shard_map/ppermute | solution.py:431
  40.1 1.5 %collective-permute-start.19 = (bf16[2,72,384]{2,1,0:T(8,128)(2,1)S(1)}, bf16[2,72,384]{2,1,0:T(8,128)(2,1)S(1)}, u32[]{:S(2)}, u32[]{:S(2)}) collective-permute-start(bf16[2,72,384]{2,1,0:T(8,128)(2,1)S(1)} %collective-permute-done.16.refs_0_), channel_id=1, source_target_pairs={{0,1},{1,0},{2,3},{3,2},{4,5},{5,4},{6,7},{7,6},{8,9},{9,8},{10,11... | collective-permute-start | bytes 331784 | tf_op jit(solution)/shard_map/ppermute | solution.py:431
  40.1 1.5 %collective-permute-start.20 = (bf16[2,72,384]{2,1,0:T(8,128)(2,1)S(1)}, bf16[2,72,384]{2,1,0:T(8,128)(2,1)S(1)}, u32[]{:S(2)}, u32[]{:S(2)}) collective-permute-start(bf16[2,72,384]{2,1,0:T(8,128)(2,1)S(1)} %collective-permute-done.17.refs_1_), channel_id=1, source_target_pairs={{0,1},{1,0},{2,3},{3,2},{4,5},{5,4},{6,7},{7,6},{8,9},{9,8},{10,11... | collective-permute-start | bytes 331784 | tf_op jit(solution)/shard_map/ppermute | solution.py:431
  43.9 6.8 %collective-permute-start.24 = (bf16[2,4,48,384]{3,2,1,0:T(8,128)(2,1)S(1)}, bf16[2,4,48,384]{3,2,1,0:T(8,128)(2,1)S(1)}, u32[]{:S(2)}, u32[]{:S(2)}) collective-permute-start(bf16[2,4,48,384]{3,2,1,0:T(8,128)(2,1)S(1)} %get-tuple-element.47), channel_id=1, source_target_pairs={{0,1},{1,0},{2,3},{3,2},{4,5},{5,4},{6,7},{7,6},{8,9},{9,8},{10,11... | collective-permute-start | bytes 884744 | tf_op jit(solution)/shard_map/ppermute | solution.py:410
  44.3 10.0 %collective-permute-start.21 = (bf16[2,48,384]{2,1,0:T(8,128)(2,1)S(1)}, bf16[2,48,384]{2,1,0:T(8,128)(2,1)S(1)}, u32[]{:S(2)}, u32[]{:S(2)}) collective-permute-start(bf16[2,48,384]{2,1,0:T(8,128)(2,1)S(1)} %get-tuple-element.54), channel_id=1, source_target_pairs={{0,2},{1,3},{2,0},{3,1},{4,6},{5,7},{6,4},{7,5},{8,10},{9,11},{10,... | collective-permute-start | bytes 221192 | tf_op jit(solution)/shard_map/ppermute | solution.py:410
  48.6 6.4 %collective-permute-start.22 = (bf16[2,48,384]{2,1,0:T(8,128)(2,1)S(1)}, bf16[2,48,384]{2,1,0:T(8,128)(2,1)S(1)}, u32[]{:S(2)}, u32[]{:S(2)}) collective-permute-start(bf16[2,48,384]{2,1,0:T(8,128)(2,1)S(1)} %get-tuple-element.56), channel_id=1, source_target_pairs={{0,4},{1,5},{2,6},{3,7},{4,0},{5,1},{6,2},{7,3},{8,12},{9,13},{10,... | collective-permute-start | bytes 221192 | tf_op jit(solution)/shard_map/ppermute | solution.py:410
  50.7 5.7 %collective-permute-start.23 = (bf16[2,48,384]{2,1,0:T(8,128)(2,1)S(1)}, bf16[2,48,384]{2,1,0:T(8,128)(2,1)S(1)}, u32[]{:S(2)}, u32[]{:S(2)}) collective-permute-start(bf16[2,48,384]{2,1,0:T(8,128)(2,1)S(1)} %get-tuple-element.55), channel_id=1, source_target_pairs={{0,6},{1,7},{2,4},{3,5},{4,2},{5,3},{6,0},{7,1},{8,14},{9,15},{10,... | collective-permute-start | bytes 221192 | tf_op jit(solution)/shard_map/ppermute | solution.py:410
  50.8 5.5 %collective-permute-start.25 = (bf16[2,48,384]{2,1,0:T(8,128)(2,1)S(1)}, bf16[2,48,384]{2,1,0:T(8,128)(2,1)S(1)}, u32[]{:S(2)}, u32[]{:S(2)}) collective-permute-start(bf16[2,48,384]{2,1,0:T(8,128)(2,1)S(1)} %get-tuple-element.51), channel_id=1, source_target_pairs={{0,2},{1,3},{2,0},{3,1},{4,6},{5,7},{6,4},{7,5},{8,10},{9,11},{10,... | collective-permute-start | bytes 221192 | tf_op jit(solution)/shard_map/ppermute | solution.py:410
  52.3 5.1 %collective-permute-start.26 = (bf16[2,48,384]{2,1,0:T(8,128)(2,1)S(1)}, bf16[2,48,384]{2,1,0:T(8,128)(2,1)S(1)}, u32[]{:S(2)}, u32[]{:S(2)}) collective-permute-start(bf16[2,48,384]{2,1,0:T(8,128)(2,1)S(1)} %get-tuple-element.53), channel_id=1, source_target_pairs={{0,4},{1,5},{2,6},{3,7},{4,0},{5,1},{6,2},{7,3},{8,12},{9,13},{10,... | collective-permute-start | bytes 221192 | tf_op jit(solution)/shard_map/ppermute | solution.py:410
  54.4 5.3 %collective-permute-start.27 = (bf16[2,48,384]{2,1,0:T(8,128)(2,1)S(1)}, bf16[2,48,384]{2,1,0:T(8,128)(2,1)S(1)}, u32[]{:S(2)}, u32[]{:S(2)}) collective-permute-start(bf16[2,48,384]{2,1,0:T(8,128)(2,1)S(1)} %get-tuple-element.52), channel_id=1, source_target_pairs={{0,6},{1,7},{2,4},{3,5},{4,2},{5,3},{6,0},{7,1},{8,14},{9,15},{10,... | collective-permute-start | bytes 221192 | tf_op jit(solution)/shard_map/ppermute | solution.py:410
  59.8 5.6 %collective-permute-start.28 = (bf16[48,384]{1,0:T(8,128)(2,1)S(1)}, bf16[48,384]{1,0:T(8,128)(2,1)S(1)}, u32[]{:S(2)}, u32[]{:S(2)}) collective-permute-start(bf16[48,384]{1,0:T(8,128)(2,1)S(1)} %get-tuple-element.48), channel_id=1, source_target_pairs={{0,8},{1,9},{2,10},{3,11},{4,12},{5,13},{6,14},{7,15},{8,0},{9,1},... | collective-permute-start | bytes 110600 | tf_op jit(solution)/shard_map/ppermute | solution.py:410
  59.8 5.5 %collective-permute-start.29 = (bf16[48,384]{1,0:T(8,128)(2,1)S(1)}, bf16[48,384]{1,0:T(8,128)(2,1)S(1)}, u32[]{:S(2)}, u32[]{:S(2)}) collective-permute-start(bf16[48,384]{1,0:T(8,128)(2,1)S(1)} %get-tuple-element.50), channel_id=1, source_target_pairs={{0,16},{1,17},{2,18},{3,19},{4,20},{5,21},{6,22},{7,23},{8,24},{9,... | collective-permute-start | bytes 110600 | tf_op jit(solution)/shard_map/ppermute | solution.py:410
  59.9 6.6 %collective-permute-start.30 = (bf16[48,384]{1,0:T(8,128)(2,1)S(1)}, bf16[48,384]{1,0:T(8,128)(2,1)S(1)}, u32[]{:S(2)}, u32[]{:S(2)}) collective-permute-start(bf16[48,384]{1,0:T(8,128)(2,1)S(1)} %get-tuple-element.49), channel_id=1, source_target_pairs={{0,24},{1,25},{2,26},{3,27},{4,28},{5,29},{6,30},{7,31},{8,16},{9,... | collective-permute-start | bytes 110600 | tf_op jit(solution)/shard_map/ppermute | solution.py:410

commit v6 on v5

--- a/solution.py
+++ b/solution.py
@@ -195,10 +195,10 @@
         x_out[n * PER : (n + 1) * PER, :] = tile[0:PER, :]
         flag_rows.append(tile[PER:BLK, :].astype(F32)[0:1, 0:PER])
     x = x_out[...]
-    k_normal, _ = head_normalise(dot(x, wk_out[...]), ones, width)
+    k_normal, _ = head_normalise(dot(x, w_scr[1]), ones, width)
     keys = k_normal.astype(BF16)
-    values = dot(x, wv_out[...]).astype(BF16)
-    q_normal, _ = head_normalise(dot(x[0:own], wq_out[...]), ones, width)
+    values = dot(x, w_scr[2]).astype(BF16)
+    q_normal, _ = head_normalise(dot(x[0:own], w_scr[0]), ones, width)
     queries = q_normal.astype(BF16)
     k_out[...] = keys
     v_out[...] = values

time: 67.4 us -> 67.4 us (level)
  no operation moved by 1% of the time
where the time goes in v6:
time: 67.4 us; the launch traced here: 67.2 us
  starting transfers between devices  32.8 us (49%)
  waiting for transfers between devices  21 us (31%)
  Pallas kernels  11.5 us (17%)
  between operations  0.82 us (1%)
  local copies, waits for them, and re-layouts  0.78 us (1%)
    ppermute x21, starting transfers between devices, swap(): return lax.ppermute(value, AXES, [(i, i ^ mask) for i in range(count)])  26.7 us
    ppermute x21, waiting for transfers between devices, swap(): return lax.ppermute(value, AXES, [(i, i ^ mask) for i in range(count)])  15.9 us
    pallas_call x7, Pallas kernels, call(): pl.pallas_call(kernel, out_shape=[pltpu.VMEM(s, t) if n < kept else jax.S...  11.5 us
    ppermute x2, waiting for transfers between devices, beside(): near = lax.ppermute(strip, 'rows', side_pairs(rows, 0))  4.23 us
    ppermute x2, starting transfers between devices, beside(): near = lax.ppermute(strip, 'rows', side_pairs(rows, 0))  3.11 us
    ppermute x6, starting transfers between devices, across(): sides.append(lax.ppermute(strip, 'cols', side_pairs(cols, n)))  1.68 us
  transfers between devices with their start and end apart: 31, of which 12 were waited for; matrix products, arithmetic and copies ran while one was open for 0% of the time, Pallas kernels for 3%

profile of v6, /device:TPU:0, one launch (start us, length us, event | category | flops | bytes accessed | tf_op | source)
XLA Modules:
  0.0 67.2 jit_solution(7285049742513809948)
XLA Ops:
  0.6 1.1 %shard_map.60.refs_11_ = bf16[2,72,384]{2,1,0:T(8,128)(2,1)S(1)} custom-call(s32[1,2]{1,0:T(1,128)} %tissue.1, bf16[8,16,384]{2,1,0:T(8,128)(2,1)} %tokens.3), custom_call_target="tpu_custom_call" | custom-call | tf_op jit(solution)/shard_map/pallas_call | solution.py:396
  1.7 3.0 %collective-permute-start.10 = (bf16[2,72,384]{2,1,0:T(8,128)(2,1)S(1)}, bf16[2,72,384]{2,1,0:T(8,128)(2,1)S(1)}, u32[]{:S(2)}, u32[]{:S(2)}) collective-permute-start(bf16[2,72,384]{2,1,0:T(8,128)(2,1)S(1)} %shard_map.60.refs_11_), channel_id=1, source_target_pairs={{0,2},{2,0},{4,6},{6,4},{8,10},{10,8},{12,14},{14,12},{16,18},{18,... | collective-permute-start | bytes 331784 | tf_op jit(solution)/shard_map/ppermute | solution.py:422
  4.8 0.7 collective-permute-start.11
  5.5 4.3 %collective-permute-start = (bf16[1,48,384]{2,1,0:T(8,128)(2,1)S(1)}, bf16[1,48,384]{2,1,0:T(8,128)(2,1)S(1)}, u32[]{:S(2)}, u32[]{:S(2)}) collective-permute-start(bf16[1,48,384]{2,1,0:T(8,128)(2,1)S(1)} %reshape.17.refs_0_), channel_id=1, source_target_pairs={{0,8},{1,9},{2,10},{3,11},{4,12},{5,13},{6,14},{7,15},{8,0},{9,1},... | collective-permute-start | bytes 110600 | tf_op jit(solution)/shard_map/ppermute | solution.py:410
  9.7 2.6 %collective-permute-start.1 = (bf16[1,48,384]{2,1,0:T(8,128)(2,1)S(1)}, bf16[1,48,384]{2,1,0:T(8,128)(2,1)S(1)}, u32[]{:S(2)}, u32[]{:S(2)}) collective-permute-start(bf16[1,48,384]{2,1,0:T(8,128)(2,1)S(1)} %reshape.17.refs_0_), channel_id=1, source_target_pairs={{0,16},{1,17},{2,18},{3,19},{4,20},{5,21},{6,22},{7,23},{8,24},{9,... | collective-permute-start | bytes 110600 | tf_op jit(solution)/shard_map/ppermute | solution.py:410
  12.3 0.0 collective-permute-start.2
  12.3 1.0 %collective-permute-done.refs_1_ = bf16[1,48,384]{2,1,0:T(8,128)(2,1)S(1)} collective-permute-done((bf16[1,48,384]{2,1,0:T(8,128)(2,1)S(1)}, bf16[1,48,384]{2,1,0:T(8,128)(2,1)S(1)}, u32[]{:S(2)}, u32[]{:S(2)}) %collective-permute-start) | collective-permute-done | bytes 36896 | tf_op jit(solution)/shard_map/ppermute | solution.py:410
  13.3 1.6 %collective-permute-done.1.refs_2_ = bf16[1,48,384]{2,1,0:T(8,128)(2,1)S(1)} collective-permute-done((bf16[1,48,384]{2,1,0:T(8,128)(2,1)S(1)}, bf16[1,48,384]{2,1,0:T(8,128)(2,1)S(1)}, u32[]{:S(2)}, u32[]{:S(2)}) %collective-permute-start.1) | collective-permute-done | bytes 36896 | tf_op jit(solution)/shard_map/ppermute | solution.py:410
  14.9 3.2 %collective-permute-done.2.refs_3_ = bf16[1,48,384]{2,1,0:T(8,128)(2,1)S(1)} collective-permute-done((bf16[1,48,384]{2,1,0:T(8,128)(2,1)S(1)}, bf16[1,48,384]{2,1,0:T(8,128)(2,1)S(1)}, u32[]{:S(2)}, u32[]{:S(2)}) %collective-permute-start.2) | collective-permute-done | bytes 36896 | tf_op jit(solution)/shard_map/ppermute | solution.py:410
  18.1 1.7 %collective-permute-start.4 = (bf16[4,48,384]{2,1,0:T(8,128)(2,1)S(1)}, bf16[4,48,384]{2,1,0:T(8,128)(2,1)S(1)}, u32[]{:S(2)}, u32[]{:S(2)}) collective-permute-start(bf16[4,48,384]{2,1,0:T(8,128)(2,1)S(1)} %shard_map.59.refs_3_), channel_id=1, source_target_pairs={{0,2},{1,3},{2,0},{3,1},{4,6},{5,7},{6,4},{7,5},{8,10},{9,11},{10,... | collective-permute-start | bytes 442376 | tf_op jit(solution)/shard_map/ppermute | solution.py:410
  19.8 0.0 collective-permute-start.6
  19.8 1.9 %collective-permute-start.8 = (bf16[4,48,384]{2,1,0:T(8,128)(2,1)S(1)}, bf16[4,48,384]{2,1,0:T(8,128)(2,1)S(1)}, u32[]{:S(2)}, u32[]{:S(2)}) collective-permute-start(bf16[4,48,384]{2,1,0:T(8,128)(2,1)S(1)} %shard_map.59.refs_3_), channel_id=1, source_target_pairs={{0,6},{1,7},{2,4},{3,5},{4,2},{5,3},{6,0},{7,1},{8,14},{9,15},{10,... | collective-permute-start | bytes 442376 | tf_op jit(solution)/shard_map/ppermute | solution.py:410
  21.7 0.0 collective-permute-done.10.refs_12_
  21.7 0.0 collective-permute-start.3
  21.7 0.0 collective-permute-done.11.refs_13_
  21.7 0.5 collective-permute-start.12
  22.2 1.8 %collective-permute-done.4.refs_5_ = bf16[4,48,384]{2,1,0:T(8,128)(2,1)S(1)} collective-permute-done((bf16[4,48,384]{2,1,0:T(8,128)(2,1)S(1)}, bf16[4,48,384]{2,1,0:T(8,128)(2,1)S(1)}, u32[]{:S(2)}, u32[]{:S(2)}) %collective-permute-start.4) | collective-permute-done | bytes 147488 | tf_op jit(solution)/shard_map/ppermute | solution.py:410
  24.0 0.0 collective-permute-start.5
  24.0 2.5 %collective-permute-done.6.refs_7_ = bf16[4,48,384]{2,1,0:T(8,128)(2,1)S(1)} collective-permute-done((bf16[4,48,384]{2,1,0:T(8,128)(2,1)S(1)}, bf16[4,48,384]{2,1,0:T(8,128)(2,1)S(1)}, u32[]{:S(2)}, u32[]{:S(2)}) %collective-permute-start.6) | collective-permute-done | bytes 147488 | tf_op jit(solution)/shard_map/ppermute | solution.py:410
  26.5 0.0 collective-permute-start.7
  26.5 0.5 collective-permute-start.9
  27.0 0.1 collective-permute-start.13
  27.1 0.4 collective-permute-start.14
  27.5 0.1 pad_add_fusion.refs_0_.scalars
  27.6 0.7 %collective-permute-done.13.refs_15_ = bf16[2,72,384]{2,1,0:T(8,128)(2,1)S(1)} collective-permute-done((bf16[2,72,384]{2,1,0:T(8,128)(2,1)S(1)}, bf16[2,72,384]{2,1,0:T(8,128)(2,1)S(1)}, u32[]{:S(2)}, u32[]{:S(2)}) %collective-permute-start.13) | collective-permute-done | bytes 110624 | tf_op jit(solution)/shard_map/ppermute | solution.py:431
  28.3 0.2 collective-permute-done.14.refs_16_
  28.5 0.0 collective-permute-done.7.refs_8_
  28.5 0.0 collective-permute-done.9.refs_10_
  28.5 3.6 %shard_map.61 = (bf16[384,384]{1,0:T(8,128)(2,1)S(1)}, bf16[384,384]{1,0:T(8,128)(2,1)S(1)}, bf16[384,384]{1,0:T(8,128)(2,1)S(1)}, bf16[576,384]{1,0:T(8,128)(2,...) custom-call(s32[4]{0:T(128)S(1)} %pad_add_fusion.refs_0_.scalars, ...), custom_call_target="tpu_custom_call" | custom-call | tf_op jit(solution)/shard_map/pallas_call | solution.py:396
  32.1 2.4 %shard_map.62 = (bf16[128,384]{1,0:T(8,128)(2,1)S(1)}, bf16[2,4,48,384]{3,2,1,0:T(8,128)(2,1)S(1)}, bf16[2,4,48,384]{3,2,1,0:T(8,128)(2,1)S(1)}) custom-call(s32[4]{0:T(128)S(1)} %pad_add_fusion.refs_0_.scalars, bf16[384,384]{1,0:T(8,128)(2,1)S(1)} %get-tuple-element.25.wq, bf16[576,384]{1,0:T(8,128)(2,1)S(1)} %get-tuple-element.28.k, ...), custom_call_target="tpu_custom_call" | custom-call | tf_op jit(solution)/shard_map/pallas_call | solution.py:396
  34.6 0.4 collective-permute-start.15
  35.0 0.1 collective-permute-start.16
  35.1 0.7 collective-permute-start.17
  35.8 0.2 collective-permute-start.18
  35.9 4.2 %collective-permute-done.16.refs_0_ = bf16[2,72,384]{2,1,0:T(8,128)(2,1)S(1)} collective-permute-done((bf16[2,72,384]{2,1,0:T(8,128)(2,1)S(1)}, bf16[2,72,384]{2,1,0:T(8,128)(2,1)S(1)}, u32[]{:S(2)}, u32[]{:S(2)}) %collective-permute-start.16) | collective-permute-done | bytes 110624 | tf_op jit(solution)/shard_map/ppermute | solution.py:422
  40.1 0.0 collective-permute-start.19
  40.1 0.0 collective-permute-done.17.refs_1_
  40.1 0.5 collective-permute-start.20
  40.7 0.0 collective-permute-done.15.refs_1_
  40.7 0.9 %shard_map.63 = (bf16[576,384]{1,0:T(8,128)(2,1)S(1)}, f32[128,384]{1,0:T(8,128)S(1)}, f32[128,384]{1,0:T(8,128)S(1)}, bf16[2,4,48,384]{3,2,1,0:T(8,128)(2,1)S(1)}) custom-call(bf16[384,384]{1,0:T(8,128)(2,1)S(1)} %get-tuple-element.25.wq, bf16[576,384]{1,0:T(8,128)(2,1)S(1)} %get-tuple-element.36.x, bf16[384,384]{1,0:T(8,128)(2,1)S(1)} %get-tuple-element.26.wk, ...), custom_call_target="tpu_custom_call" | custom-call | tf_op jit(solution)/shard_map/pallas_call | solution.py:396
  41.6 0.0 collective-permute-done.19.refs_3_
  41.6 0.0 collective-permute-done.20.refs_4_
  41.6 2.3 %shard_map.64 = (bf16[128,384]{1,0:T(8,128)(2,1)S(1)}, bf16[128,384]{1,0:T(8,128)(2,1)S(1)}, bf16[2,4,48,384]{3,2,1,0:T(8,128)(2,1)S(1)}, bf16[2,4,48,384]{3,2,1,0:T(8,128)(2,1)S(1)}) custom-call(s32[4]{0:T(128)S(1)} %pad_add_fusion.refs_0_.scalars, bf16[528,384]{1,0:T(8,128)(2,1)S(1)} %get-tuple-element.34.mine, bf16[576,384]{1,0:T(8,128)(2,1)S(1)} %get-tuple-element.39.q, ...), custom_call_target="tpu_custom_call" | custom-call | tf_op jit(solution)/shard_map/pallas_call | solution.py:396
  43.9 0.4 collective-permute-start.24
  44.4 4.2 %collective-permute-start.21 = (bf16[2,48,384]{2,1,0:T(8,128)(2,1)S(1)}, bf16[2,48,384]{2,1,0:T(8,128)(2,1)S(1)}, u32[]{:S(2)}, u32[]{:S(2)}) collective-permute-start(bf16[2,48,384]{2,1,0:T(8,128)(2,1)S(1)} %get-tuple-element.54), channel_id=1, source_target_pairs={{0,2},{1,3},{2,0},{3,1},{4,6},{5,7},{6,4},{7,5},{8,10},{9,11},{10,... | collective-permute-start | bytes 221192 | tf_op jit(solution)/shard_map/ppermute | solution.py:410
  48.6 2.1 %collective-permute-start.22 = (bf16[2,48,384]{2,1,0:T(8,128)(2,1)S(1)}, bf16[2,48,384]{2,1,0:T(8,128)(2,1)S(1)}, u32[]{:S(2)}, u32[]{:S(2)}) collective-permute-start(bf16[2,48,384]{2,1,0:T(8,128)(2,1)S(1)} %get-tuple-element.56), channel_id=1, source_target_pairs={{0,4},{1,5},{2,6},{3,7},{4,0},{5,1},{6,2},{7,3},{8,12},{9,13},{10,... | collective-permute-start | bytes 221192 | tf_op jit(solution)/shard_map/ppermute | solution.py:410
  50.7 0.1 add_convert_fusion
  50.8 1.5 %collective-permute-start.25 = (bf16[2,48,384]{2,1,0:T(8,128)(2,1)S(1)}, bf16[2,48,384]{2,1,0:T(8,128)(2,1)S(1)}, u32[]{:S(2)}, u32[]{:S(2)}) collective-permute-start(bf16[2,48,384]{2,1,0:T(8,128)(2,1)S(1)} %get-tuple-element.51), channel_id=1, source_target_pairs={{0,2},{1,3},{2,0},{3,1},{4,6},{5,7},{6,4},{7,5},{8,10},{9,11},{10,... | collective-permute-start | bytes 221192 | tf_op jit(solution)/shard_map/ppermute | solution.py:410
  52.3 2.0 %collective-permute-start.26 = (bf16[2,48,384]{2,1,0:T(8,128)(2,1)S(1)}, bf16[2,48,384]{2,1,0:T(8,128)(2,1)S(1)}, u32[]{:S(2)}, u32[]{:S(2)}) collective-permute-start(bf16[2,48,384]{2,1,0:T(8,128)(2,1)S(1)} %get-tuple-element.53), channel_id=1, source_target_pairs={{0,4},{1,5},{2,6},{3,7},{4,0},{5,1},{6,2},{7,3},{8,12},{9,13},{10,... | collective-permute-start | bytes 221192 | tf_op jit(solution)/shard_map/ppermute | solution.py:410
  54.4 0.0 collective-permute-done.21
  54.4 0.6 collective-permute-start.27
  55.0 1.4 %collective-permute-done.23 = bf16[2,48,384]{2,1,0:T(8,128)(2,1)S(1)} collective-permute-done((bf16[2,48,384]{2,1,0:T(8,128)(2,1)S(1)}, bf16[2,48,384]{2,1,0:T(8,128)(2,1)S(1)}, u32[]{:S(2)}, u32[]{:S(2)}) %collective-permute-start.23) | collective-permute-done | bytes 73760 | tf_op jit(solution)/shard_map/ppermute | solution.py:410
  56.3 0.0 collective-permute-done.25
  56.3 1.1 %collective-permute-done.26 = bf16[2,48,384]{2,1,0:T(8,128)(2,1)S(1)} collective-permute-done((bf16[2,48,384]{2,1,0:T(8,128)(2,1)S(1)}, bf16[2,48,384]{2,1,0:T(8,128)(2,1)S(1)}, u32[]{:S(2)}, u32[]{:S(2)}) %collective-permute-start.26) | collective-permute-done | bytes 73760 | tf_op jit(solution)/shard_map/ppermute | solution.py:410
  57.4 2.2 %collective-permute-done.27 = bf16[2,48,384]{2,1,0:T(8,128)(2,1)S(1)} collective-permute-done((bf16[2,48,384]{2,1,0:T(8,128)(2,1)S(1)}, bf16[2,48,384]{2,1,0:T(8,128)(2,1)S(1)}, u32[]{:S(2)}, u32[]{:S(2)}) %collective-permute-start.27) | collective-permute-done | bytes 73760 | tf_op jit(solution)/shard_map/ppermute | solution.py:410
  59.6 0.1 fusion.1
  59.8 0.1 collective-permute-start.28
  59.9 0.1 collective-permute-start.29
  59.9 4.3 %collective-permute-start.30 = (bf16[48,384]{1,0:T(8,128)(2,1)S(1)}, bf16[48,384]{1,0:T(8,128)(2,1)S(1)}, u32[]{:S(2)}, u32[]{:S(2)}) collective-permute-start(bf16[48,384]{1,0:T(8,128)(2,1)S(1)} %get-tuple-element.49), channel_id=1, source_target_pairs={{0,24},{1,25},{2,26},{3,27},{4,28},{5,29},{6,30},{7,31},{8,16},{9,... | collective-permute-start | bytes 110600 | tf_op jit(solution)/shard_map/ppermute | solution.py:410
  64.2 1.2 %shard_map.65 = bf16[8,16,384]{2,1,0:T(8,128)(2,1)} custom-call(bf16[8,16,384]{2,1,0:T(8,128)(2,1)S(1)} %copy-done, bf16[384,384]{1,0:T(8,128)(2,1)S(1)} %get-tuple-element.25.wq, bf16[384,384]{1,0:T(8,128)(2,1)S(1)} %get-tuple-element.26.wk, bf16[384,384]{1,0:T(8,128)(2,1)S(1)} %get-tuple-element.27.wv, bf16[128,384]{1,0:T(8,128)(2,1)S(1)} %get-tuple-element.35.gq, ...), custom_call_target="tpu_custom_call" | custom-call | tf_op jit(solution)/shard_map/pallas_call | solution.py:396
  65.4 0.0 collective-permute-done.28
  65.4 0.0 collective-permute-done.29
  65.4 1.2 %collective-permute-done.30 = bf16[48,384]{1,0:T(8,128)(2,1)S(1)} collective-permute-done((bf16[48,384]{1,0:T(8,128)(2,1)S(1)}, bf16[48,384]{1,0:T(8,128)(2,1)S(1)}, u32[]{:S(2)}, u32[]{:S(2)}) %collective-permute-start.30) | collective-permute-done | bytes 36896 | tf_op jit(solution)/shard_map/ppermute | solution.py:410
  66.6 0.6 reshape.18
  (20 shorter events, 0.2 us)
Async XLA Ops:
  0.6 4.8 %copy-start.1 = (bf16[18432]{0:T(1024)(128)(2,1)S(1)}, bf16[18432]{0:T(1024)(128)(2,1)}, u32[]{:S(2)}) copy-start(bf16[18432]{0:T(1024)(128)(2,1)} %param.7) | copy-start | bytes 110596
  1.7 19.9 %collective-permute-start.10 = (bf16[2,72,384]{2,1,0:T(8,128)(2,1)S(1)}, bf16[2,72,384]{2,1,0:T(8,128)(2,1)S(1)}, u32[]{:S(2)}, u32[]{:S(2)}) collective-permute-start(bf16[2,72,384]{2,1,0:T(8,128)(2,1)S(1)} %shard_map.60.refs_11_), channel_id=1, source_target_pairs={{0,2},{2,0},{4,6},{6,4},{8,10},{10,8},{12,14},{14,12},{16,18},{18,... | collective-permute-start | bytes 331784 | tf_op jit(solution)/shard_map/ppermute | solution.py:422
  4.8 16.9 %collective-permute-start.11 = (bf16[2,72,384]{2,1,0:T(8,128)(2,1)S(1)}, bf16[2,72,384]{2,1,0:T(8,128)(2,1)S(1)}, u32[]{:S(2)}, u32[]{:S(2)}) collective-permute-start(bf16[2,72,384]{2,1,0:T(8,128)(2,1)S(1)} %shard_map.60.refs_11_), channel_id=1, source_target_pairs={{2,4},{4,2},{6,8},{8,6},{10,12},{12,10},{14,16},{16,14},{18,20},{2... | collective-permute-start | bytes 331784 | tf_op jit(solution)/shard_map/ppermute | solution.py:423
  5.5 7.8 %collective-permute-start = (bf16[1,48,384]{2,1,0:T(8,128)(2,1)S(1)}, bf16[1,48,384]{2,1,0:T(8,128)(2,1)S(1)}, u32[]{:S(2)}, u32[]{:S(2)}) collective-permute-start(bf16[1,48,384]{2,1,0:T(8,128)(2,1)S(1)} %reshape.17.refs_0_), channel_id=1, source_target_pairs={{0,8},{1,9},{2,10},{3,11},{4,12},{5,13},{6,14},{7,15},{8,0},{9,1},... | collective-permute-start | bytes 110600 | tf_op jit(solution)/shard_map/ppermute | solution.py:410
  9.7 5.2 %collective-permute-start.1 = (bf16[1,48,384]{2,1,0:T(8,128)(2,1)S(1)}, bf16[1,48,384]{2,1,0:T(8,128)(2,1)S(1)}, u32[]{:S(2)}, u32[]{:S(2)}) collective-permute-start(bf16[1,48,384]{2,1,0:T(8,128)(2,1)S(1)} %reshape.17.refs_0_), channel_id=1, source_target_pairs={{0,16},{1,17},{2,18},{3,19},{4,20},{5,21},{6,22},{7,23},{8,24},{9,... | collective-permute-start | bytes 110600 | tf_op jit(solution)/shard_map/ppermute | solution.py:410
  12.3 5.8 %collective-permute-start.2 = (bf16[1,48,384]{2,1,0:T(8,128)(2,1)S(1)}, bf16[1,48,384]{2,1,0:T(8,128)(2,1)S(1)}, u32[]{:S(2)}, u32[]{:S(2)}) collective-permute-start(bf16[1,48,384]{2,1,0:T(8,128)(2,1)S(1)} %reshape.17.refs_0_), channel_id=1, source_target_pairs={{0,24},{1,25},{2,26},{3,27},{4,28},{5,29},{6,30},{7,31},{8,16},{9,... | collective-permute-start | bytes 110600 | tf_op jit(solution)/shard_map/ppermute | solution.py:410
  18.1 10.4 %copy-start = (bf16[8,16,384]{2,1,0:T(8,128)(2,1)S(1)}, bf16[8,16,384]{2,1,0:T(8,128)(2,1)}, u32[]{:S(2)}) copy-start(bf16[8,16,384]{2,1,0:T(8,128)(2,1)} %tokens.3) | copy-start | bytes 294916
  18.1 5.9 %collective-permute-start.4 = (bf16[4,48,384]{2,1,0:T(8,128)(2,1)S(1)}, bf16[4,48,384]{2,1,0:T(8,128)(2,1)S(1)}, u32[]{:S(2)}, u32[]{:S(2)}) collective-permute-start(bf16[4,48,384]{2,1,0:T(8,128)(2,1)S(1)} %shard_map.59.refs_3_), channel_id=1, source_target_pairs={{0,2},{1,3},{2,0},{3,1},{4,6},{5,7},{6,4},{7,5},{8,10},{9,11},{10,... | collective-permute-start | bytes 442376 | tf_op jit(solution)/shard_map/ppermute | solution.py:410
  19.8 6.7 %collective-permute-start.6 = (bf16[4,48,384]{2,1,0:T(8,128)(2,1)S(1)}, bf16[4,48,384]{2,1,0:T(8,128)(2,1)S(1)}, u32[]{:S(2)}, u32[]{:S(2)}) collective-permute-start(bf16[4,48,384]{2,1,0:T(8,128)(2,1)S(1)} %shard_map.59.refs_3_), channel_id=1, source_target_pairs={{0,4},{1,5},{2,6},{3,7},{4,0},{5,1},{6,2},{7,3},{8,12},{9,13},{10,... | collective-permute-start | bytes 442376 | tf_op jit(solution)/shard_map/ppermute | solution.py:410
  19.8 6.7 %collective-permute-start.8 = (bf16[4,48,384]{2,1,0:T(8,128)(2,1)S(1)}, bf16[4,48,384]{2,1,0:T(8,128)(2,1)S(1)}, u32[]{:S(2)}, u32[]{:S(2)}) collective-permute-start(bf16[4,48,384]{2,1,0:T(8,128)(2,1)S(1)} %shard_map.59.refs_3_), channel_id=1, source_target_pairs={{0,6},{1,7},{2,4},{3,5},{4,2},{5,3},{6,0},{7,1},{8,14},{9,15},{10,... | collective-permute-start | bytes 442376 | tf_op jit(solution)/shard_map/ppermute | solution.py:410
  21.7 5.4 %collective-permute-start.3 = (bf16[4,48,384]{2,1,0:T(8,128)(2,1)S(1)}, bf16[4,48,384]{2,1,0:T(8,128)(2,1)S(1)}, u32[]{:S(2)}, u32[]{:S(2)}) collective-permute-start(bf16[4,48,384]{2,1,0:T(8,128)(2,1)S(1)} %shard_map.59.refs_3_), channel_id=1, source_target_pairs={{0,1},{1,0},{2,3},{3,2},{4,5},{5,4},{6,7},{7,6},{8,9},{9,8},{10,11... | collective-permute-start | bytes 442376 | tf_op jit(solution)/shard_map/ppermute | solution.py:410
  21.7 5.3 %collective-permute-start.12 = (bf16[2,72,384]{2,1,0:T(8,128)(2,1)S(1)}, bf16[2,72,384]{2,1,0:T(8,128)(2,1)S(1)}, u32[]{:S(2)}, u32[]{:S(2)}) collective-permute-start(bf16[2,72,384]{2,1,0:T(8,128)(2,1)S(1)} %shard_map.60.refs_11_), channel_id=1, source_target_pairs={{0,1},{1,0},{2,3},{3,2},{4,5},{5,4},{6,7},{7,6},{8,9},{9,8},{10,11... | collective-permute-start | bytes 331784 | tf_op jit(solution)/shard_map/ppermute | solution.py:431
  24.0 4.5 %collective-permute-start.5 = (bf16[4,48,384]{2,1,0:T(8,128)(2,1)S(1)}, bf16[4,48,384]{2,1,0:T(8,128)(2,1)S(1)}, u32[]{:S(2)}, u32[]{:S(2)}) collective-permute-start(bf16[4,48,384]{2,1,0:T(8,128)(2,1)S(1)} %collective-permute-done.4.refs_5_), channel_id=1, source_target_pairs={{0,1},{1,0},{2,3},{3,2},{4,5},{5,4},{6,7},{7,6},{8,9},{9,8},{10,11... | collective-permute-start | bytes 442376 | tf_op jit(solution)/shard_map/ppermute | solution.py:410
  26.5 2.0 %collective-permute-start.7 = (bf16[4,48,384]{2,1,0:T(8,128)(2,1)S(1)}, bf16[4,48,384]{2,1,0:T(8,128)(2,1)S(1)}, u32[]{:S(2)}, u32[]{:S(2)}) collective-permute-start(bf16[4,48,384]{2,1,0:T(8,128)(2,1)S(1)} %collective-permute-done.6.refs_7_), channel_id=1, source_target_pairs={{0,1},{1,0},{2,3},{3,2},{4,5},{5,4},{6,7},{7,6},{8,9},{9,8},{10,11... | collective-permute-start | bytes 442376 | tf_op jit(solution)/shard_map/ppermute | solution.py:410
  26.5 2.0 %collective-permute-start.9 = (bf16[4,48,384]{2,1,0:T(8,128)(2,1)S(1)}, bf16[4,48,384]{2,1,0:T(8,128)(2,1)S(1)}, u32[]{:S(2)}, u32[]{:S(2)}) collective-permute-start(bf16[4,48,384]{2,1,0:T(8,128)(2,1)S(1)} %collective-permute-done.8.refs_9_), channel_id=1, source_target_pairs={{0,1},{1,0},{2,3},{3,2},{4,5},{5,4},{6,7},{7,6},{8,9},{9,8},{10,11... | collective-permute-start | bytes 442376 | tf_op jit(solution)/shard_map/ppermute | solution.py:410
  27.0 1.3 %collective-permute-start.13 = (bf16[2,72,384]{2,1,0:T(8,128)(2,1)S(1)}, bf16[2,72,384]{2,1,0:T(8,128)(2,1)S(1)}, u32[]{:S(2)}, u32[]{:S(2)}) collective-permute-start(bf16[2,72,384]{2,1,0:T(8,128)(2,1)S(1)} %collective-permute-done.10.refs_12_), channel_id=1, source_target_pairs={{0,1},{1,0},{2,3},{3,2},{4,5},{5,4},{6,7},{7,6},{8,9},{9,8},{10,11... | collective-permute-start | bytes 331784 | tf_op jit(solution)/shard_map/ppermute | solution.py:431
  27.1 1.4 %collective-permute-start.14 = (bf16[2,72,384]{2,1,0:T(8,128)(2,1)S(1)}, bf16[2,72,384]{2,1,0:T(8,128)(2,1)S(1)}, u32[]{:S(2)}, u32[]{:S(2)}) collective-permute-start(bf16[2,72,384]{2,1,0:T(8,128)(2,1)S(1)} %collective-permute-done.11.refs_13_), channel_id=1, source_target_pairs={{0,1},{1,0},{2,3},{3,2},{4,5},{5,4},{6,7},{7,6},{8,9},{9,8},{10,11... | collective-permute-start | bytes 331784 | tf_op jit(solution)/shard_map/ppermute | solution.py:431
  34.6 6.1 %collective-permute-start.15 = (bf16[2,4,48,384]{3,2,1,0:T(8,128)(2,1)S(1)}, bf16[2,4,48,384]{3,2,1,0:T(8,128)(2,1)S(1)}, u32[]{:S(2)}, u32[]{:S(2)}) collective-permute-start(bf16[2,4,48,384]{3,2,1,0:T(8,128)(2,1)S(1)} %get-tuple-element.38), channel_id=1, source_target_pairs={{0,1},{1,0},{2,3},{3,2},{4,5},{5,4},{6,7},{7,6},{8,9},{9,8},{10,11... | collective-permute-start | bytes 884744 | tf_op jit(solution)/shard_map/ppermute | solution.py:410
  35.0 5.1 %collective-permute-start.16 = (bf16[2,72,384]{2,1,0:T(8,128)(2,1)S(1)}, bf16[2,72,384]{2,1,0:T(8,128)(2,1)S(1)}, u32[]{:S(2)}, u32[]{:S(2)}) collective-permute-start(bf16[2,72,384]{2,1,0:T(8,128)(2,1)S(1)} %get-tuple-element.42), channel_id=1, source_target_pairs={{0,2},{2,0},{4,6},{6,4},{8,10},{10,8},{12,14},{14,12},{16,18},{18,... | collective-permute-start | bytes 331784 | tf_op jit(solution)/shard_map/ppermute | solution.py:422
  35.1 5.1 %collective-permute-start.17 = (bf16[2,72,384]{2,1,0:T(8,128)(2,1)S(1)}, bf16[2,72,384]{2,1,0:T(8,128)(2,1)S(1)}, u32[]{:S(2)}, u32[]{:S(2)}) collective-permute-start(bf16[2,72,384]{2,1,0:T(8,128)(2,1)S(1)} %get-tuple-element.42), channel_id=1, source_target_pairs={{2,4},{4,2},{6,8},{8,6},{10,12},{12,10},{14,16},{16,14},{18,20},{2... | collective-permute-start | bytes 331784 | tf_op jit(solution)/shard_map/ppermute | solution.py:423
  35.8 5.8 %collective-permute-start.18 = (bf16[2,72,384]{2,1,0:T(8,128)(2,1)S(1)}, bf16[2,72,384]{2,1,0:T(8,128)(2,1)S(1)}, u32[]{:S(2)}, u32[]{:S(2)}) collective-permute-start(bf16[2,72,384]{2,1,0:T(8,128)(2,1)S(1)} %get-tuple-element.42), channel_id=1, source_target_pairs={{0,1},{1,0},{2,3},{3,2},{4,5},{5,4},{6,7},{7,6},{8,9},{9,8},{10,11... | collective-permute-start | bytes 331784 | tf_op jit(solution)/shard_map/ppermute | solution.py:431
  40.1 1.5 %collective-permute-start.19 = (bf16[2,72,384]{2,1,0:T(8,128)(2,1)S(1)}, bf16[2,72,384]{2,1,0:T(8,128)(2,1)S(1)}, u32[]{:S(2)}, u32[]{:S(2)}) collective-permute-start(bf16[2,72,384]{2,1,0:T(8,128)(2,1)S(1)} %collective-permute-done.16.refs_0_), channel_id=1, source_target_pairs={{0,1},{1,0},{2,3},{3,2},{4,5},{5,4},{6,7},{7,6},{8,9},{9,8},{10,11... | collective-permute-start | bytes 331784 | tf_op jit(solution)/shard_map/ppermute | solution.py:431
  40.1 1.5 %collective-permute-start.20 = (bf16[2,72,384]{2,1,0:T(8,128)(2,1)S(1)}, bf16[2,72,384]{2,1,0:T(8,128)(2,1)S(1)}, u32[]{:S(2)}, u32[]{:S(2)}) collective-permute-start(bf16[2,72,384]{2,1,0:T(8,128)(2,1)S(1)} %collective-permute-done.17.refs_1_), channel_id=1, source_target_pairs={{0,1},{1,0},{2,3},{3,2},{4,5},{5,4},{6,7},{7,6},{8,9},{9,8},{10,11... | collective-permute-start | bytes 331784 | tf_op jit(solution)/shard_map/ppermute | solution.py:431
  43.9 6.8 %collective-permute-start.24 = (bf16[2,4,48,384]{3,2,1,0:T(8,128)(2,1)S(1)}, bf16[2,4,48,384]{3,2,1,0:T(8,128)(2,1)S(1)}, u32[]{:S(2)}, u32[]{:S(2)}) collective-permute-start(bf16[2,4,48,384]{3,2,1,0:T(8,128)(2,1)S(1)} %get-tuple-element.47), channel_id=1, source_target_pairs={{0,1},{1,0},{2,3},{3,2},{4,5},{5,4},{6,7},{7,6},{8,9},{9,8},{10,11... | collective-permute-start | bytes 884744 | tf_op jit(solution)/shard_map/ppermute | solution.py:410
  44.4 10.0 %collective-permute-start.21 = (bf16[2,48,384]{2,1,0:T(8,128)(2,1)S(1)}, bf16[2,48,384]{2,1,0:T(8,128)(2,1)S(1)}, u32[]{:S(2)}, u32[]{:S(2)}) collective-permute-start(bf16[2,48,384]{2,1,0:T(8,128)(2,1)S(1)} %get-tuple-element.54), channel_id=1, source_target_pairs={{0,2},{1,3},{2,0},{3,1},{4,6},{5,7},{6,4},{7,5},{8,10},{9,11},{10,... | collective-permute-start | bytes 221192 | tf_op jit(solution)/shard_map/ppermute | solution.py:410
  48.6 6.4 %collective-permute-start.22 = (bf16[2,48,384]{2,1,0:T(8,128)(2,1)S(1)}, bf16[2,48,384]{2,1,0:T(8,128)(2,1)S(1)}, u32[]{:S(2)}, u32[]{:S(2)}) collective-permute-start(bf16[2,48,384]{2,1,0:T(8,128)(2,1)S(1)} %get-tuple-element.56), channel_id=1, source_target_pairs={{0,4},{1,5},{2,6},{3,7},{4,0},{5,1},{6,2},{7,3},{8,12},{9,13},{10,... | collective-permute-start | bytes 221192 | tf_op jit(solution)/shard_map/ppermute | solution.py:410
  50.7 5.7 %collective-permute-start.23 = (bf16[2,48,384]{2,1,0:T(8,128)(2,1)S(1)}, bf16[2,48,384]{2,1,0:T(8,128)(2,1)S(1)}, u32[]{:S(2)}, u32[]{:S(2)}) collective-permute-start(bf16[2,48,384]{2,1,0:T(8,128)(2,1)S(1)} %get-tuple-element.55), channel_id=1, source_target_pairs={{0,6},{1,7},{2,4},{3,5},{4,2},{5,3},{6,0},{7,1},{8,14},{9,15},{10,... | collective-permute-start | bytes 221192 | tf_op jit(solution)/shard_map/ppermute | solution.py:410
  50.8 5.5 %collective-permute-start.25 = (bf16[2,48,384]{2,1,0:T(8,128)(2,1)S(1)}, bf16[2,48,384]{2,1,0:T(8,128)(2,1)S(1)}, u32[]{:S(2)}, u32[]{:S(2)}) collective-permute-start(bf16[2,48,384]{2,1,0:T(8,128)(2,1)S(1)} %get-tuple-element.51), channel_id=1, source_target_pairs={{0,2},{1,3},{2,0},{3,1},{4,6},{5,7},{6,4},{7,5},{8,10},{9,11},{10,... | collective-permute-start | bytes 221192 | tf_op jit(solution)/shard_map/ppermute | solution.py:410
  52.3 5.1 %collective-permute-start.26 = (bf16[2,48,384]{2,1,0:T(8,128)(2,1)S(1)}, bf16[2,48,384]{2,1,0:T(8,128)(2,1)S(1)}, u32[]{:S(2)}, u32[]{:S(2)}) collective-permute-start(bf16[2,48,384]{2,1,0:T(8,128)(2,1)S(1)} %get-tuple-element.53), channel_id=1, source_target_pairs={{0,4},{1,5},{2,6},{3,7},{4,0},{5,1},{6,2},{7,3},{8,12},{9,13},{10,... | collective-permute-start | bytes 221192 | tf_op jit(solution)/shard_map/ppermute | solution.py:410
  54.4 5.3 %collective-permute-start.27 = (bf16[2,48,384]{2,1,0:T(8,128)(2,1)S(1)}, bf16[2,48,384]{2,1,0:T(8,128)(2,1)S(1)}, u32[]{:S(2)}, u32[]{:S(2)}) collective-permute-start(bf16[2,48,384]{2,1,0:T(8,128)(2,1)S(1)} %get-tuple-element.52), channel_id=1, source_target_pairs={{0,6},{1,7},{2,4},{3,5},{4,2},{5,3},{6,0},{7,1},{8,14},{9,15},{10,... | collective-permute-start | bytes 221192 | tf_op jit(solution)/shard_map/ppermute | solution.py:410
  59.8 5.6 %collective-permute-start.28 = (bf16[48,384]{1,0:T(8,128)(2,1)S(1)}, bf16[48,384]{1,0:T(8,128)(2,1)S(1)}, u32[]{:S(2)}, u32[]{:S(2)}) collective-permute-start(bf16[48,384]{1,0:T(8,128)(2,1)S(1)} %get-tuple-element.48), channel_id=1, source_target_pairs={{0,8},{1,9},{2,10},{3,11},{4,12},{5,13},{6,14},{7,15},{8,0},{9,1},... | collective-permute-start | bytes 110600 | tf_op jit(solution)/shard_map/ppermute | solution.py:410
  59.9 5.5 %collective-permute-start.29 = (bf16[48,384]{1,0:T(8,128)(2,1)S(1)}, bf16[48,384]{1,0:T(8,128)(2,1)S(1)}, u32[]{:S(2)}, u32[]{:S(2)}) collective-permute-start(bf16[48,384]{1,0:T(8,128)(2,1)S(1)} %get-tuple-element.50), channel_id=1, source_target_pairs={{0,16},{1,17},{2,18},{3,19},{4,20},{5,21},{6,22},{7,23},{8,24},{9,... | collective-permute-start | bytes 110600 | tf_op jit(solution)/shard_map/ppermute | solution.py:410
  59.9 6.6 %collective-permute-start.30 = (bf16[48,384]{1,0:T(8,128)(2,1)S(1)}, bf16[48,384]{1,0:T(8,128)(2,1)S(1)}, u32[]{:S(2)}, u32[]{:S(2)}) collective-permute-start(bf16[48,384]{1,0:T(8,128)(2,1)S(1)} %get-tuple-element.49), channel_id=1, source_target_pairs={{0,24},{1,25},{2,26},{3,27},{4,28},{5,29},{6,30},{7,31},{8,16},{9,... | collective-permute-start | bytes 110600 | tf_op jit(solution)/shard_map/ppermute | solution.py:410
